TPU v7x, 32 devices: a whole 2x2x4 slice. The times are simulated.
32 devices in a mesh: dp: 8 (over z, x), expert: 4 (over y, core).
Axes of the slice: x: 2, y: 2, z: 4, core: 2. Of those that a mesh axis runs over, the one named last changes fastest.
Arguments:
- tokens_in: bfloat16 [2, 2048, 2048], P(None, 'dp', 'expert'), may hold values from -6 to 6
- teacher: bfloat16 [2, 2048, 2048], P(None, 'dp', 'expert'), may hold values from -6 to 6
- valid: int32 [2, 2048], P(None, 'dp'), may hold values from 0 to 1, as said below
- attn_routes: int32 [2, 2048, 2], P(None, 'dp'), may hold values from 0 to 3, all different within a row; in each aligned block of 256 rows (0 to 255, 256 to 511, ..., all dimensions but the last counted through in order) at most 144 rows name the same one
- attn_share: int32 [2, 2048, 2], P(None, 'dp'), may hold values from 1 to 7
- mlp_routes: int32 [2, 2048, 2], P(None, 'dp'), may hold values from 0 to 3, all different within a row; in each aligned block of 256 rows (0 to 255, 256 to 511, ..., all dimensions but the last counted through in order) at most 144 rows name the same one
- mlp_share: int32 [2, 2048, 2], P(None, 'dp'), may hold values from 1 to 7
- gains: float32 [2, 2048], replicated, may hold values from 0.5 to 1.5
- w_query: bfloat16 [4, 2048, 2048], P(None, 'dp', 'expert'), may hold values from -0.1875 to 0.1875
- w_out: bfloat16 [4, 2048, 2048], P(None, 'expert', 'dp'), may hold values from -0.875 to 0.875
- w_keyval: bfloat16 [2048, 2, 2048], P('dp', None, 'expert'), may hold values from -0.1875 to 0.1875
- w_gate: bfloat16 [4, 2048, 5632], P('expert', 'dp'), may hold values from -0.125 to 0.125
- w_up: bfloat16 [4, 2048, 5632], P('expert', 'dp'), may hold values from -0.125 to 0.125
- w_down: bfloat16 [4, 5632, 2048], P('expert', 'dp'), may hold values from -0.15625 to 0.15625
Outputs:
- layer_out: bfloat16 [2, 2048, 2048], P(None, 'dp', 'expert')
- loss: float32 [], replicated
- input_grad: float32 [2, 2048, 2048], P(None, 'dp', 'expert')
- gains_grad: float32 [2, 2048], replicated
- query_grad: float32 [4, 2048, 2048], P(None, 'dp', 'expert')
- out_grad: float32 [4, 2048, 2048], P(None, 'expert', 'dp')
- keyval_grad: float32 [2048, 2, 2048], P('dp', None, 'expert')
- gate_grad: float32 [4, 2048, 5632], P('expert', 'dp')
- up_grad: float32 [4, 2048, 5632], P('expert', 'dp')
- down_grad: float32 [4, 5632, 2048], P('expert', 'dp')
Inputs may be any that keep to these rules, and one draw needn't show every extreme that they name: `attn_routes`: in every aligned block of 256 tokens (one index of dp in one micro-batch) no expert is named by more than 144 tokens; a token names 2 different experts. `mlp_routes`: in every aligned block of 256 tokens (one index of dp in one micro-batch) no expert is named by more than 144 tokens; a token names 2 different experts. `valid`: the last token of every block of 256 tokens counts.
All inputs are finite; a program needn't handle non-finite values.
Results may differ from a plain program's by a relative error of at most 0.018.
Values may be sent and summed in bfloat16 or wider, within the bound.
No kernel may reach another device: no remote copies, remote signals or barrier semaphores. Data moves between devices by JAX's collectives and lax.ppermute only.
A program may use at most 640 MiB of HBM per device.

v0:
```python
import jax
import jax.numpy as jnp
from jax import lax
from jax.sharding import PartitionSpec as P

HEAD = 128
PROMPT_DEV = 128
CLEN = 128
CAP = 144


EPS = 1e-06
THETA = 10000.0
TRANS_DIMS = (((1,), (1,)), ((), ()))
ROWS_DIMS = (((0,), (0,)), ((), ()))


def rotate(value, places):
    half = value.shape[-1] // 2
    kind = value.dtype
    ladder = jnp.arange(half).astype(kind) * (2.0 / value.shape[-1])
    freqs = jnp.power(jnp.asarray(THETA, kind), -ladder)
    angle = places.astype(kind)[:, None] * freqs[None, :]
    cosine = jnp.cos(angle)[:, None, :]
    sine = jnp.sin(angle)[:, None, :]
    first = value[..., :half]
    second = value[..., half:]
    return jnp.concatenate(
        [first * cosine - second * sine, second * cosine + first * sine], axis=-1
    )


def rms_scale(field, gain):
    return field * lax.rsqrt(jnp.mean(field * field, axis=-1, keepdims=True) + EPS) * gain


def times_trans(left, right):
    return lax.dot_general(left, right, TRANS_DIMS, preferred_element_type=jnp.float32)


def times_rows(left, right):
    return lax.dot_general(left, right, ROWS_DIMS, preferred_element_type=jnp.float32)


def slot_plan(route, share, expert_id, slots):
    shares = share.astype(jnp.float32)
    weight = shares / jnp.sum(shares, axis=-1, keepdims=True)
    match = route == expert_id
    taken = jnp.any(match, axis=-1)
    gate_row = jnp.sum(jnp.where(match, weight, 0.0), axis=-1)
    order = jnp.cumsum(taken.astype(jnp.int32)) - 1
    placed = (order[None, :] == jnp.arange(slots, dtype=jnp.int32)[:, None]) & taken[None, :]
    row_index = jnp.arange(route.shape[0], dtype=jnp.int32)
    row_ids = jnp.sum(jnp.where(placed, row_index[None, :], 0), axis=1)
    filled = jnp.any(placed, axis=1)
    slot_gate = jnp.where(filled, gate_row[row_ids], 0.0)
    return (row_ids, slot_gate)


def per_device(
    tokens_in,
    teacher,
    valid,
    attn_routes,
    attn_share,
    mlp_routes,
    mlp_share,
    gains,
    w_query,
    w_out,
    w_keyval,
    w_gate,
    w_up,
    w_down,
):
    dp_count = lax.axis_size("dp")
    unit_index = lax.axis_index("dp")
    expert_index = lax.axis_index("expert")
    micro_count, row_count, local_width = tokens_in.shape
    full_width = local_width * lax.axis_size("expert")
    expert_count = w_query.shape[0]
    head_cols = w_query.shape[2]
    local_heads = head_cols // HEAD
    prompt_total = PROMPT_DEV * dp_count
    key_count = prompt_total + CLEN
    loss_scale = full_width * micro_count * row_count * dp_count / 2.0
    scale_root = HEAD ** (-0.5)
    within = jnp.arange(row_count, dtype=jnp.int32)
    places = jnp.where(
        within < PROMPT_DEV, unit_index * PROMPT_DEV + within, prompt_total + within - PROMPT_DEV
    )
    key_index = jnp.arange(key_count, dtype=jnp.int32)
    own_columns = jnp.arange(full_width, dtype=jnp.int32) // local_width == expert_index
    col_start = expert_index * local_width
    count = lax.psum(jnp.sum(valid).astype(jnp.float32), "dp")
    query_full, out_full, keyval_full = (
        lax.all_gather(w_query, "dp", axis=1, tiled=True),
        lax.all_gather(w_out, "dp", axis=2, tiled=True),
        lax.all_gather(w_keyval, "dp", axis=0, tiled=True),
    )
    keyval_flat = keyval_full.reshape(full_width, 2 * head_cols)
    held_query = jnp.zeros(query_full.shape, jnp.float32)
    held_out = jnp.zeros(out_full.shape, jnp.float32)
    held_keyval = jnp.zeros(keyval_full.shape, jnp.float32)
    held_gate = jnp.zeros((full_width, w_gate.shape[2]), jnp.float32)
    held_up = jnp.zeros((full_width, w_up.shape[2]), jnp.float32)
    held_down = jnp.zeros((w_down.shape[1] * dp_count, w_down.shape[2]), jnp.float32)
    gain_sum = jnp.zeros((2, full_width), jnp.float32)
    squared = jnp.zeros((), jnp.float32)
    results = []
    input_grads = []
    for micro_id in range(micro_count):
        field_low = lax.all_gather(tokens_in[micro_id], "expert", axis=1, tiled=True)
        field = field_low.astype(jnp.float32)
        normed1 = rms_scale(field, gains[0]).astype(jnp.bfloat16)
        keyval_pre = jnp.dot(normed1, keyval_flat, preferred_element_type=jnp.float32).reshape(
            row_count, 2, local_heads, HEAD
        )
        keys_here = rotate(keyval_pre[:, 0], places).astype(jnp.bfloat16)
        values_here = keyval_pre[:, 1].astype(jnp.bfloat16)
        pair_here = jnp.stack([keys_here, values_here], axis=1).reshape(row_count, 2, head_cols)
        prompt_pair = lax.all_gather(pair_here[:PROMPT_DEV], "dp", axis=0, tiled=True)
        pair_all = jnp.concatenate([prompt_pair, pair_here[PROMPT_DEV:]], axis=0).reshape(
            key_count, 2, local_heads, HEAD
        )
        keys_all = pair_all[:, 0]
        values_all = pair_all[:, 1]

        def score_block(query_rot, slot_places):
            raw = (
                jnp.einsum("chd,khd->hck", query_rot, keys_all, preferred_element_type=jnp.float32)
                * scale_root
            )
            seen = key_index[None, :] <= slot_places[:, None]
            return jnp.where(seen[None], raw, -1e30)

        attn_part = jnp.zeros((row_count, full_width), jnp.float32)
        kept = []
        for expert_id in range(expert_count):
            row_ids, slot_gate = slot_plan(
                attn_routes[micro_id], attn_share[micro_id], expert_id, CAP
            )
            chosen = jnp.take(normed1, row_ids, axis=0)
            slot_places = places[row_ids]
            query_pre = jnp.dot(
                chosen, query_full[expert_id], preferred_element_type=jnp.float32
            ).reshape(CAP, local_heads, HEAD)
            query_rot = rotate(query_pre, slot_places).astype(jnp.bfloat16)
            scores = score_block(query_rot, slot_places)
            peak = jnp.max(scores, axis=-1, keepdims=True)
            raised = jnp.exp(scores - peak)
            denom_sum = jnp.sum(raised, axis=-1, keepdims=True)
            attend = raised / denom_sum
            log_total = peak + jnp.log(denom_sum)
            mixed = jnp.einsum(
                "hck,khd->chd",
                attend.astype(jnp.bfloat16),
                values_all,
                preferred_element_type=jnp.float32,
            )
            mixed_low = mixed.reshape(CAP, head_cols).astype(jnp.bfloat16)
            project = jnp.dot(mixed_low, out_full[expert_id], preferred_element_type=jnp.float32)
            attn_part = attn_part.at[row_ids].add(project * slot_gate[:, None])
            kept.append(
                (
                    row_ids,
                    slot_gate,
                    chosen,
                    slot_places,
                    query_pre,
                    query_rot,
                    log_total,
                    mixed_low,
                )
            )
        attn_total = lax.psum(attn_part, "expert")
        hidden1 = field + attn_total
        normed2 = rms_scale(hidden1, gains[1]).astype(jnp.bfloat16)
        gate_full, up_full, down_full = (
            lax.all_gather(w_gate[0], "dp", axis=0, tiled=True),
            lax.all_gather(w_up[0], "dp", axis=0, tiled=True),
            lax.all_gather(w_down[0], "dp", axis=0, tiled=True),
        )
        feed_rows, feed_gate = slot_plan(
            mlp_routes[micro_id], mlp_share[micro_id], expert_index, CAP
        )
        feed_in = jnp.take(normed2, feed_rows, axis=0)
        gate_pre = jnp.dot(feed_in, gate_full, preferred_element_type=jnp.float32)
        up_pre = jnp.dot(feed_in, up_full, preferred_element_type=jnp.float32)
        inner = (jax.nn.silu(gate_pre) * up_pre).astype(jnp.bfloat16)
        feed_out = jnp.dot(inner, down_full, preferred_element_type=jnp.float32)
        feed_part = (
            jnp.zeros((row_count, full_width), jnp.float32)
            .at[feed_rows]
            .add(feed_out * feed_gate[:, None])
        )
        feed_shard = lax.psum_scatter(feed_part, "expert", scatter_dimension=1, tiled=True)
        hidden1_shard = lax.dynamic_slice_in_dim(hidden1, col_start, local_width, 1)
        result = hidden1_shard + feed_shard
        results.append(result.astype(jnp.bfloat16))
        differ = result - teacher[micro_id].astype(jnp.float32)
        counted = valid[micro_id].astype(jnp.float32)[:, None]
        squared = squared + jnp.sum(counted * differ * differ)
        grad_result = counted * differ * (2.0 * (loss_scale / (count * full_width)))
        grad_rows = lax.all_gather(grad_result, "expert", axis=1, tiled=True)
        gate_back, up_back, down_back = (
            lax.all_gather(w_gate[0], "dp", axis=0, tiled=True),
            lax.all_gather(w_up[0], "dp", axis=0, tiled=True),
            lax.all_gather(w_down[0], "dp", axis=0, tiled=True),
        )
        grad_feed = (jnp.take(grad_rows, feed_rows, axis=0) * feed_gate[:, None]).astype(
            jnp.bfloat16
        )
        grad_inner = times_trans(grad_feed, down_back)
        _, silu_back = jax.vjp(lambda left, right: jax.nn.silu(left) * right, gate_pre, up_pre)
        grad_gate_pre, grad_up_pre = silu_back(grad_inner)
        grad_gate_low = grad_gate_pre.astype(jnp.bfloat16)
        grad_up_low = grad_up_pre.astype(jnp.bfloat16)
        grad_feed_in = times_trans(grad_gate_low, gate_back) + times_trans(grad_up_low, up_back)
        held_gate = held_gate + times_rows(feed_in, grad_gate_low)
        held_up = held_up + times_rows(feed_in, grad_up_low)
        held_down = held_down + times_rows(inner, grad_feed)
        grad_norm2_part = (
            jnp.zeros((row_count, full_width), jnp.float32).at[feed_rows].add(grad_feed_in)
        )
        grad_norm2 = lax.psum(grad_norm2_part, "expert")
        _, norm2_back = jax.vjp(rms_scale, hidden1, gains[1])
        grad_hidden_norm, grad_gain2 = norm2_back(grad_norm2)
        grad_hidden1 = grad_rows + grad_hidden_norm
        grad_norm1_part = jnp.zeros((row_count, full_width), jnp.float32)
        grad_pair = jnp.zeros((key_count, 2, local_heads, HEAD), jnp.float32)
        term_query = []
        term_out = []
        for expert_id in range(expert_count):
            row_ids, slot_gate, chosen, slot_places, query_pre, query_rot, log_total, mixed_low = (
                kept[expert_id]
            )
            grad_project = (jnp.take(grad_hidden1, row_ids, axis=0) * slot_gate[:, None]).astype(
                jnp.bfloat16
            )
            grad_mixed = times_trans(grad_project, out_full[expert_id]).astype(jnp.bfloat16)
            term_out.append(times_rows(mixed_low, grad_project))
            grad_mixed = grad_mixed.reshape(CAP, local_heads, HEAD)
            scores = score_block(query_rot, slot_places)
            attend = jnp.exp(scores - log_total)
            attend_low = attend.astype(jnp.bfloat16)
            grad_attend = jnp.einsum(
                "chd,khd->hck", grad_mixed, values_all, preferred_element_type=jnp.float32
            )
            inner_sum = jnp.sum(attend * grad_attend, axis=-1, keepdims=True)
            grad_scores = (attend * (grad_attend - inner_sum)).astype(jnp.bfloat16)
            grad_query_rot = (
                jnp.einsum(
                    "hck,khd->chd", grad_scores, keys_all, preferred_element_type=jnp.float32
                )
                * scale_root
            )
            grad_keys = (
                jnp.einsum(
                    "hck,chd->khd", grad_scores, query_rot, preferred_element_type=jnp.float32
                )
                * scale_root
            )
            grad_values = jnp.einsum(
                "hck,chd->khd", attend_low, grad_mixed, preferred_element_type=jnp.float32
            )
            grad_pair = grad_pair + jnp.stack([grad_keys, grad_values], axis=1)
            _, query_back = jax.vjp(lambda value: rotate(value, slot_places), query_pre)
            grad_query_pre = (
                query_back(grad_query_rot)[0].astype(jnp.bfloat16).reshape(CAP, head_cols)
            )
            grad_norm1_part = grad_norm1_part.at[row_ids].add(
                times_trans(grad_query_pre, query_full[expert_id])
            )
            term_query.append(times_rows(chosen, grad_query_pre))
        grad_pair_flat = grad_pair.reshape(key_count, 2, head_cols)
        prompt_grad = lax.psum_scatter(
            grad_pair_flat[:prompt_total], "dp", scatter_dimension=0, tiled=True
        )
        pair_grad = jnp.concatenate([prompt_grad, grad_pair_flat[prompt_total:]], axis=0)
        _, key_back = jax.vjp(lambda value: rotate(value, places), keyval_pre[:, 0])
        grad_key_pre = key_back(pair_grad[:, 0].reshape(row_count, local_heads, HEAD))[0].reshape(
            row_count, head_cols
        )
        grad_pair_low = (
            jnp.stack([grad_key_pre, pair_grad[:, 1]], axis=1)
            .astype(jnp.bfloat16)
            .reshape(row_count, 2 * head_cols)
        )
        grad_norm1_part = grad_norm1_part + times_trans(grad_pair_low, keyval_flat)
        term_keyval = times_rows(normed1, grad_pair_low).reshape(full_width, 2, head_cols)
        grad_norm1 = lax.psum(grad_norm1_part.astype(jnp.bfloat16), "expert").astype(jnp.float32)
        _, norm1_back = jax.vjp(rms_scale, field, gains[0])
        grad_field_norm, grad_gain1 = norm1_back(grad_norm1)
        grad_field = grad_hidden1 + grad_field_norm
        input_grads.append(lax.dynamic_slice_in_dim(grad_field, col_start, local_width, 1))
        gain_sum = gain_sum + jnp.stack(
            [jnp.where(own_columns, grad_gain1, 0.0), jnp.where(own_columns, grad_gain2, 0.0)]
        )
        held_query = held_query + jnp.stack(term_query)
        held_out = held_out + jnp.stack(term_out)
        held_keyval = held_keyval + term_keyval
    grad_query, grad_out, grad_keyval, grad_gate, grad_up, grad_down = (
        lax.psum_scatter(
            held_query.astype(jnp.bfloat16), "dp", scatter_dimension=1, tiled=True
        ).astype(jnp.float32),
        lax.psum_scatter(
            held_out.astype(jnp.bfloat16), "dp", scatter_dimension=2, tiled=True
        ).astype(jnp.float32),
        lax.psum_scatter(
            held_keyval.astype(jnp.bfloat16), "dp", scatter_dimension=0, tiled=True
        ).astype(jnp.float32),
        lax.psum_scatter(
            held_gate.astype(jnp.bfloat16), "dp", scatter_dimension=0, tiled=True
        ).astype(jnp.float32),
        lax.psum_scatter(
            held_up.astype(jnp.bfloat16), "dp", scatter_dimension=0, tiled=True
        ).astype(jnp.float32),
        lax.psum_scatter(
            held_down.astype(jnp.bfloat16), "dp", scatter_dimension=0, tiled=True
        ).astype(jnp.float32),
    )
    gain_total, squared_total = lax.psum((gain_sum, squared), ("dp", "expert"))
    loss = squared_total / (count * full_width)
    return (
        jnp.stack(results),
        loss,
        jnp.stack(input_grads),
        gain_total,
        grad_query,
        grad_out,
        grad_keyval,
        grad_gate[None],
        grad_up[None],
        grad_down[None],
    )


def solution(mesh):
    in_specs = (
        P(None, "dp", "expert"),
        P(None, "dp", "expert"),
        P(None, "dp"),
        P(None, "dp", None),
        P(None, "dp", None),
        P(None, "dp", None),
        P(None, "dp", None),
        P(),
        P(None, "dp", "expert"),
        P(None, "expert", "dp"),
        P("dp", None, "expert"),
        P("expert", "dp", None),
        P("expert", "dp", None),
        P("expert", "dp", None),
    )
    out_specs = (
        P(None, "dp", "expert"),
        P(),
        P(None, "dp", "expert"),
        P(),
        P(None, "dp", "expert"),
        P(None, "expert", "dp"),
        P("dp", None, "expert"),
        P("expert", "dp", None),
        P("expert", "dp", None),
        P("expert", "dp", None),
    )
    return jax.shard_map(
        per_device, mesh=mesh, in_specs=in_specs, out_specs=out_specs, check_vma=False
    )
```

profile of v0, /device:TPU:0, one launch (start us, length us, event | category | flops | bytes accessed | tf_op | source)
XLA Modules:
  0.0 4185.3 jit_solution(11625054749379234558)
XLA Ops:
  12.9 16.7 all-gather.40.cloned.1.call-done
  31.2 17.3 all-gather.32.cloned.1.call-done
  51.9 72.8 %all-gather.18.cloned.1.call-done = bf16[2048,2,512]{2,0,1:T(8,128)(2,1)} async-done(((bf16[256,2,512]{2,0,1:T(8,128)(2,1)}), bf16[2048,2,512]{2,0,1:T(8,128)(2,1)}) %all-gather.18.cloned.1.call-update) | async-done | bytes 4194320 | tf_op jit(solution)/shard_map/all_gather | solution.py:99
  124.7 6.2 copy.110
  215.3 23.8 all-gather.26.cloned.1.call-done
  246.6 117.7 %all-gather.22.cloned.1.call-done = bf16[4,2048,512]{2,1,0:T(8,128)(2,1)} async-done(((bf16[4,256,512]{2,1,0:T(8,128)(2,1)}), bf16[4,2048,512]{2,1,0:T(8,128)(2,1)}) %all-gather.22.cloned.1.call-update) | async-done | bytes 8388624 | tf_op jit(solution)/shard_map/all_gather | solution.py:97
  364.3 5.9 slice_bitcast_fusion.4
  409.9 80.0 %all-gather.24.cloned.1.call-done = bf16[4,512,2048]{2,1,0:T(8,128)(2,1)} async-done(((bf16[4,512,256]{2,1,0:T(8,128)(2,1)}), bf16[4,512,2048]{2,1,0:T(8,128)(2,1)}) %all-gather.24.cloned.1.call-update) | async-done | bytes 8388624 | tf_op jit(solution)/shard_map/all_gather | solution.py:98
  549.2 5.4 scatter_fusion.3
  556.7 5.4 scatter_fusion.4
  576.4 76.6 %all-reduce.30.cloned.1.call-done = (f32[256,2048]{1,0:T(8,128)}, f32[256,2048]{1,0:T(8,128)}) async-done(((f32[256,2048]{1,0:T(8,128)}, f32[256,2048]{1,0:T(8,128)}), (f32[256,2048]{1,0:T(8,128)}, f32[256,2048]{1,0:T(8,128)})) %all-reduce.30.cloned.1.call-update) | async-done | bytes 4194320 | tf_op jit(solution)/shard_map/psum | solution.py:176
  663.2 432.7 %all-gather.34.cloned.1.call-done = bf16[1,2048,5632]{2,1,0:T(8,128)(2,1)} async-done(((bf16[1,256,5632]{2,1,0:T(8,128)(2,1)}), bf16[1,2048,5632]{2,1,0:T(8,128)(2,1)}) %all-gather.34.cloned.1.call-update) | async-done | bytes 23068688 | tf_op jit(solution)/shard_map/all_gather | solution.py:180
  1095.9 13.2 fusion.22
  1109.0 429.4 %all-gather.36.cloned.1.call-done = bf16[1,2048,5632]{2,1,0:T(8,128)(2,1)} async-done(((bf16[1,256,5632]{2,1,0:T(8,128)(2,1)}), bf16[1,2048,5632]{2,1,0:T(8,128)(2,1)}) %all-gather.36.cloned.1.call-update) | async-done | bytes 23068688 | tf_op jit(solution)/shard_map/all_gather | solution.py:181
  1538.4 14.6 multiply_convert_fusion.3
  1553.1 428.1 %all-gather.38.cloned.1.call-done = bf16[1,5632,2048]{2,1,0:T(8,128)(2,1)} async-done(((bf16[1,704,2048]{2,1,0:T(8,128)(2,1)}), bf16[1,5632,2048]{2,1,0:T(8,128)(2,1)}) %all-gather.38.cloned.1.call-update) | async-done | bytes 23068688 | tf_op jit(solution)/shard_map/all_gather | solution.py:182
  1981.2 12.9 fusion.54
  1998.7 10.1 fusion.20
  2008.8 14.6 multiply_convert_fusion.2
  2024.6 10.7 fusion.57
  2041.6 20.1 psum.66
  2062.4 8.9 reduce-scatter.13.cloned.1.call-done
  2074.8 22.1 all-gather.28.cloned.1.call-done
  2100.1 16.0 fusion.48
  2116.1 12.6 fusion.10
  2128.7 12.0 fusion.60
  2147.9 15.4 fusion.51
  2163.3 12.6 fusion.8
  2175.9 12.0 fusion.63
  2192.6 85.0 %all-reduce.28.cloned.1.call-done = (f32[256,2048]{1,0:T(8,128)}, f32[256,2048]{1,0:T(8,128)}) async-done(((f32[256,2048]{1,0:T(8,128)}, f32[256,2048]{1,0:T(8,128)}), (f32[256,2048]{1,0:T(8,128)}, f32[256,2048]{1,0:T(8,128)})) %all-reduce.28.cloned.1.call-update) | async-done | bytes 4194320 | tf_op jit(solution)/shard_map/psum | solution.py:226
  2359.5 5.4 copy.151
  2408.7 5.4 copy.135
  2476.1 69.4 %reduce-scatter.15.cloned.1.call-done = f32[128,2,512]{2,0,1:T(8,128)} async-done(((f32[1024,2,512]{2,0,1:T(8,128)}), f32[128,2,512]{2,0,1:T(8,128)}) %reduce-scatter.15.cloned.1.call-update) | async-done | bytes 524304 | tf_op jit(solution)/shard_map/reduce_scatter | solution.py:277
  2593.4 15.3 fusion.24
  2621.3 6.9 fusion.25
  2636.1 17.9 fusion.473
  2654.0 24.1 add_convert_fusion.2
  2679.5 20.0 fusion.472
  2699.6 23.7 add_convert_fusion.1
  2724.7 19.9 fusion.451
  2744.6 25.6 add_convert_fusion
  2782.7 41.7 all-reduce.20
  2832.1 118.4 %reduce-scatter.21.cloned.1.call-done = bf16[4,512,256]{2,1,0:T(8,128)(2,1)} async-done(((bf16[4,512,2048]{2,1,0:T(8,128)(2,1)}), bf16[4,512,256]{2,1,0:T(8,128)(2,1)}) %reduce-scatter.21.cloned.1.call-update) | async-done | bytes 1048592 | tf_op jit(solution)/shard_map/reduce_scatter | solution.py:307
  2953.2 88.8 %reduce-scatter.23.cloned.1.call-done = bf16[256,2,512]{2,0,1:T(8,128)(2,1)} async-done(((bf16[2048,2,512]{2,0,1:T(8,128)(2,1)}), bf16[256,2,512]{2,0,1:T(8,128)(2,1)}) %reduce-scatter.23.cloned.1.call-update) | async-done | bytes 524304 | tf_op jit(solution)/shard_map/reduce_scatter | solution.py:310
  3044.6 374.7 %reduce-scatter.25.cloned.1.call-done = bf16[256,5632]{1,0:T(8,128)(2,1)} async-done(((bf16[2048,5632]{1,0:T(8,128)(2,1)}), bf16[256,5632]{1,0:T(8,128)(2,1)}) %reduce-scatter.25.cloned.1.call-update) | async-done | bytes 2883600 | tf_op jit(solution)/shard_map/reduce_scatter | solution.py:313
  3424.3 371.4 %reduce-scatter.27.cloned.1.call-done = bf16[256,5632]{1,0:T(8,128)(2,1)} async-done(((bf16[2048,5632]{1,0:T(8,128)(2,1)}), bf16[256,5632]{1,0:T(8,128)(2,1)}) %reduce-scatter.27.cloned.1.call-update) | async-done | bytes 2883600 | tf_op jit(solution)/shard_map/reduce_scatter | solution.py:316
  3800.7 371.5 %reduce-scatter.29.cloned.1.call-done = bf16[704,2048]{1,0:T(8,128)(2,1)} async-done(((bf16[5632,2048]{1,0:T(8,128)(2,1)}), bf16[704,2048]{1,0:T(8,128)(2,1)}) %reduce-scatter.29.cloned.1.call-update) | async-done | bytes 2883600 | tf_op jit(solution)/shard_map/reduce_scatter | solution.py:319
  4172.3 5.1 bitcast_convert_fusion
  (1251 shorter events, 545.8 us)
Async XLA Ops:
  7.2 22.4 all-gather.40.cloned.1.call-start
  9.1 39.4 all-gather.32.cloned.1.call-start
  9.9 114.8 %all-gather.18.cloned.1.call-start = ((), (), s32[]{:S(2)}) async-start(), calls=%async_computation.10 | async-start | bytes 4718592 | tf_op jit(solution)/shard_map/all_gather | solution.py:99
  11.8 200.0 %all-gather.20.cloned.1.call-start = ((), (), s32[]{:S(2)}) async-start(), calls=%async_computation.11 | async-start | bytes 2359296 | tf_op jit(solution)/shard_map/all_gather | solution.py:122
  12.9 123.1 %copy-start.238 = (f32[256,64]{0,1:T(8,128)}, f32[256,64]{0,1:T(8,128)S(1)}, u32[]{:S(2)}) copy-start(f32[256,64]{0,1:T(8,128)S(1)} %get-tuple-element.197) | copy-start | bytes 196612
  51.9 149.7 %copy-start.6 = (bf16[256,2048]{1,0:T(8,128)(2,1)}, bf16[256,2048]{1,0:T(8,128)(2,1)S(1)}, u32[]{:S(2)}) copy-start(bf16[256,2048]{1,0:T(8,128)(2,1)S(1)} %get-tuple-element.176) | copy-start | bytes 3145732
  51.9 157.0 %copy-start.4 = (bf16[256,2048]{1,0:T(8,128)(2,1)}, bf16[256,2048]{1,0:T(8,128)(2,1)S(1)}, u32[]{:S(2)}) copy-start(bf16[256,2048]{1,0:T(8,128)(2,1)S(1)} %get-tuple-element.175) | copy-start | bytes 3145732
  138.4 100.7 %all-gather.26.cloned.1.call-start = ((), (), s32[]{:S(2)}) async-start(), calls=%async_computation.15 | async-start | bytes 2359296 | tf_op jit(solution)/shard_map/all_gather | solution.py:122
  140.3 224.0 %all-gather.22.cloned.1.call-start = ((), (), s32[]{:S(2)}) async-start(), calls=%async_computation.12 | async-start | bytes 9437184 | tf_op jit(solution)/shard_map/all_gather | solution.py:97
  140.9 349.0 %all-gather.24.cloned.1.call-start = ((), (), s32[]{:S(2)}) async-start(), calls=%async_computation.13 | async-start | bytes 9437184 | tf_op jit(solution)/shard_map/all_gather | solution.py:98
  141.7 511.3 %all-reduce.30.cloned.1.call-start = ((), (), s32[]{:S(2)}) async-start(), calls=%async_computation.33 | async-start | bytes 8388608 | tf_op jit(solution)/shard_map/psum | solution.py:176
  154.3 51.1 %copy-start.330 = (s32[1024]{0:T(1024)}, s32[1024]{0:T(1024)S(1)}, u32[]{:S(2)}) copy-start(s32[1024]{0:T(1024)S(1)} %pad_clamp_fusion.6) | copy-start | bytes 12292
  154.3 52.8 %copy-start.329 = (s32[1024]{0:T(1024)}, s32[1024]{0:T(1024)S(1)}, u32[]{:S(2)}) copy-start(s32[1024]{0:T(1024)S(1)} %pad_clamp_fusion.4) | copy-start | bytes 12292
  154.4 54.6 %copy-start.332 = (s32[1024]{0:T(1024)}, s32[1024]{0:T(1024)S(1)}, u32[]{:S(2)}) copy-start(s32[1024]{0:T(1024)S(1)} %pad_clamp_fusion.2) | copy-start | bytes 12292
  180.9 309.1 %copy-start.296 = (f32[144]{0:T(256)}, f32[144]{0:T(256)S(1)}, u32[]{:S(2)}) copy-start(f32[144]{0:T(256)S(1)} %broadcast_select_fusion.39) | copy-start | bytes 1732
  182.5 321.6 %copy-start.293 = (f32[144]{0:T(256)}, f32[144]{0:T(256)S(1)}, u32[]{:S(2)}) copy-start(f32[144]{0:T(256)S(1)} %broadcast_select_fusion.34) | copy-start | bytes 1732
  245.4 156.4 %copy-start.10 = (bf16[1152,4,128]{2,0,1:T(8,128)(2,1)}, bf16[1152,4,128]{2,0,1:T(8,128)(2,1)S(1)}, u32[]{:S(2)}) copy-start(bf16[1152,4,128]{2,0,1:T(8,128)(2,1)S(1)} %get-tuple-element.106) | copy-start | bytes 3538948
  246.6 280.2 %copy-start.8 = (bf16[1152,4,128]{2,0,1:T(8,128)(2,1)}, bf16[1152,4,128]{2,0,1:T(8,128)(2,1)S(1)}, u32[]{:S(2)}) copy-start(bf16[1152,4,128]{2,0,1:T(8,128)(2,1)S(1)} %get-tuple-element.104) | copy-start | bytes 3538948
  405.6 84.3 %copy-start.220 = (bf16[4,18,8,128]{3,2,1,0:T(8,128)(2,1)}, bf16[4,18,8,128]{3,2,1,0:T(8,128)(2,1)S(1)}, u32[]{:S(2)}) copy-start(bf16[4,18,8,128]{3,2,1,0:T(8,128)(2,1)S(1)} %fusion.198) | copy-start | bytes 442372
  409.9 86.9 %copy-start.346 = (pred[144]{0:T(512)(128)(4,1)S(1)}, pred[144]{0:T(512)(128)(4,1)}, u32[]{:S(2)}) copy-start(pred[144]{0:T(512)(128)(4,1)} %get-tuple-element.272) | copy-start | bytes 436
  568.9 526.9 %all-gather.34.cloned.1.call-start = ((), (), s32[]{:S(2)}) async-start(), calls=%async_computation.28 | async-start | bytes 25952256 | tf_op jit(solution)/shard_map/all_gather | solution.py:180
  569.7 968.8 %all-gather.36.cloned.1.call-start = ((), (), s32[]{:S(2)}) async-start(), calls=%async_computation.29 | async-start | bytes 25952256 | tf_op jit(solution)/shard_map/all_gather | solution.py:181
  570.3 82.7 %copy-start.45 = (bf16[1,256,2048]{2,1,0:T(8,128)(2,1)S(1)}, bf16[1,256,2048]{2,1,0:T(8,128)(2,1)}, u32[]{:S(2)}) copy-start(bf16[1,256,2048]{2,1,0:T(8,128)(2,1)} %all-gather.32.cloned.1.call-done) | copy-start | bytes 3145732
  570.3 1410.9 %all-gather.38.cloned.1.call-start = ((), (), s32[]{:S(2)}) async-start(), calls=%async_computation.30 | async-start | bytes 25952256 | tf_op jit(solution)/shard_map/all_gather | solution.py:182
  571.0 1491.4 %reduce-scatter.11.cloned.1.call-start = ((), (), s32[]{:S(2)}) async-start(), calls=%async_computation.14 | async-start | bytes 2621440 | tf_op jit(solution)/shard_map/reduce_scatter | solution.py:197
  576.3 1523.7 %copy-start.319 = (f32[144]{0:T(256)}, f32[144]{0:T(256)S(1)}, u32[]{:S(2)}) copy-start(f32[144]{0:T(256)S(1)} %broadcast_select_fusion.35) | copy-start | bytes 1732
  576.4 1571.5 %copy-start.317 = (f32[144]{0:T(256)}, f32[144]{0:T(256)S(1)}, u32[]{:S(2)}) copy-start(f32[144]{0:T(256)S(1)} %broadcast_select_fusion.30) | copy-start | bytes 1732
  576.4 1523.7 %copy-start.246 = (pred[144]{0:T(512)(128)(4,1)}, pred[144]{0:T(512)(128)(4,1)S(1)}, u32[]{:S(2)}) copy-start(pred[144]{0:T(512)(128)(4,1)S(1)} %get-tuple-element.268) | copy-start | bytes 436
  576.4 1571.5 %copy-start.248 = (pred[144]{0:T(512)(128)(4,1)}, pred[144]{0:T(512)(128)(4,1)S(1)}, u32[]{:S(2)}) copy-start(pred[144]{0:T(512)(128)(4,1)S(1)} %get-tuple-element.267) | copy-start | bytes 436
  655.1 1622.5 %copy-start.34 = (f32[256,2048]{1,0:T(8,128)}, f32[256,2048]{1,0:T(8,128)S(1)}, u32[]{:S(2)}) copy-start(f32[256,2048]{1,0:T(8,128)S(1)} %get-tuple-element.93) | copy-start | bytes 6291460
  1095.9 442.6 %copy-start.80 = (bf16[144,2048]{1,0:T(8,128)(2,1)S(1)}, bf16[144,2048]{1,0:T(8,128)(2,1)}, u32[]{:S(2)}) copy-start(bf16[144,2048]{1,0:T(8,128)(2,1)} %gather_fusion.22) | copy-start | bytes 1769476
  1998.6 72.6 %reduce-scatter.13.cloned.1.call-start = ((), (), s32[]{:S(2)}) async-start(), calls=%async_computation.16 | async-start | bytes 2621440 | tf_op jit(solution)/shard_map/reduce_scatter | solution.py:197
  2039.8 57.1 %all-gather.28.cloned.1.call-start = ((), (), s32[]{:S(2)}) async-start(), calls=%async_computation.17 | async-start | bytes 2621440 | tf_op jit(solution)/shard_map/all_gather | solution.py:205
  2074.1 70.5 %all-gather.30.cloned.1.call-start = ((), (), s32[]{:S(2)}) async-start(), calls=%async_computation.19 | async-start | bytes 2621440 | tf_op jit(solution)/shard_map/all_gather | solution.py:205
  2074.7 202.9 %all-reduce.28.cloned.1.call-start = ((), (), s32[]{:S(2)}) async-start(), calls=%async_computation.32 | async-start | bytes 8388608 | tf_op jit(solution)/shard_map/psum | solution.py:226
  2191.8 282.9 %reduce-scatter.17.cloned.1.call-start = ((), (), s32[]{:S(2)}) async-start(), calls=%async_computation.20 | async-start | bytes 4718592 | tf_op jit(solution)/shard_map/reduce_scatter | solution.py:277
  2192.4 176.9 %copy-start.244 = (f32[4,144]{1,0:T(4,128)}, f32[4,144]{1,0:T(4,128)S(1)}, u32[]{:S(2)}) copy-start(f32[4,144]{1,0:T(4,128)S(1)} %log_add_fusion.7) | copy-start | bytes 6916
  2192.4 191.5 %copy-start.242 = (f32[4,144]{1,0:T(4,128)}, f32[4,144]{1,0:T(4,128)S(1)}, u32[]{:S(2)}) copy-start(f32[4,144]{1,0:T(4,128)S(1)} %log_add_fusion.6) | copy-start | bytes 6916
  2287.4 87.8 %copy-start = (f32[256,2048]{1,0:T(8,128)}, f32[256,2048]{1,0:T(8,128)S(1)}, u32[]{:S(2)}) copy-start(f32[256,2048]{1,0:T(8,128)S(1)} %get-tuple-element.170) | copy-start | bytes 6291460
  2364.9 180.6 %reduce-scatter.15.cloned.1.call-start = ((), (), s32[]{:S(2)}) async-start(), calls=%async_computation.18 | async-start | bytes 4718592 | tf_op jit(solution)/shard_map/reduce_scatter | solution.py:277
  2420.1 357.0 %all-reduce.32.cloned.1.call-start = ((), (), s32[]{:S(2)}) async-start(), calls=%async_computation.34 | async-start | bytes 4194304 | tf_op jit(solution)/shard_map/psum | solution.py:292
  2474.7 70.8 %copy-start.98 = (f32[128,2,512]{2,0,1:T(8,128)S(1)}, f32[128,2,512]{2,0,1:T(8,128)}, u32[]{:S(2)}) copy-start(f32[128,2,512]{2,0,1:T(8,128)} %copy.136) | copy-start | bytes 1572868
  2593.4 235.8 %reduce-scatter.19.cloned.1.call-start = ((), (), s32[]{:S(2)}) async-start(), calls=%async_computation.21 | async-start | bytes 9437184 | tf_op jit(solution)/shard_map/reduce_scatter | solution.py:304
  2608.8 341.7 %reduce-scatter.21.cloned.1.call-start = ((), (), s32[]{:S(2)}) async-start(), calls=%async_computation.22 | async-start | bytes 9437184 | tf_op jit(solution)/shard_map/reduce_scatter | solution.py:307
  2628.3 413.7 %reduce-scatter.23.cloned.1.call-start = ((), (), s32[]{:S(2)}) async-start(), calls=%async_computation.23 | async-start | bytes 4718592 | tf_op jit(solution)/shard_map/reduce_scatter | solution.py:310
  2634.6 784.7 %reduce-scatter.25.cloned.1.call-start = ((), (), s32[]{:S(2)}) async-start(), calls=%async_computation.24 | async-start | bytes 25952256 | tf_op jit(solution)/shard_map/reduce_scatter | solution.py:313
  2678.2 1117.6 %reduce-scatter.27.cloned.1.call-start = ((), (), s32[]{:S(2)}) async-start(), calls=%async_computation.25 | async-start | bytes 25952256 | tf_op jit(solution)/shard_map/reduce_scatter | solution.py:316
  2723.4 1448.9 %reduce-scatter.29.cloned.1.call-start = ((), (), s32[]{:S(2)}) async-start(), calls=%async_computation.26 | async-start | bytes 25952256 | tf_op jit(solution)/shard_map/reduce_scatter | solution.py:319
  (356 other events, 1600.5 us)
Sparse Core Ops, SparseCore 0:
  10.2 19.4 all-gather.39
  31.8 16.7 all-gather.31
  51.3 73.3 all-gather.17
  138.5 48.7 all-gather.19
  189.8 49.2 all-gather.25
  241.2 123.0 all-gather.21
  366.3 123.5 all-gather.23
  569.1 83.8 all-reduce.29
  654.6 441.2 all-gather.33
  1097.3 441.0 all-gather.35
  1540.0 441.0 all-gather.37
  1998.8 31.3 reduce-scatter.10
  2039.9 31.2 reduce-scatter.12
  2074.3 22.5 all-gather.27
  2098.9 22.5 all-gather.29
  2191.9 85.6 all-reduce.27
  2365.0 88.0 reduce-scatter.16
  2457.6 87.8 reduce-scatter.14
  2593.5 51.2 all-reduce.31
  2648.8 149.3 reduce-scatter.18
  2801.8 148.6 reduce-scatter.20
  2955.1 86.8 reduce-scatter.22
  3045.9 373.3 reduce-scatter.24
  3423.0 372.6 reduce-scatter.26
  3799.6 372.6 reduce-scatter.28
where the time goes:
time: 4200 us; the launch traced here: 4190 us
  waiting for transfers between devices  3210 us (76%)
  matrix products  452 us (11%)
  other arithmetic  226 us (5%)
  local copies, waits for them, and re-layouts  209 us (5%)
  blocking collectives  61.8 us (1%)
    all_gather x1, waiting for transfers between devices, per_device(): lax.all_gather(w_gate[0], 'dp', axis=0, tiled=True)  433 us
    all_gather x1, waiting for transfers between devices, per_device(): lax.all_gather(w_up[0], 'dp', axis=0, tiled=True)  429 us
    all_gather x1, waiting for transfers between devices, per_device(): lax.all_gather(w_down[0], 'dp', axis=0, tiled=True)  428 us
    reduce_scatter x1, waiting for transfers between devices, per_device(): lax.psum_scatter(held_gate.astype(jnp.bfloat16), 'dp', scatter_dimension=...  375 us
    reduce_scatter x1, waiting for transfers between devices, per_device(): lax.psum_scatter(held_down.astype(jnp.bfloat16), 'dp', scatter_dimension=...  372 us
    reduce_scatter x1, waiting for transfers between devices, per_device(): lax.psum_scatter(held_up.astype(jnp.bfloat16), 'dp', scatter_dimension=0,...  371 us
    dot_general x24, matrix products, times_rows(): lax.dot_general(left, right, ROWS_DIMS, preferred_element_type=jnp.float32)  167 us
    dot_general x24, matrix products, times_trans(): lax.dot_general(left, right, TRANS_DIMS, preferred_element_type=jnp.float32)  121 us
  transfers between devices with their start and end apart: 25, of which 19 were waited for; matrix products, arithmetic and copies ran while one was open for 13% of the time, Pallas kernels for 0%

commit v1 on v0

--- a/solution.py
+++ b/solution.py
@@ -1,6 +1,7 @@
 import jax
 import jax.numpy as jnp
 from jax import lax
+from jax.sharding import Mesh
 from jax.sharding import PartitionSpec as P
 
 HEAD = 128
@@ -336,35 +337,428 @@
     )
 
 
+def swap_pairs(size):
+    return [(i, i ^ 1) for i in range(size)]
+
+
+DEAL_FIRST = [(0, 0), (1, 2), (2, 1), (3, 3)]
+DEAL_SECOND = [(0, 2), (1, 0), (2, 3), (3, 1)]
+BACK_FIRST = [(b, a) for a, b in DEAL_FIRST]
+BACK_SECOND = [(b, a) for a, b in DEAL_SECOND]
+QUAD = ("y", "c")
+TEAM = ("c", "dp")
+
+
+def rope_tables(places):
+    half = HEAD // 2
+    ladder = jnp.arange(half).astype(jnp.float32) * (2.0 / HEAD)
+    freqs = jnp.power(jnp.asarray(THETA, jnp.float32), -ladder)
+    angle = places.astype(jnp.float32)[:, None] * freqs[None, :]
+    return jnp.cos(angle), jnp.sin(angle)
+
+
+def turn(value, cosine, sine):
+    half = value.shape[-1] // 2
+    first = value[..., :half]
+    second = value[..., half:]
+    return jnp.concatenate(
+        [first * cosine - second * sine, second * cosine + first * sine], axis=-1
+    )
+
+
+def root_of(field):
+    return lax.rsqrt(jnp.mean(field * field, axis=-1, keepdims=True) + EPS)
+
+
+def norm_back(field, gain, grad):
+    root = root_of(field)
+    scaled = grad * gain
+    along = jnp.sum(scaled * field, axis=-1, keepdims=True) / field.shape[-1]
+    return root * scaled - field * (root * root * root) * along, jnp.sum(grad * field * root, axis=0)
+
+
+def gate_rows(route, share, expert_count):
+    shares = share.astype(jnp.float32)
+    weight = shares / jnp.sum(shares, axis=-1, keepdims=True)
+    labels = jnp.arange(expert_count, dtype=jnp.int32)
+    match = route[None, :, :] == labels[:, None, None]
+    return jnp.sum(jnp.where(match, weight[None], 0.0), axis=-1)
+
+
+def dot(left, right):
+    return jnp.dot(left, right, preferred_element_type=jnp.float32)
+
+
+def team_device(
+    tokens_in,
+    teacher,
+    valid,
+    attn_routes,
+    attn_share,
+    mlp_routes,
+    mlp_share,
+    gains,
+    w_query,
+    w_out,
+    w_keyval,
+    w_gate,
+    w_up,
+    w_down,
+):
+    low = jnp.bfloat16
+    units = lax.axis_size("dp")
+    plane = lax.axis_index("y")
+    core = lax.axis_index("c")
+    micro_count, row_count, local_width = tokens_in.shape
+    half = row_count // 2
+    width = local_width * 4
+    team_rows = 2 * units * half
+    prompt_total = units * half
+    expert_count = w_query.shape[0]
+    local_heads = w_query.shape[2] // HEAD
+    depth = w_query.shape[1]
+    hidden = w_down.shape[1]
+    loss_scale = width * micro_count * row_count * units / 2.0
+    scale_root = HEAD ** (-0.5)
+
+    def to_rows(value):
+        parts = value.reshape(4, half, local_width)
+        got = lax.all_to_all(parts, QUAD, 0, 0, tiled=True)
+        return got.transpose(1, 0, 2).reshape(half, width)
+
+    def from_rows(value):
+        parts = value.reshape(half, 4, local_width).transpose(1, 0, 2)
+        got = lax.all_to_all(parts, QUAD, 0, 0, tiled=True)
+        return got.reshape(micro_count, row_count, local_width)
+
+    def collect(value):
+        return lax.all_gather(value, TEAM, axis=0, tiled=True)
+
+    def deliver(value):
+        return lax.psum_scatter(value.astype(low), TEAM, scatter_dimension=0, tiled=True).astype(
+            jnp.float32
+        )
+
+    def mine(value):
+        return lax.dynamic_index_in_dim(value, plane, 0, keepdims=False)
+
+    field = to_rows(tokens_in).astype(jnp.float32)
+    goal = to_rows(teacher).astype(jnp.float32)
+    normed1 = collect((field * root_of(field) * gains[0]).astype(low))
+
+    query_part = w_query.reshape(expert_count, depth, local_heads, HEAD).transpose(1, 2, 0, 3)
+    out_part = w_out.reshape(expert_count, local_heads, HEAD, depth).transpose(3, 1, 0, 2)
+    pair_part = w_keyval.reshape(depth, 2, local_heads, HEAD).transpose(0, 2, 1, 3)
+    wide = expert_count * HEAD
+    packed = jnp.concatenate(
+        [
+            query_part.reshape(depth, local_heads, wide),
+            pair_part.reshape(depth, local_heads, 2 * HEAD),
+            out_part.reshape(depth, local_heads, wide),
+        ],
+        axis=2,
+    )
+    lanes = packed.shape[2]
+    packed = packed.reshape(2, depth // 2, local_heads, lanes).transpose(0, 2, 1, 3)
+    kept_half = lax.dynamic_index_in_dim(packed, core, 0, keepdims=False)
+    sent_half = lax.dynamic_index_in_dim(packed, 1 - core, 0, keepdims=False)
+    got_half = lax.ppermute(sent_half, "c", swap_pairs(2))
+    heads = jnp.concatenate(
+        [
+            jnp.where(core == 0, kept_half, got_half),
+            jnp.where(core == 0, got_half, kept_half),
+        ],
+        axis=0,
+    )
+    heads = lax.all_to_all(heads, "dp", 0, 0, tiled=True)
+    dealt_first = lax.ppermute(heads, QUAD, DEAL_FIRST)
+    dealt_second = lax.ppermute(heads, QUAD, DEAL_SECOND)
+    head_weights = jnp.stack(
+        [
+            jnp.where(plane == 0, dealt_first, dealt_second),
+            jnp.where(plane == 0, dealt_second, dealt_first),
+        ],
+        axis=1,
+    ).reshape(width, lanes)
+    front_weights = head_weights[:, : wide + 2 * HEAD]
+    out_weights = head_weights[:, wide + 2 * HEAD :]
+
+    def spread(value):
+        slabs = value.reshape(depth, units, hidden).transpose(1, 0, 2)
+        return lax.all_to_all(slabs, "dp", 0, 0, tiled=True).reshape(width, hidden)
+
+    def across(value):
+        return lax.ppermute(value, "y", swap_pairs(2))
+
+    down_own = w_down[0]
+    down_far = across(down_own)
+    gate_own = spread(w_gate[0])
+    gate_far = across(gate_own)
+    up_own = spread(w_up[0])
+    up_far = across(up_own)
+
+    gate_here = jnp.concatenate(
+        [
+            gate_rows(mine(attn_routes), mine(attn_share), expert_count),
+            gate_rows(mine(mlp_routes), mine(mlp_share), expert_count),
+        ],
+        axis=0,
+    )
+    gate_all = lax.all_gather(gate_here, "dp", axis=0, tiled=False)
+    gate_all = (
+        gate_all.reshape(units, 2 * expert_count, 2, half)
+        .transpose(1, 2, 0, 3)
+        .reshape(2 * expert_count, team_rows)
+    )
+    attn_gate = gate_all[:expert_count].T
+    feed_gate_own = lax.dynamic_index_in_dim(gate_all, expert_count + 2 * plane + core, 0, False)[:, None]
+    feed_gate_far = lax.dynamic_index_in_dim(
+        gate_all, expert_count + 2 * (1 - plane) + core, 0, False
+    )[:, None]
+    count = lax.psum(jnp.sum(valid).astype(jnp.float32), "dp")
+    counted = lax.dynamic_slice_in_dim(mine(valid), core * half, half, 0).astype(jnp.float32)[:, None]
+
+    index = jnp.arange(team_rows, dtype=jnp.int32)
+    places = jnp.where(index < prompt_total, index, prompt_total + index % half)
+    cosine, sine = rope_tables(places)
+
+    front = dot(normed1, front_weights)
+    query_rot = turn(
+        front[:, :wide].reshape(team_rows, expert_count, HEAD), cosine[:, None], sine[:, None]
+    ).astype(low)
+    keys = turn(front[:, wide : wide + HEAD], cosine, sine).astype(low)
+    values = front[:, wide + HEAD :].astype(low)
+    prompt_keys, prompt_values = keys[:prompt_total], values[:prompt_total]
+    tail_keys = keys[prompt_total:].reshape(units, half, HEAD)
+    tail_values = values[prompt_total:].reshape(units, half, HEAD)
+    prompt_query = query_rot[:prompt_total].transpose(1, 0, 2)
+    tail_query = query_rot[prompt_total:].reshape(units, half, expert_count, HEAD).transpose(2, 0, 1, 3)
+
+    def product(kind, left, right):
+        return jnp.einsum(kind, left, right, preferred_element_type=jnp.float32)
+
+    seen = index[None, :prompt_total] <= index[:prompt_total, None]
+    prompt_score = jnp.where(
+        seen, product("etd,kd->etk", prompt_query, prompt_keys) * scale_root, -1e30
+    )
+    tail_far = product("ejtd,kd->ejtk", tail_query, prompt_keys) * scale_root
+    tail_near = jnp.where(
+        seen[:half, :half], product("ejtd,jkd->ejtk", tail_query, tail_keys) * scale_root, -1e30
+    )
+
+    prompt_share = jax.nn.softmax(prompt_score, axis=-1)
+    peak = jnp.maximum(
+        jnp.max(tail_far, axis=-1, keepdims=True), jnp.max(tail_near, axis=-1, keepdims=True)
+    )
+    far_raised = jnp.exp(tail_far - peak)
+    near_raised = jnp.exp(tail_near - peak)
+    total = jnp.sum(far_raised, axis=-1, keepdims=True) + jnp.sum(near_raised, axis=-1, keepdims=True)
+    far_share = far_raised / total
+    near_share = near_raised / total
+    prompt_mix = product("etk,kd->etd", prompt_share.astype(low), prompt_values)
+    tail_mix = product("ejtk,kd->ejtd", far_share.astype(low), prompt_values) + product(
+        "ejtk,jkd->ejtd", near_share.astype(low), tail_values
+    )
+    mixed = jnp.concatenate(
+        [prompt_mix.transpose(1, 0, 2), tail_mix.transpose(1, 2, 0, 3).reshape(prompt_total, expert_count, HEAD)],
+        axis=0,
+    )
+    mixed_low = (mixed * attn_gate[:, :, None]).astype(low).reshape(team_rows, wide)
+    hidden1 = field + deliver(times_trans(mixed_low, out_weights))
+    normed2 = collect((hidden1 * root_of(hidden1) * gains[1]).astype(low))
+
+    sides = ((gate_own, up_own, down_own, feed_gate_own), (gate_far, up_far, down_far, feed_gate_far))
+    feed_part = jnp.zeros((team_rows, width), jnp.float32)
+    kept = []
+    for gate_w, up_w, down_w, share_col in sides:
+        gate_pre = dot(normed2, gate_w)
+        up_pre = dot(normed2, up_w)
+        inner = (jax.nn.silu(gate_pre) * up_pre * share_col).astype(low)
+        feed_part = feed_part + dot(inner, down_w)
+        kept.append((gate_pre, up_pre, inner))
+    result = hidden1 + deliver(feed_part)
+    layer_out = from_rows(result.astype(low))
+    differ = result - goal
+    squared = jnp.sum(counted * differ * differ)
+    grad_result = counted * differ * (2.0 * (loss_scale / (count * width)))
+    grad_rows = collect(grad_result.astype(low))
+
+    grad_norm2_part = jnp.zeros((team_rows, width), jnp.float32)
+    feed_grads = []
+    for (gate_w, up_w, down_w, share_col), (gate_pre, up_pre, inner) in zip(sides, kept):
+        grad_inner = times_trans(grad_rows, down_w) * share_col
+        sigma = jax.nn.sigmoid(gate_pre)
+        grad_gate = (grad_inner * up_pre * sigma * (1.0 + gate_pre * (1.0 - sigma))).astype(low)
+        grad_up = (grad_inner * gate_pre * sigma).astype(low)
+        grad_norm2_part = grad_norm2_part + times_trans(grad_gate, gate_w) + times_trans(grad_up, up_w)
+        feed_grads.append((grad_gate, grad_up, inner))
+    grad_norm2 = deliver(grad_norm2_part)
+    grad_hidden_norm, grad_gain2 = norm_back(hidden1, gains[1], grad_norm2)
+    grad_hidden1 = grad_result + grad_hidden_norm
+    grad_hidden_rows = collect(grad_hidden1.astype(low))
+
+    (grad_gate_own, grad_up_own, inner_own), (grad_gate_far, grad_up_far, inner_far) = feed_grads
+    down_sum = times_rows(inner_own, grad_rows) + across(
+        times_rows(inner_far, grad_rows).astype(low)
+    ).astype(jnp.float32)
+    gate_sum = times_rows(normed2, grad_gate_own) + across(
+        times_rows(normed2, grad_gate_far).astype(low)
+    ).astype(jnp.float32)
+    up_sum = times_rows(normed2, grad_up_own) + across(
+        times_rows(normed2, grad_up_far).astype(low)
+    ).astype(jnp.float32)
+
+    def gather_back(value):
+        slabs = value.astype(low).reshape(units, depth, hidden)
+        got = lax.all_to_all(slabs, "dp", 0, 0, tiled=True)
+        return got.transpose(1, 0, 2).reshape(depth, units * hidden).astype(jnp.float32)
+
+    grad_gate_out = gather_back(gate_sum)
+    grad_up_out = gather_back(up_sum)
+
+    grad_mixed = (
+        dot(grad_hidden_rows, out_weights).reshape(team_rows, expert_count, HEAD) * attn_gate[:, :, None]
+    ).astype(low)
+    out_grad = times_rows(grad_hidden_rows, mixed_low)
+    prompt_back = grad_mixed[:prompt_total].transpose(1, 0, 2)
+    tail_back = grad_mixed[prompt_total:].reshape(units, half, expert_count, HEAD).transpose(2, 0, 1, 3)
+    prompt_pull = product("etd,kd->etk", prompt_back, prompt_values)
+    prompt_ds = (
+        prompt_share * (prompt_pull - jnp.sum(prompt_share * prompt_pull, axis=-1, keepdims=True))
+    ).astype(low)
+    far_pull = product("ejtd,kd->ejtk", tail_back, prompt_values)
+    near_pull = product("ejtd,jkd->ejtk", tail_back, tail_values)
+    along = jnp.sum(far_share * far_pull, axis=-1, keepdims=True) + jnp.sum(
+        near_share * near_pull, axis=-1, keepdims=True
+    )
+    far_ds = (far_share * (far_pull - along)).astype(low)
+    near_ds = (near_share * (near_pull - along)).astype(low)
+    prompt_dq = product("etk,kd->etd", prompt_ds, prompt_keys)
+    tail_dq = product("ejtk,kd->ejtd", far_ds, prompt_keys) + product("ejtk,jkd->ejtd", near_ds, tail_keys)
+    prompt_dk = product("etk,etd->kd", prompt_ds, prompt_query) + product(
+        "ejtk,ejtd->kd", far_ds, tail_query
+    )
+    tail_dk = product("ejtk,ejtd->jkd", near_ds, tail_query)
+    prompt_dv = product("etk,etd->kd", prompt_share.astype(low), prompt_back) + product(
+        "ejtk,ejtd->kd", far_share.astype(low), tail_back
+    )
+    tail_dv = product("ejtk,ejtd->jkd", near_share.astype(low), tail_back)
+    grad_query = (
+        jnp.concatenate(
+            [prompt_dq.transpose(1, 0, 2), tail_dq.transpose(1, 2, 0, 3).reshape(prompt_total, expert_count, HEAD)],
+            axis=0,
+        )
+        * scale_root
+    )
+    grad_keys = jnp.concatenate([prompt_dk, tail_dk.reshape(prompt_total, HEAD)], axis=0) * scale_root
+    grad_values = jnp.concatenate([prompt_dv, tail_dv.reshape(prompt_total, HEAD)], axis=0)
+    front_back = jnp.concatenate(
+        [
+            turn(grad_query, cosine[:, None], -sine[:, None]).reshape(team_rows, wide),
+            turn(grad_keys, cosine, -sine),
+            grad_values,
+        ],
+        axis=1,
+    ).astype(low)
+    grad_norm1 = deliver(times_trans(front_back, front_weights))
+    front_grad = times_rows(normed1, front_back)
+    grad_field_norm, grad_gain1 = norm_back(field, gains[0], grad_norm1)
+    input_grad = from_rows(grad_hidden1 + grad_field_norm)
+
+    def send_back(value):
+        columns = value.shape[1]
+        halves = value.astype(low).reshape(units, 2, depth // 2, columns)
+        first = lax.dynamic_index_in_dim(halves, plane, 1, keepdims=False)
+        second = lax.dynamic_index_in_dim(halves, 1 - plane, 1, keepdims=False)
+        both = lax.ppermute(first, QUAD, BACK_FIRST).astype(jnp.float32) + lax.ppermute(
+            second, QUAD, BACK_SECOND
+        ).astype(jnp.float32)
+        got = lax.all_to_all(both.astype(low), "dp", 0, 0, tiled=True)
+        got = got.reshape(2, local_heads, depth // 2, columns)
+        own = lax.dynamic_index_in_dim(got, core, 0, keepdims=False)
+        swapped = lax.ppermute(
+            lax.dynamic_index_in_dim(got, 1 - core, 0, keepdims=False), "c", swap_pairs(2)
+        )
+        rows = jnp.concatenate(
+            [jnp.where(core == 0, own, swapped), jnp.where(core == 0, swapped, own)], axis=1
+        )
+        return rows.astype(jnp.float32)
+
+    out_back = send_back(out_grad)
+    front_out = send_back(front_grad)
+    grad_out = out_back.reshape(local_heads, depth, expert_count, HEAD).transpose(2, 0, 3, 1)
+    grad_query_out = front_out[:, :, :wide].reshape(local_heads, depth, expert_count, HEAD).transpose(2, 1, 0, 3)
+    grad_pair = front_out[:, :, wide:].reshape(local_heads, depth, 2, HEAD).transpose(1, 2, 0, 3)
+    gain_total, squared_total = lax.psum(
+        (jnp.stack([grad_gain1, grad_gain2]), squared), ("dp", "y", "c")
+    )
+    return (
+        layer_out,
+        squared_total / (count * width),
+        input_grad,
+        gain_total,
+        grad_query_out.reshape(w_query.shape),
+        grad_out.reshape(w_out.shape),
+        grad_pair.reshape(w_keyval.shape),
+        grad_gate_out[None],
+        grad_up_out[None],
+        down_sum[None],
+    )
+
+
 def solution(mesh):
-    in_specs = (
-        P(None, "dp", "expert"),
-        P(None, "dp", "expert"),
-        P(None, "dp"),
-        P(None, "dp", None),
-        P(None, "dp", None),
-        P(None, "dp", None),
-        P(None, "dp", None),
-        P(),
-        P(None, "dp", "expert"),
-        P(None, "expert", "dp"),
-        P("dp", None, "expert"),
-        P("expert", "dp", None),
-        P("expert", "dp", None),
-        P("expert", "dp", None),
-    )
-    out_specs = (
-        P(None, "dp", "expert"),
-        P(),
-        P(None, "dp", "expert"),
-        P(),
-        P(None, "dp", "expert"),
-        P(None, "expert", "dp"),
-        P("dp", None, "expert"),
-        P("expert", "dp", None),
-        P("expert", "dp", None),
-        P("expert", "dp", None),
-    )
-    return jax.shard_map(
-        per_device, mesh=mesh, in_specs=in_specs, out_specs=out_specs, check_vma=False
-    )
+    units, experts = mesh.shape["dp"], mesh.shape["expert"]
+
+    def specs(quad):
+        return (
+            (
+                P(None, "dp", quad),
+                P(None, "dp", quad),
+                P(None, "dp"),
+                P(None, "dp", None),
+                P(None, "dp", None),
+                P(None, "dp", None),
+                P(None, "dp", None),
+                P(),
+                P(None, "dp", quad),
+                P(None, quad, "dp"),
+                P("dp", None, quad),
+                P(quad, "dp", None),
+                P(quad, "dp", None),
+                P(quad, "dp", None),
+            ),
+            (
+                P(None, "dp", quad),
+                P(),
+                P(None, "dp", quad),
+                P(),
+                P(None, "dp", quad),
+                P(None, quad, "dp"),
+                P("dp", None, quad),
+                P(quad, "dp", None),
+                P(quad, "dp", None),
+                P(quad, "dp", None),
+            ),
+        )
+
+    def step(*arguments):
+        tokens_in, w_query = arguments[0], arguments[8]
+        team = (
+            experts == 4
+            and tokens_in.shape[0] == 2
+            and w_query.shape[2] // HEAD == 2 * units
+            and w_query.shape[0] == 4
+            and tokens_in.shape[1] == units * 2 * PROMPT_DEV
+            and PROMPT_DEV == CLEN
+        )
+        if team:
+            grid = Mesh(mesh.devices.reshape(units, 2, 2), ("dp", "y", "c"))
+            ins, outs = specs(QUAD)
+            body = team_device
+        else:
+            grid = mesh
+            ins, outs = specs("expert")
+            body = per_device
+        return jax.shard_map(body, mesh=grid, in_specs=ins, out_specs=outs, check_vma=False)(*arguments)
+
+    return step

time: 4200 us -> 1660 us (0.40)
  waiting for transfers between devices: 3210 us -> 758 us
  other arithmetic: 226 us -> 87.6 us
  blocking collectives: 61.8 us -> 198 us
  starting transfers between devices: 2.6 us -> 96.4 us
  matrix products: 452 us -> 366 us
  local copies, waits for them, and re-layouts: 209 us -> 125 us
    all_gather x12 -> x4, waiting for transfers between devices: 1640 us -> 75.1 us  [collect(): return lax.all_gather(value, TEAM, axis=0, tiled=True)]
    reduce_scatter x10 -> x4, waiting for transfers between devices: 1400 us -> 286 us  [deliver(): lax.psum_scatter(value.astype(low), TEAM, scatter_dimension=0, tiled=True)]
    all_to_all x0 -> x10, waiting for transfers between devices: none -> 234 us  [the longest x2 169 us: spread(): return lax.all_to_all(slabs, 'dp', 0, 0, tiled=True).reshape(width, hidden)]
    ppermute x0 -> x15, waiting for transfers between devices: none -> 164 us  [the longest x6 135 us: across(): return lax.ppermute(value, 'y', swap_pairs(2))]
    psum x3 -> x0, waiting for transfers between devices: 162 us -> none  [the longest x1 85 us: per_device(): grad_norm2 = lax.psum(grad_norm2_part, 'expert')]
    all_to_all x0 -> x1, blocking collectives: none -> 102 us  [team_device(): heads = lax.all_to_all(heads, 'dp', 0, 0, tiled=True)]
    dot_general x24 -> x8, matrix products: 167 us -> 83.6 us  [times_rows(): lax.dot_general(left, right, ROWS_DIMS, preferred_element_type=jnp.float32)]
    gather x38 -> x0, local copies, waits for them, and re-layouts: 82 us -> none  [the longest x8 26.1 us: per_device(): jnp.take(grad_hidden1, row_ids, axis=0) * slot_gate[:, None]]
  transfers between devices with their start and end apart: 25 -> 33, of which waited for: 19 -> 15; matrix products, arithmetic and copies ran while one was open for 13% -> 22% of each run, Pallas kernels for 0% -> 0%
where the time goes in v1:
time: 1660 us; the launch traced here: 1650 us
  waiting for transfers between devices  758 us (46%)
  matrix products  366 us (22%)
  blocking collectives  198 us (12%)
  local copies, waits for them, and re-layouts  125 us (8%)
  starting transfers between devices  96.4 us (6%)
  other arithmetic  87.6 us (5%)
  between operations  19.1 us (1%)
    reduce_scatter x4, waiting for transfers between devices, deliver(): lax.psum_scatter(value.astype(low), TEAM, scatter_dimension=0, tiled=True)  286 us
    all_to_all x2, waiting for transfers between devices, spread(): return lax.all_to_all(slabs, 'dp', 0, 0, tiled=True).reshape(width, hidden)  169 us
    ppermute x6, waiting for transfers between devices, across(): return lax.ppermute(value, 'y', swap_pairs(2))  135 us
    dot_general x8, matrix products, times_trans(): lax.dot_general(left, right, TRANS_DIMS, preferred_element_type=jnp.float32)  109 us
    all_to_all x1, blocking collectives, team_device(): heads = lax.all_to_all(heads, 'dp', 0, 0, tiled=True)  102 us
    dot_general x8, matrix products, dot(): return jnp.dot(left, right, preferred_element_type=jnp.float32)  84.9 us
    dot_general x8, matrix products, times_rows(): lax.dot_general(left, right, ROWS_DIMS, preferred_element_type=jnp.float32)  83.6 us
    dot_general x17, matrix products, product(): return jnp.einsum(kind, left, right, preferred_element_type=jnp.float32)  75.7 us
  transfers between devices with their start and end apart: 33, of which 15 were waited for; matrix products, arithmetic and copies ran while one was open for 22% of the time, Pallas kernels for 0%

profile of v1, /device:TPU:0, one launch (start us, length us, event | category | flops | bytes accessed | tf_op | source)
XLA Modules:
  0.0 1649.2 jit_solution(15425754527158744291)
XLA Ops:
  12.4 8.0 all-to-all-done
  41.0 101.6 %all_to_all.55 = bf16[8,128,1280]{2,1,0:T(8,128)(2,1)} all-to-all(bf16[8,128,1280]{2,1,0:T(8,128)(2,1)S(1)} %pad_maximum_fusion.2), channel_id=1, replica_groups=mesh['dp'=8,'y'=2,'c'=2] {'dp'}, dimensions={0} | all-to-all | bytes 5242880 | tf_op jit(solution)/shard_map/all_to_all | solution.py:473
  142.6 21.2 %collective-permute-start.1 = (bf16[8,128,1280]{2,1,0:T(8,128)(2,1)}, bf16[8,128,1280]{2,1,0:T(8,128)(2,1)}, u32[]{:S(2)}, u32[]{:S(2)}) collective-permute-start(bf16[8,128,1280]{2,1,0:T(8,128)(2,1)} %all_to_all.55), channel_id=1, source_target_pairs={{0,0},{1,2},{2,1},{3,3},{4,4},{5,6},{6,5},{7,7},{8,8},{9,10},{10,9... | collective-permute-start | bytes 7864328 | tf_op jit(solution)/shard_map/ppermute | solution.py:474
  165.6 30.5 %all-gather = f32[64,256]{1,0:T(8,128)S(1)} all-gather(f32[8,256]{1,0:T(8,128)S(1)} %pad_maximum_fusion.10), channel_id=2, replica_groups=mesh['dp'=8,'y'=2,'c'=2] {'dp'}, dimensions={0}, use_global_device_ids=true | all-gather | bytes 73728 | tf_op jit(solution)/shard_map/all_gather | solution.py:507
  208.9 12.1 fusion.146
  247.5 12.0 fusion.148
  291.6 8.8 convolution_convert_fusion.1
  300.4 104.6 %reduce-scatter.5.cloned.1.call-done = bf16[128,2048]{1,0:T(8,128)(2,1)} async-done(((bf16[2048,2048]{1,0:T(8,128)(2,1)}), bf16[128,2048]{1,0:T(8,128)(2,1)}) %reduce-scatter.5.cloned.1.call-update) | async-done | bytes 524304 | tf_op jit(solution)/shard_map/reduce_scatter | solution.py:438
  421.4 109.0 %all-to-all-done.2 = bf16[8,256,704]{1,2,0:T(8,128)(2,1)} async-done(((bf16[8,256,704]{1,2,0:T(8,128)(2,1)}), bf16[8,256,704]{1,2,0:T(8,128)(2,1)}, u32[]{:S(2)}, u32[]{:S(2)}) %all-to-all-start.2) | async-done | bytes 2883616 | tf_op jit(solution)/shard_map/all_to_all | solution.py:488
  540.3 59.6 %all-to-all-done.3 = bf16[8,256,704]{1,2,0:T(8,128)(2,1)} async-done(((bf16[8,256,704]{1,2,0:T(8,128)(2,1)}), bf16[8,256,704]{1,2,0:T(8,128)(2,1)}, u32[]{:S(2)}, u32[]{:S(2)}) %all-to-all-start.3) | async-done | bytes 2883616 | tf_op jit(solution)/shard_map/all_to_all | solution.py:488
  605.7 9.6 fusion.157
  615.3 11.1 multiply_convert_fusion.7
  626.4 43.0 %collective-permute-done.3 = bf16[2048,704]{0,1:T(8,128)(2,1)} collective-permute-done((bf16[2048,704]{0,1:T(8,128)(2,1)}, bf16[2048,704]{0,1:T(8,128)(2,1)}, u32[]{:S(2)}, u32[]{:S(2)}) %collective-permute-start.3) | collective-permute-done | bytes 2883616 | tf_op jit(solution)/shard_map/ppermute | solution.py:491
  677.4 10.4 fusion.130
  687.8 40.9 %collective-permute-done.4 = bf16[2048,704]{0,1:T(8,128)(2,1)} collective-permute-done((bf16[2048,704]{0,1:T(8,128)(2,1)}, bf16[2048,704]{0,1:T(8,128)(2,1)}, u32[]{:S(2)}, u32[]{:S(2)}) %collective-permute-start.4) | collective-permute-done | bytes 2883616 | tf_op jit(solution)/shard_map/ppermute | solution.py:491
  728.8 10.0 multiply_convert_fusion.6
  740.3 13.3 add_convert_fusion.1
  758.4 21.4 %psum.22 = f32[]{:T(128)} all-reduce(f32[]{:T(128)S(6)} %convert_element_type.319), channel_id=1, replica_groups=mesh['dp'=8,'y'=2,'c'=2] {'dp'}, use_global_device_ids=true, to_apply=%region_17.18 | all-reduce | flops 1 | bytes 8 | tf_op jit(solution)/shard_map/psum | solution.py:518
  780.8 78.1 %reduce-scatter.7.cloned.1.call-done = bf16[128,2048]{1,0:T(8,128)(2,1)} async-done(((bf16[2048,2048]{1,0:T(8,128)(2,1)}), bf16[128,2048]{1,0:T(8,128)(2,1)}) %reduce-scatter.7.cloned.1.call-update) | async-done | bytes 524304 | tf_op jit(solution)/shard_map/reduce_scatter | solution.py:438
  861.1 75.1 %all-gather.10.cloned.1.call-done = bf16[2048,2048]{1,0:T(8,128)(2,1)} async-done(((bf16[128,2048]{1,0:T(8,128)(2,1)}), bf16[2048,2048]{1,0:T(8,128)(2,1)}) %all-gather.10.cloned.1.call-update) | async-done | bytes 8388624 | tf_op jit(solution)/shard_map/all_gather | solution.py:435
  936.1 13.8 multiply_convert_fusion.4
  950.0 14.3 fusion.160
  964.3 12.3 fusion.159
  976.6 12.1 multiply_convert_fusion.3
  988.7 14.3 fusion.161
  1003.0 22.8 %add_convert_fusion = bf16[2048,2048]{1,0:T(8,128)(2,1)} fusion(f32[2048,2048]{1,0:T(8,128)} %fusion.161, f32[2048,2048]{1,0:T(8,128)} %fusion.159, f32[2048,2048]{1,0:T(8,128)} %fusion.160, bf16[2048,704]{0,1:T(8,128)(2,1)S(1)} %get-tuple-element.74, bf16[2048,704]{0,1:T(8,128)(2,1)} %collective-permute-done.4), kind=kOutput, calls=%fused_computation.5 | convolution fusion | flops 5922357248 | bytes 64487424 | tf_op jit(solution)/shard_map/dot_general | solution.py:39
  1026.0 103.0 %reduce-scatter.9.cloned.1.call-done = bf16[128,2048]{1,0:T(8,128)(2,1)} async-done(((bf16[2048,2048]{1,0:T(8,128)(2,1)}), bf16[128,2048]{1,0:T(8,128)(2,1)}) %reduce-scatter.9.cloned.1.call-update) | async-done | bytes 524304 | tf_op jit(solution)/shard_map/reduce_scatter | solution.py:438
  1134.2 10.8 convolution_convert_fusion.3
  1148.8 10.7 convolution_convert_fusion.4
  1160.0 50.7 %collective-permute-done.13 = bf16[2048,704]{0,1:T(8,128)(2,1)} collective-permute-done((bf16[2048,704]{0,1:T(8,128)(2,1)}, bf16[2048,704]{0,1:T(8,128)(2,1)}, u32[]{:S(2)}, u32[]{:S(2)}) %collective-permute-start.13) | collective-permute-done | bytes 2883616 | tf_op jit(solution)/shard_map/ppermute | solution.py:491
  1210.7 10.2 add_convert_fusion.2
  1227.4 10.6 fusion.24
  1247.3 13.5 multiply_reduce_fusion.1
  1264.1 9.1 multiply_reduce_fusion
  1277.1 8.6 multiply_convert_fusion
  1291.6 9.3 fusion.33
  1301.3 11.8 multiply_convert_fusion.1
  1348.6 11.0 convolution_convert_fusion
  1361.5 10.1 add_convert_fusion.3
  1379.8 11.3 convolution_convert_fusion.5
  1393.4 8.5 convolution_convert_fusion.6
  1403.6 9.6 collective-permute-start.9
  1413.2 10.5 convolution_convert_fusion.2
  1423.7 52.7 %all-to-all-done.9 = bf16[8,256,704]{1,2,0:T(8,128)(2,1)S(1)} async-done(((bf16[8,256,704]{1,2,0:T(8,128)(2,1)}), bf16[8,256,704]{1,2,0:T(8,128)(2,1)S(1)}, u32[]{:S(2)}, u32[]{:S(2)}) %all-to-all-start.9) | async-done | bytes 2883616 | tf_op jit(solution)/shard_map/all_to_all | solution.py:613
  1483.7 13.3 collective-permute-start.6
  1504.2 19.1 %collective-permute-done.7 = bf16[8,128,768]{2,1,0:T(8,128)(2,1)} collective-permute-done((bf16[8,128,768]{2,1,0:T(8,128)(2,1)}, bf16[8,128,768]{2,1,0:T(8,128)(2,1)}, u32[]{:S(2)}, u32[]{:S(2)}) %collective-permute-start.7) | collective-permute-done | bytes 1572896 | tf_op jit(solution)/shard_map/ppermute | solution.py:673
  1539.1 11.4 add_bitcast_fusion
  1593.2 44.1 %all-reduce = (f32[]{:T(128)}, f32[2,2048]{1,0:T(2,128)}) all-reduce(f32[]{:T(128)} %get-tuple-element.64, f32[2,2048]{1,0:T(2,128)S(1)} %pad_maximum_fusion.9), channel_id=1, replica_groups=mesh['dp'=8,'y'=2,'c'=2] {'dp','y','c'}, use_global_device_ids=true, to_apply=%region_15.16 | all-reduce | flops 4097 | bytes 32776 | tf_op jit(solution)/shard_map/psum | solution.py:692
  (406 shorter events, 310.4 us)
Async XLA Ops:
  7.2 13.2 all-to-all-start
  11.6 197.4 %all-gather.6.cloned.1.call-start = ((), (), s32[]{:S(2)}) async-start(), calls=%async_computation.15 | async-start | bytes 8912896 | tf_op jit(solution)/shard_map/all_gather | solution.py:435
  12.4 394.5 %copy-start.62 = (f32[1,2048]{1,0:T(1,128)}, f32[1,2048]{1,0:T(1,128)S(1)}, u32[]{:S(2)}) copy-start(f32[1,2048]{1,0:T(1,128)S(1)} %get-tuple-element.108) | copy-start | bytes 24580
  20.6 384.4 %copy-start.6 = (f32[4,16,8,512]{3,2,0,1:T(8,128)}, f32[4,16,8,512]{3,2,0,1:T(8,128)S(1)}, u32[]{:S(2)}) copy-start(f32[4,16,8,512]{3,2,0,1:T(8,128)S(1)} %copy.470) | copy-start | bytes 3145732
  22.5 382.6 %reduce-scatter.5.cloned.1.call-start = ((), (), s32[]{:S(2)}) async-start(), calls=%async_computation.16 | async-start | bytes 8912896 | tf_op jit(solution)/shard_map/reduce_scatter | solution.py:438
  35.5 3.2 collective-permute-start
  40.9 124.5 %copy-start.73 = (s32[2,256,2]{1,2,0:T(2,128)S(1)}, s32[2,256,2]{1,2,0:T(2,128)}, u32[]{:S(2)}) copy-start(s32[2,256,2]{1,2,0:T(2,128)} %param.20) | copy-start | bytes 12292
  40.9 124.5 %copy-start.74 = (s32[2,256,2]{1,2,0:T(2,128)S(1)}, s32[2,256,2]{1,2,0:T(2,128)}, u32[]{:S(2)}) copy-start(s32[2,256,2]{1,2,0:T(2,128)} %param.18) | copy-start | bytes 12292
  40.9 124.5 %copy-start.78 = (s32[2,256,2]{1,2,0:T(2,128)S(1)}, s32[2,256,2]{1,2,0:T(2,128)}, u32[]{:S(2)}) copy-start(s32[2,256,2]{1,2,0:T(2,128)} %param.17) | copy-start | bytes 12292
  40.9 124.5 %copy-start.79 = (s32[2,256,2]{1,2,0:T(2,128)S(1)}, s32[2,256,2]{1,2,0:T(2,128)}, u32[]{:S(2)}) copy-start(s32[2,256,2]{1,2,0:T(2,128)} %param.19) | copy-start | bytes 12292
  142.6 53.6 %collective-permute-start.1 = (bf16[8,128,1280]{2,1,0:T(8,128)(2,1)}, bf16[8,128,1280]{2,1,0:T(8,128)(2,1)}, u32[]{:S(2)}, u32[]{:S(2)}) collective-permute-start(bf16[8,128,1280]{2,1,0:T(8,128)(2,1)} %all_to_all.55), channel_id=1, source_target_pairs={{0,0},{1,2},{2,1},{3,3},{4,4},{5,6},{6,5},{7,7},{8,8},{9,10},{10,9... | collective-permute-start | bytes 7864328 | tf_op jit(solution)/shard_map/ppermute | solution.py:474
  163.7 39.2 %collective-permute-start.2 = (bf16[8,128,1280]{2,1,0:T(8,128)(2,1)}, bf16[8,128,1280]{2,1,0:T(8,128)(2,1)}, u32[]{:S(2)}, u32[]{:S(2)}) collective-permute-start(bf16[8,128,1280]{2,1,0:T(8,128)(2,1)} %all_to_all.55), channel_id=1, source_target_pairs={{0,2},{1,0},{2,3},{3,1},{4,6},{5,4},{6,7},{7,5},{8,10},{9,8},{10,1... | collective-permute-start | bytes 7864328 | tf_op jit(solution)/shard_map/ppermute | solution.py:475
  196.1 93.6 %copy-start.46 = (f32[1,4,16,128]{3,1,2,0:T(4,128)}, f32[1,4,16,128]{3,1,2,0:T(4,128)S(1)}, u32[]{:S(2)}) copy-start(f32[1,4,16,128]{3,1,2,0:T(4,128)S(1)} %copy.529) | copy-start | bytes 98308
  300.4 305.3 %all-gather.8.cloned.1.call-start = ((), (), s32[]{:S(2)}) async-start(), calls=%async_computation.17 | async-start | bytes 8912896 | tf_op jit(solution)/shard_map/all_gather | solution.py:435
  412.4 118.0 %all-to-all-start.2 = ((bf16[8,256,704]{1,2,0:T(8,128)(2,1)}), bf16[8,256,704]{1,2,0:T(8,128)(2,1)}, u32[]{:S(2)}, u32[]{:S(2)}) async-start(bf16[8,256,704]{1,2,0:T(8,128)(2,1)} %bitcast.385), calls=%async_computation.3 | async-start | bytes 5767168 | tf_op jit(solution)/shard_map/all_to_all | solution.py:488
  530.4 69.5 %all-to-all-start.3 = ((bf16[8,256,704]{1,2,0:T(8,128)(2,1)}), bf16[8,256,704]{1,2,0:T(8,128)(2,1)}, u32[]{:S(2)}, u32[]{:S(2)}) async-start(bf16[8,256,704]{1,2,0:T(8,128)(2,1)} %bitcast.383), calls=%async_computation.4 | async-start | bytes 5767168 | tf_op jit(solution)/shard_map/all_to_all | solution.py:488
  534.8 324.1 %reduce-scatter.7.cloned.1.call-start = ((), (), s32[]{:S(2)}) async-start(), calls=%async_computation.18 | async-start | bytes 8912896 | tf_op jit(solution)/shard_map/reduce_scatter | solution.py:438
  534.8 203.9 %collective-permute-start.5 = (bf16[704,2048]{1,0:T(8,128)(2,1)}, bf16[704,2048]{1,0:T(8,128)(2,1)}, u32[]{:S(2)}, u32[]{:S(2)}) collective-permute-start(bf16[704,2048]{1,0:T(8,128)(2,1)} %bitcast.448), channel_id=1, source_target_pairs={{0,2},{2,0},{1,3},{3,1},{4,6},{6,4},{5,7},{7,5},{8,10},{10,8},{9,1... | collective-permute-start | bytes 8650760 | tf_op jit(solution)/shard_map/ppermute | solution.py:491
  603.6 65.7 %collective-permute-start.3 = (bf16[2048,704]{0,1:T(8,128)(2,1)}, bf16[2048,704]{0,1:T(8,128)(2,1)}, u32[]{:S(2)}, u32[]{:S(2)}) collective-permute-start(bf16[2048,704]{0,1:T(8,128)(2,1)} %bitcast.143), channel_id=1, source_target_pairs={{0,2},{2,0},{1,3},{3,1},{4,6},{6,4},{5,7},{7,5},{8,10},{10,8},{9,1... | collective-permute-start | bytes 8650760 | tf_op jit(solution)/shard_map/ppermute | solution.py:491
  605.1 123.6 %collective-permute-start.4 = (bf16[2048,704]{0,1:T(8,128)(2,1)}, bf16[2048,704]{0,1:T(8,128)(2,1)}, u32[]{:S(2)}, u32[]{:S(2)}) collective-permute-start(bf16[2048,704]{0,1:T(8,128)(2,1)} %bitcast.145), channel_id=1, source_target_pairs={{0,2},{2,0},{1,3},{3,1},{4,6},{6,4},{5,7},{7,5},{8,10},{10,8},{9,1... | collective-permute-start | bytes 8650760 | tf_op jit(solution)/shard_map/ppermute | solution.py:491
  626.4 51.0 %copy-start.84 = (bf16[2048,704]{0,1:T(8,128)(2,1)}, bf16[2048,704]{0,1:T(8,128)(2,1)S(1)}, u32[]{:S(2)}) copy-start(bf16[2048,704]{0,1:T(8,128)(2,1)S(1)} %get-tuple-element.127) | copy-start | bytes 8650756
  626.4 51.0 %copy-start.83 = (bf16[1,704,2048]{2,1,0:T(8,128)(2,1)S(1)}, bf16[1,704,2048]{2,1,0:T(8,128)(2,1)}, u32[]{:S(2)}) copy-start(bf16[1,704,2048]{2,1,0:T(8,128)(2,1)} %param.27) | copy-start | bytes 8650756
  677.4 51.4 %copy-start.85 = (f32[2048,704]{0,1:T(8,128)}, f32[2048,704]{0,1:T(8,128)S(1)}, u32[]{:S(2)}) copy-start(f32[2048,704]{0,1:T(8,128)S(1)} %fusion.158) | copy-start | bytes 17301508
  753.6 27.0 %all-to-all-start.5 = ((bf16[4,128,512]{2,1,0:T(8,128)(2,1)}), bf16[4,128,512]{2,1,0:T(8,128)(2,1)S(1)}, u32[]{:S(2)}, u32[]{:S(2)}) async-start(bf16[4,128,512]{2,1,0:T(8,128)(2,1)} %bitcast.51), calls=%async_computation.7 | async-start | bytes 1048576 | tf_op jit(solution)/shard_map/all_to_all | solution.py:426
  757.1 179.1 %all-gather.10.cloned.1.call-start = ((), (), s32[]{:S(2)}) async-start(), calls=%async_computation.19 | async-start | bytes 8912896 | tf_op jit(solution)/shard_map/all_gather | solution.py:435
  861.0 267.9 %reduce-scatter.9.cloned.1.call-start = ((), (), s32[]{:S(2)}) async-start(), calls=%async_computation.20 | async-start | bytes 8912896 | tf_op jit(solution)/shard_map/reduce_scatter | solution.py:438
  1025.9 103.1 %copy-start.18 = (bf16[128,2048]{1,0:T(8,128)(2,1)S(1)}, bf16[128,2048]{1,0:T(8,128)(2,1)}, u32[]{:S(2)}) copy-start(bf16[128,2048]{1,0:T(8,128)(2,1)} %reduce-scatter.7.cloned.1.call-done) | copy-start | bytes 1572868
  1025.9 103.1 %copy-start.63 = (f32[1,2048]{1,0:T(1,128)S(1)}, f32[1,2048]{1,0:T(1,128)}, u32[]{:S(2)}) copy-start(f32[1,2048]{1,0:T(1,128)} %copy-done.62) | copy-start | bytes 24580
  1025.9 103.1 %copy-start.72 = (f32[128]{0:T(128)S(1)}, f32[128]{0:T(128)}, u32[]{:S(2)}) copy-start(f32[128]{0:T(128)} %copy-done.71) | copy-start | bytes 1540
  1025.9 105.4 %copy-start.81 = (f32[128]{0:T(128)S(1)}, f32[128]{0:T(128)}, u32[]{:S(2)}) copy-start(f32[128]{0:T(128)} %get-tuple-element.117) | copy-start | bytes 1540
  1025.9 201.5 %all-gather.12.cloned.1.call-start = ((), (), s32[]{:S(2)}) async-start(), calls=%async_computation.21 | async-start | bytes 8912896 | tf_op jit(solution)/shard_map/all_gather | solution.py:435
  1145.0 65.7 %collective-permute-start.13 = (bf16[2048,704]{0,1:T(8,128)(2,1)}, bf16[2048,704]{0,1:T(8,128)(2,1)}, u32[]{:S(2)}, u32[]{:S(2)}) collective-permute-start(bf16[2048,704]{0,1:T(8,128)(2,1)} %convolution_convert_fusion.3), channel_id=1, source_target_pairs={{0,2},{2,0},{1,3},{3,1},{4,6},{6,4},{5,7},{7,5},{8,10},{10,8},{9,1... | collective-permute-start | bytes 8650760 | tf_op jit(solution)/shard_map/ppermute | solution.py:491
  1148.8 61.9 %copy-start.90 = (bf16[2048,704]{0,1:T(8,128)(2,1)S(1)}, bf16[2048,704]{0,1:T(8,128)(2,1)}, u32[]{:S(2)}) copy-start(bf16[2048,704]{0,1:T(8,128)(2,1)} %copy-done.89) | copy-start | bytes 8650756
  1159.5 200.3 %collective-permute-start.12 = (bf16[2048,704]{0,1:T(8,128)(2,1)}, bf16[2048,704]{0,1:T(8,128)(2,1)}, u32[]{:S(2)}, u32[]{:S(2)}) collective-permute-start(bf16[2048,704]{0,1:T(8,128)(2,1)} %convolution_convert_fusion.4), channel_id=1, source_target_pairs={{0,2},{2,0},{1,3},{3,1},{4,6},{6,4},{5,7},{7,5},{8,10},{10,8},{9,1... | collective-permute-start | bytes 8650760 | tf_op jit(solution)/shard_map/ppermute | solution.py:491
  1222.7 150.7 %all-to-all-start.10 = ((bf16[8,256,704]{1,2,0:T(8,128)(2,1)}), bf16[8,256,704]{1,2,0:T(8,128)(2,1)}, u32[]{:S(2)}, u32[]{:S(2)}) async-start(bf16[8,256,704]{1,2,0:T(8,128)(2,1)} %bitcast.354), calls=%async_computation.14 | async-start | bytes 5767168 | tf_op jit(solution)/shard_map/all_to_all | solution.py:613
  1227.1 352.8 %reduce-scatter.11.cloned.1.call-start = ((), (), s32[]{:S(2)}) async-start(), calls=%async_computation.22 | async-start | bytes 8912896 | tf_op jit(solution)/shard_map/reduce_scatter | solution.py:438
  1373.4 103.0 %all-to-all-start.9 = ((bf16[8,256,704]{1,2,0:T(8,128)(2,1)}), bf16[8,256,704]{1,2,0:T(8,128)(2,1)S(1)}, u32[]{:S(2)}, u32[]{:S(2)}) async-start(bf16[8,256,704]{1,2,0:T(8,128)(2,1)} %bitcast.384), calls=%async_computation.13 | async-start | bytes 5767168 | tf_op jit(solution)/shard_map/all_to_all | solution.py:613
  1391.1 148.0 %collective-permute-start.14 = (bf16[704,2048]{1,0:T(8,128)(2,1)}, bf16[704,2048]{1,0:T(8,128)(2,1)}, u32[]{:S(2)}, u32[]{:S(2)}) collective-permute-start(bf16[704,2048]{1,0:T(8,128)(2,1)} %convolution_convert_fusion.5), channel_id=1, source_target_pairs={{0,2},{2,0},{1,3},{3,1},{4,6},{6,4},{5,7},{7,5},{8,10},{10,8},{9,1... | collective-permute-start | bytes 8650760 | tf_op jit(solution)/shard_map/ppermute | solution.py:491
  1403.6 93.4 %collective-permute-start.10 = (bf16[8,128,512]{2,1,0:T(8,128)(2,1)}, bf16[8,128,512]{2,1,0:T(8,128)(2,1)}, u32[]{:S(2)}, u32[]{:S(2)}) collective-permute-start(bf16[8,128,512]{2,1,0:T(8,128)(2,1)} %get-tuple-element.92), channel_id=1, source_target_pairs={{2,0},{0,1},{3,2},{1,3},{6,4},{4,5},{7,6},{5,7},{10,8},{8,9},{11,1... | collective-permute-start | bytes 3145736 | tf_op jit(solution)/shard_map/ppermute | solution.py:673
  1403.6 93.4 %collective-permute-start.9 = (bf16[8,128,512]{2,1,0:T(8,128)(2,1)}, bf16[8,128,512]{2,1,0:T(8,128)(2,1)}, u32[]{:S(2)}, u32[]{:S(2)}) collective-permute-start(bf16[8,128,512]{2,1,0:T(8,128)(2,1)} %get-tuple-element.91), channel_id=1, source_target_pairs={{0,0},{2,1},{1,2},{3,3},{4,4},{6,5},{5,6},{7,7},{8,8},{10,9},{9,10... | collective-permute-start | bytes 3145736 | tf_op jit(solution)/shard_map/ppermute | solution.py:673
  1476.4 23.5 %all-to-all-start.4 = ((bf16[4,128,512]{2,1,0:T(8,128)(2,1)}), bf16[4,128,512]{2,1,0:T(8,128)(2,1)S(1)}, u32[]{:S(2)}, u32[]{:S(2)}) async-start(bf16[4,128,512]{2,1,0:T(8,128)(2,1)} %bitcast.414), calls=%async_computation.6 | async-start | bytes 1048576 | tf_op jit(solution)/shard_map/all_to_all | solution.py:431
  1483.7 20.4 %collective-permute-start.6 = (bf16[8,128,768]{2,1,0:T(8,128)(2,1)}, bf16[8,128,768]{2,1,0:T(8,128)(2,1)}, u32[]{:S(2)}, u32[]{:S(2)}) collective-permute-start(bf16[8,128,768]{2,1,0:T(8,128)(2,1)} %get-tuple-element.87), channel_id=1, source_target_pairs={{0,0},{2,1},{1,2},{3,3},{4,4},{6,5},{5,6},{7,7},{8,8},{10,9},{9,10... | collective-permute-start | bytes 4718600 | tf_op jit(solution)/shard_map/ppermute | solution.py:673
  1497.0 26.2 %collective-permute-start.7 = (bf16[8,128,768]{2,1,0:T(8,128)(2,1)}, bf16[8,128,768]{2,1,0:T(8,128)(2,1)}, u32[]{:S(2)}, u32[]{:S(2)}) collective-permute-start(bf16[8,128,768]{2,1,0:T(8,128)(2,1)} %get-tuple-element.88), channel_id=1, source_target_pairs={{2,0},{0,1},{3,2},{1,3},{6,4},{4,5},{7,6},{5,7},{10,8},{8,9},{11,1... | collective-permute-start | bytes 4718600 | tf_op jit(solution)/shard_map/ppermute | solution.py:673
  1499.9 31.0 %all-to-all-start.8 = ((bf16[8,128,512]{2,1,0:T(8,128)(2,1)}), bf16[8,128,512]{2,1,0:T(8,128)(2,1)}, u32[]{:S(2)}, u32[]{:S(2)}) async-start(bf16[8,128,512]{2,1,0:T(8,128)(2,1)} %add_convert_fusion.7), calls=%async_computation.12 | async-start | bytes 2097152 | tf_op jit(solution)/shard_map/all_to_all | solution.py:676
  1530.9 43.0 %all-to-all-start.7 = ((bf16[8,128,768]{2,1,0:T(8,128)(2,1)}), bf16[8,128,768]{2,1,0:T(8,128)(2,1)}, u32[]{:S(2)}, u32[]{:S(2)}) async-start(bf16[8,128,768]{2,1,0:T(8,128)(2,1)} %add_convert_fusion.6), calls=%async_computation.11 | async-start | bytes 3145728 | tf_op jit(solution)/shard_map/all_to_all | solution.py:676
  1538.4 32.7 %collective-permute-start.11 = (bf16[4,128,512]{1,2,0:T(8,128)(2,1)}, bf16[4,128,512]{1,2,0:T(8,128)(2,1)}, u32[]{:S(2)}, u32[]{:S(2)}) collective-permute-start(bf16[4,128,512]{1,2,0:T(8,128)(2,1)} %bitcast.424), channel_id=1, source_target_pairs={{0,1},{1,0},{2,3},{3,2},{4,5},{5,4},{6,7},{7,6},{8,9},{9,8},{10,11... | collective-permute-start | bytes 1572872 | tf_op jit(solution)/shard_map/ppermute | solution.py:679
  1578.7 9.3 collective-permute-start.8
  1583.8 54.2 %all-to-all-start.6 = ((f32[4,128,512]{2,1,0:T(8,128)}), f32[4,128,512]{2,1,0:T(8,128)}, u32[]{:S(2)}, u32[]{:S(2)}) async-start(f32[4,128,512]{2,1,0:T(8,128)} %bitcast.358), calls=%async_computation.10 | async-start | bytes 2097152 | tf_op jit(solution)/shard_map/all_to_all | solution.py:431
  (85 other events, 904.9 us)
Sparse Core Ops, SparseCore 0:
  22.6 115.4 all-gather.5
  300.5 104.5 reduce-scatter.4
  407.9 127.7 all-gather.7
  753.7 105.0 reduce-scatter.6
  861.5 74.6 all-gather.9
  1026.0 102.8 reduce-scatter.8
  1134.3 74.6 all-gather.11
  1359.8 147.6 reduce-scatter.10

commit v2 on v1

--- a/solution.py
+++ b/solution.py
@@ -1,6 +1,10 @@
+import functools
+
 import jax
 import jax.numpy as jnp
 from jax import lax
+from jax.experimental import pallas as pl
+from jax.experimental.pallas import tpu as pltpu
 from jax.sharding import Mesh
 from jax.sharding import PartitionSpec as P
 
@@ -389,6 +393,247 @@
     return jnp.dot(left, right, preferred_element_type=jnp.float32)
 
 
+BLOCK = 128
+MASKED = -1e30
+NT_DIMS = (((1,), (1,)), ((), ()))
+ROOM = 56 * 1024 * 1024
+
+
+def nt(left, right):
+    return lax.dot_general(left, right, NT_DIMS, preferred_element_type=jnp.float32)
+
+
+def spin(value, cosine, sine):
+    return value * cosine + pltpu.roll(value, HEAD // 2, 1) * sine
+
+
+def stack_experts(block, count):
+    return jnp.concatenate([block[:, e * HEAD : (e + 1) * HEAD] for e in range(count)], axis=0)
+
+
+def near_mask(columns):
+    key_at = lax.broadcasted_iota(jnp.int32, (BLOCK, columns), 0)
+    row_at = lax.broadcasted_iota(jnp.int32, (BLOCK, columns), 1) % BLOCK
+    return key_at <= row_at
+
+
+def attend_kernel(
+    prompts, experts, front, cosine, sine, gate, mixed, query_out, pair_out, log_out, key_far, value_far
+):
+    step = pl.program_id(0)
+    wide = experts * HEAD
+    scale = HEAD ** (-0.5)
+
+    @pl.when(step == 0)
+    def _():
+        key_far[...] = jnp.zeros_like(key_far)
+        value_far[...] = jnp.zeros_like(value_far)
+
+    cos, sin = cosine[...], sine[...]
+    key = spin(front[:, wide : wide + HEAD], cos, sin).astype(jnp.bfloat16)
+    value_up = front[:, wide + HEAD : wide + 2 * HEAD].T.astype(jnp.bfloat16)
+    pair_out[:, :HEAD] = key
+    pair_out[:, HEAD:] = front[:, wide + HEAD : wide + 2 * HEAD].astype(jnp.bfloat16)
+    for e in range(experts):
+        query_out[:, e * HEAD : (e + 1) * HEAD] = spin(
+            front[:, e * HEAD : (e + 1) * HEAD], cos, sin
+        ).astype(jnp.bfloat16)
+    query = stack_experts(query_out[...], experts)
+    near = jnp.where(near_mask(wide), nt(key, query) * scale, MASKED)
+    far_tiles = jnp.minimum(step, prompts)
+
+    def finish(width):
+        far = nt(key_far[:width, :], query) * scale
+        key_at = lax.broadcasted_iota(jnp.int32, far.shape, 0)
+        far = jnp.where(key_at < far_tiles * BLOCK, far, MASKED)
+        peak = jnp.maximum(
+            jnp.max(far, axis=0, keepdims=True), jnp.max(near, axis=0, keepdims=True)
+        )
+        far = jnp.exp(far - peak)
+        close = jnp.exp(near - peak)
+        total = jnp.sum(far, axis=0, keepdims=True) + jnp.sum(close, axis=0, keepdims=True)
+        mix = jnp.dot(
+            value_far[:, :width], far.astype(jnp.bfloat16), preferred_element_type=jnp.float32
+        ) + jnp.dot(value_up, close.astype(jnp.bfloat16), preferred_element_type=jnp.float32)
+        mix = mix * (gate[0] / total)
+        log_out[0] = peak + jnp.log(total)
+        for e in range(experts):
+            mixed[:, e * HEAD : (e + 1) * HEAD] = mix[:, e * BLOCK : (e + 1) * BLOCK].T.astype(
+                jnp.bfloat16
+            )
+
+    split = prompts // 2
+
+    @pl.when(step <= split)
+    def _():
+        finish(split * BLOCK)
+
+    @pl.when(step > split)
+    def _():
+        finish(prompts * BLOCK)
+
+    @pl.when(step < prompts)
+    def _():
+        at = pl.multiple_of(step * BLOCK, BLOCK)
+        key_far[pl.ds(at, BLOCK), :] = key
+        value_far[:, pl.ds(at, BLOCK)] = value_up
+
+
+def attend(front, cosine, sine, gate, prompts, experts):
+    rows, lanes = front.shape
+    blocks = rows // BLOCK
+    wide = experts * HEAD
+    at = lambda i: (i, 0)
+    line = pl.BlockSpec((1, 1, experts * BLOCK), lambda i: (i, 0, 0))
+    return pl.pallas_call(
+        functools.partial(attend_kernel, prompts, experts),
+        grid=(blocks,),
+        in_specs=[
+            pl.BlockSpec((BLOCK, lanes), at),
+            pl.BlockSpec((BLOCK, HEAD), at),
+            pl.BlockSpec((BLOCK, HEAD), at),
+            line,
+        ],
+        out_specs=[
+            pl.BlockSpec((BLOCK, wide), at),
+            pl.BlockSpec((BLOCK, wide), at),
+            pl.BlockSpec((BLOCK, 2 * HEAD), at),
+            line,
+        ],
+        out_shape=[
+            jax.ShapeDtypeStruct((rows, wide), jnp.bfloat16),
+            jax.ShapeDtypeStruct((rows, wide), jnp.bfloat16),
+            jax.ShapeDtypeStruct((rows, 2 * HEAD), jnp.bfloat16),
+            jax.ShapeDtypeStruct((blocks, 1, experts * BLOCK), jnp.float32),
+        ],
+        scratch_shapes=[
+            pltpu.VMEM((prompts * BLOCK, HEAD), jnp.bfloat16),
+            pltpu.VMEM((HEAD, prompts * BLOCK), jnp.bfloat16),
+        ],
+        compiler_params=pltpu.CompilerParams(
+            dimension_semantics=("arbitrary",), vmem_limit_bytes=ROOM
+        ),
+        cost_estimate=pl.CostEstimate(
+            flops=4 * rows * experts * HEAD * prompts * BLOCK,
+            transcendentals=rows * experts * prompts * BLOCK,
+            bytes_accessed=rows * lanes * 8,
+        ),
+        name="attend",
+    )(front, cosine, sine, gate)
+
+
+def attend_back_kernel(
+    prompts, experts, pull, gate, query_in, pair, pair_up, log_in, cosine, sine, back, grad_key, grad_value
+):
+    step = pl.program_id(0)
+    wide = experts * HEAD
+    scale = HEAD ** (-0.5)
+
+    @pl.when(step == 0)
+    def _():
+        grad_key[...] = jnp.zeros_like(grad_key)
+        grad_value[...] = jnp.zeros_like(grad_value)
+
+    at = pl.multiple_of(step * BLOCK, BLOCK)
+    here = pl.ds(at, BLOCK)
+    query = stack_experts(query_in[...], experts)
+    grads = jnp.concatenate(
+        [
+            (pull[:, e * HEAD : (e + 1) * HEAD] * gate[:, e : e + 1]).astype(jnp.bfloat16)
+            for e in range(experts)
+        ],
+        axis=0,
+    )
+    level = log_in[0]
+    near = jnp.where(
+        near_mask(wide), jnp.exp(nt(pair[here, :HEAD], query) * scale - level), 0.0
+    )
+    near_pull = nt(pair[here, HEAD:], grads)
+    far_tiles = jnp.minimum(step, prompts)
+
+    def finish(width):
+        far = jnp.exp(nt(pair[:width, :HEAD], query) * scale - level)
+        key_at = lax.broadcasted_iota(jnp.int32, far.shape, 0)
+        far = jnp.where(key_at < far_tiles * BLOCK, far, 0.0)
+        far_pull = nt(pair[:width, HEAD:], grads)
+        along = jnp.sum(far * far_pull, axis=0, keepdims=True) + jnp.sum(
+            near * near_pull, axis=0, keepdims=True
+        )
+        far_ds = (far * (far_pull - along)).astype(jnp.bfloat16)
+        near_ds = (near * (near_pull - along)).astype(jnp.bfloat16)
+        turned = (
+            jnp.dot(pair_up[:, :width], far_ds, preferred_element_type=jnp.float32)
+            + jnp.dot(pair_up[:, here], near_ds, preferred_element_type=jnp.float32)
+        ) * scale
+        cos, sin = cosine[here, :], sine[here, :]
+        for e in range(experts):
+            back[here, e * HEAD : (e + 1) * HEAD] = spin(
+                turned[:, e * BLOCK : (e + 1) * BLOCK].T, cos, -sin
+            ).astype(jnp.bfloat16)
+        grad_key[:width, :] += jnp.dot(far_ds, query, preferred_element_type=jnp.float32)
+        grad_value[:width, :] += jnp.dot(
+            far.astype(jnp.bfloat16), grads, preferred_element_type=jnp.float32
+        )
+        grad_key[here, :] += jnp.dot(near_ds, query, preferred_element_type=jnp.float32)
+        grad_value[here, :] += jnp.dot(
+            near.astype(jnp.bfloat16), grads, preferred_element_type=jnp.float32
+        )
+
+    split = prompts // 2
+
+    @pl.when(step <= split)
+    def _():
+        finish(split * BLOCK)
+
+    @pl.when(step > split)
+    def _():
+        finish(prompts * BLOCK)
+
+    @pl.when(step == pl.num_programs(0) - 1)
+    def _():
+        back[:, wide : wide + HEAD] = spin(
+            grad_key[...] * scale, cosine[...], -sine[...]
+        ).astype(jnp.bfloat16)
+        back[:, wide + HEAD :] = grad_value[...].astype(jnp.bfloat16)
+
+
+def attend_back(pull, gate, query, pair, pair_up, log_total, cosine, sine, prompts, experts):
+    rows, wide = query.shape
+    blocks = rows // BLOCK
+    at = lambda i: (i, 0)
+    still = lambda i: (0, 0)
+    line = pl.BlockSpec((1, 1, experts * BLOCK), lambda i: (i, 0, 0))
+    return pl.pallas_call(
+        functools.partial(attend_back_kernel, prompts, experts),
+        grid=(blocks,),
+        in_specs=[
+            pl.BlockSpec((BLOCK, wide), at),
+            pl.BlockSpec((BLOCK, experts), at),
+            pl.BlockSpec((BLOCK, wide), at),
+            pl.BlockSpec((rows, 2 * HEAD), still),
+            pl.BlockSpec((HEAD, rows), still),
+            line,
+            pl.BlockSpec((rows, HEAD), still),
+            pl.BlockSpec((rows, HEAD), still),
+        ],
+        out_specs=pl.BlockSpec((rows, wide + 2 * HEAD), still),
+        out_shape=jax.ShapeDtypeStruct((rows, wide + 2 * HEAD), jnp.bfloat16),
+        scratch_shapes=[
+            pltpu.VMEM((rows, HEAD), jnp.float32),
+            pltpu.VMEM((rows, HEAD), jnp.float32),
+        ],
+        compiler_params=pltpu.CompilerParams(
+            dimension_semantics=("arbitrary",), vmem_limit_bytes=ROOM
+        ),
+        cost_estimate=pl.CostEstimate(
+            flops=10 * rows * experts * HEAD * prompts * BLOCK,
+            transcendentals=rows * experts * prompts * BLOCK,
+            bytes_accessed=rows * wide * 12,
+        ),
+        name="attend_back",
+    )(pull, gate, query, pair, pair_up, log_total, cosine, sine)
+
+
 def team_device(
     tokens_in,
     teacher,
@@ -421,15 +666,22 @@
     loss_scale = width * micro_count * row_count * units / 2.0
     scale_root = HEAD ** (-0.5)
 
+    def exchange(parts):
+        spot = 2 * plane + core
+        got = [lax.dynamic_index_in_dim(parts, spot, 0, keepdims=False)]
+        for step in (1, 2, 3):
+            part = lax.dynamic_index_in_dim(parts, spot ^ step, 0, keepdims=False)
+            got.append(lax.ppermute(part, QUAD, [(p, p ^ step) for p in range(4)]))
+        for step, flag in ((1, core), (2, plane)):
+            got = [jnp.where(flag == 0, got[p], got[p ^ step]) for p in range(4)]
+        return got
+
     def to_rows(value):
-        parts = value.reshape(4, half, local_width)
-        got = lax.all_to_all(parts, QUAD, 0, 0, tiled=True)
-        return got.transpose(1, 0, 2).reshape(half, width)
+        return jnp.concatenate(exchange(value.reshape(4, half, local_width)), axis=1)
 
     def from_rows(value):
-        parts = value.reshape(half, 4, local_width).transpose(1, 0, 2)
-        got = lax.all_to_all(parts, QUAD, 0, 0, tiled=True)
-        return got.reshape(micro_count, row_count, local_width)
+        got = exchange(value.reshape(half, 4, local_width).transpose(1, 0, 2))
+        return jnp.stack(got).reshape(micro_count, row_count, local_width)
 
     def collect(value):
         return lax.all_gather(value, TEAM, axis=0, tiled=True)
@@ -444,59 +696,6 @@
 
     field = to_rows(tokens_in).astype(jnp.float32)
     goal = to_rows(teacher).astype(jnp.float32)
-    normed1 = collect((field * root_of(field) * gains[0]).astype(low))
-
-    query_part = w_query.reshape(expert_count, depth, local_heads, HEAD).transpose(1, 2, 0, 3)
-    out_part = w_out.reshape(expert_count, local_heads, HEAD, depth).transpose(3, 1, 0, 2)
-    pair_part = w_keyval.reshape(depth, 2, local_heads, HEAD).transpose(0, 2, 1, 3)
-    wide = expert_count * HEAD
-    packed = jnp.concatenate(
-        [
-            query_part.reshape(depth, local_heads, wide),
-            pair_part.reshape(depth, local_heads, 2 * HEAD),
-            out_part.reshape(depth, local_heads, wide),
-        ],
-        axis=2,
-    )
-    lanes = packed.shape[2]
-    packed = packed.reshape(2, depth // 2, local_heads, lanes).transpose(0, 2, 1, 3)
-    kept_half = lax.dynamic_index_in_dim(packed, core, 0, keepdims=False)
-    sent_half = lax.dynamic_index_in_dim(packed, 1 - core, 0, keepdims=False)
-    got_half = lax.ppermute(sent_half, "c", swap_pairs(2))
-    heads = jnp.concatenate(
-        [
-            jnp.where(core == 0, kept_half, got_half),
-            jnp.where(core == 0, got_half, kept_half),
-        ],
-        axis=0,
-    )
-    heads = lax.all_to_all(heads, "dp", 0, 0, tiled=True)
-    dealt_first = lax.ppermute(heads, QUAD, DEAL_FIRST)
-    dealt_second = lax.ppermute(heads, QUAD, DEAL_SECOND)
-    head_weights = jnp.stack(
-        [
-            jnp.where(plane == 0, dealt_first, dealt_second),
-            jnp.where(plane == 0, dealt_second, dealt_first),
-        ],
-        axis=1,
-    ).reshape(width, lanes)
-    front_weights = head_weights[:, : wide + 2 * HEAD]
-    out_weights = head_weights[:, wide + 2 * HEAD :]
-
-    def spread(value):
-        slabs = value.reshape(depth, units, hidden).transpose(1, 0, 2)
-        return lax.all_to_all(slabs, "dp", 0, 0, tiled=True).reshape(width, hidden)
-
-    def across(value):
-        return lax.ppermute(value, "y", swap_pairs(2))
-
-    down_own = w_down[0]
-    down_far = across(down_own)
-    gate_own = spread(w_gate[0])
-    gate_far = across(gate_own)
-    up_own = spread(w_up[0])
-    up_far = across(up_own)
-
     gate_here = jnp.concatenate(
         [
             gate_rows(mine(attn_routes), mine(attn_share), expert_count),
@@ -504,78 +703,120 @@
         ],
         axis=0,
     )
-    gate_all = lax.all_gather(gate_here, "dp", axis=0, tiled=False)
+    tokens_here = jnp.full((1, row_count), jnp.sum(valid).astype(jnp.float32))
+    gate_here = jnp.concatenate([gate_here, tokens_here], axis=0)
+    slots = jnp.arange(units, dtype=jnp.int32)[:, None, None] == lax.axis_index("dp")
+    gate_all = jnp.where(slots, gate_here[None], 0.0)
+    reach = 1
+    while reach < units:
+        gate_all = gate_all + lax.ppermute(gate_all, "dp", [(i, i ^ reach) for i in range(units)])
+        reach *= 2
+    count = jnp.sum(gate_all[:, -1, 0])
+    normed1 = (field * root_of(field) * gains[0]).astype(low)
+    normed1, gate_all = lax.optimization_barrier((normed1, gate_all))
+    normed1 = collect(normed1)
+
+    query_part = w_query.reshape(expert_count, depth, local_heads, HEAD).transpose(1, 2, 0, 3)
+    out_part = w_out.reshape(expert_count, local_heads, HEAD, depth).transpose(3, 1, 0, 2)
+    pair_part = w_keyval.reshape(depth, 2, local_heads, HEAD).transpose(0, 2, 1, 3)
+    wide = expert_count * HEAD
+    def across(value):
+        return lax.ppermute(value, "y", swap_pairs(2))
+
+    def scatter_heads(value):
+        lanes = value.shape[2]
+        packed = value.reshape(2, depth // 2, local_heads, lanes).transpose(0, 2, 1, 3)
+        kept_half = lax.dynamic_index_in_dim(packed, core, 0, keepdims=False)
+        sent_half = lax.dynamic_index_in_dim(packed, 1 - core, 0, keepdims=False)
+        got_half = lax.ppermute(sent_half, "c", swap_pairs(2))
+        return jnp.concatenate(
+            [
+                jnp.where(core == 0, kept_half, got_half),
+                jnp.where(core == 0, got_half, kept_half),
+            ],
+            axis=0,
+        )
+
+    def deal_heads(heads):
+        first = lax.ppermute(heads, QUAD, DEAL_FIRST)
+        second = lax.ppermute(heads, QUAD, DEAL_SECOND)
+        return jnp.stack(
+            [jnp.where(plane == 0, first, second), jnp.where(plane == 0, second, first)], axis=1
+        ).reshape(width, heads.shape[2])
+
+    def swap_all(value, *later):
+        got = lax.all_to_all(value, "dp", 0, 0, tiled=True)
+        return lax.optimization_barrier((got, *later))
+
+    def slabs_of(value):
+        return value.T.reshape(units, hidden, depth)
+
+    down_own = w_down[0]
+    down_far = across(down_own)
+    front_heads = scatter_heads(
+        jnp.concatenate(
+            [
+                query_part.reshape(depth, local_heads, wide),
+                pair_part.reshape(depth, local_heads, 2 * HEAD),
+            ],
+            axis=2,
+        )
+    )
+    out_heads = scatter_heads(out_part.reshape(depth, local_heads, wide))
+    gate_slabs, up_slabs = slabs_of(w_gate[0]), slabs_of(w_up[0])
+    front_heads, out_heads, down_far = swap_all(front_heads, out_heads, down_far)
+    out_heads, gate_slabs = swap_all(out_heads, gate_slabs)
+    front_weights = deal_heads(front_heads)
     gate_all = (
-        gate_all.reshape(units, 2 * expert_count, 2, half)
+        gate_all[:, :-1].reshape(units, 2 * expert_count, 2, half)
         .transpose(1, 2, 0, 3)
         .reshape(2 * expert_count, team_rows)
     )
+    feed_gate_own = lax.dynamic_index_in_dim(gate_all, expert_count + 2 * plane + core, 0, False)
+    feed_gate_far = lax.dynamic_index_in_dim(gate_all, expert_count + 2 * (1 - plane) + core, 0, False)
+    counted = lax.dynamic_slice_in_dim(mine(valid), core * half, half, 0).astype(jnp.float32)[:, None]
+
+    normed1, gate_all, feed_gate_own, feed_gate_far, count, gate_slabs = lax.optimization_barrier(
+        (normed1, gate_all, feed_gate_own, feed_gate_far, count, gate_slabs)
+    )
+    gate_slabs, up_slabs = swap_all(gate_slabs, up_slabs)
+    gate_own = gate_slabs.transpose(1, 0, 2).reshape(hidden, width)
+    gate_far = across(gate_own)
     attn_gate = gate_all[:expert_count].T
-    feed_gate_own = lax.dynamic_index_in_dim(gate_all, expert_count + 2 * plane + core, 0, False)[:, None]
-    feed_gate_far = lax.dynamic_index_in_dim(
-        gate_all, expert_count + 2 * (1 - plane) + core, 0, False
-    )[:, None]
-    count = lax.psum(jnp.sum(valid).astype(jnp.float32), "dp")
-    counted = lax.dynamic_slice_in_dim(mine(valid), core * half, half, 0).astype(jnp.float32)[:, None]
-
+    blocks = team_rows // BLOCK
+    gate_lines = (
+        gate_all[:expert_count].reshape(expert_count, blocks, BLOCK).transpose(1, 0, 2)
+    ).reshape(blocks, 1, expert_count * BLOCK)
     index = jnp.arange(team_rows, dtype=jnp.int32)
     places = jnp.where(index < prompt_total, index, prompt_total + index % half)
     cosine, sine = rope_tables(places)
+    cosine = jnp.concatenate([cosine, cosine], axis=1)
+    sine = jnp.concatenate([-sine, sine], axis=1)
 
     front = dot(normed1, front_weights)
-    query_rot = turn(
-        front[:, :wide].reshape(team_rows, expert_count, HEAD), cosine[:, None], sine[:, None]
-    ).astype(low)
-    keys = turn(front[:, wide : wide + HEAD], cosine, sine).astype(low)
-    values = front[:, wide + HEAD :].astype(low)
-    prompt_keys, prompt_values = keys[:prompt_total], values[:prompt_total]
-    tail_keys = keys[prompt_total:].reshape(units, half, HEAD)
-    tail_values = values[prompt_total:].reshape(units, half, HEAD)
-    prompt_query = query_rot[:prompt_total].transpose(1, 0, 2)
-    tail_query = query_rot[prompt_total:].reshape(units, half, expert_count, HEAD).transpose(2, 0, 1, 3)
-
-    def product(kind, left, right):
-        return jnp.einsum(kind, left, right, preferred_element_type=jnp.float32)
-
-    seen = index[None, :prompt_total] <= index[:prompt_total, None]
-    prompt_score = jnp.where(
-        seen, product("etd,kd->etk", prompt_query, prompt_keys) * scale_root, -1e30
-    )
-    tail_far = product("ejtd,kd->ejtk", tail_query, prompt_keys) * scale_root
-    tail_near = jnp.where(
-        seen[:half, :half], product("ejtd,jkd->ejtk", tail_query, tail_keys) * scale_root, -1e30
-    )
-
-    prompt_share = jax.nn.softmax(prompt_score, axis=-1)
-    peak = jnp.maximum(
-        jnp.max(tail_far, axis=-1, keepdims=True), jnp.max(tail_near, axis=-1, keepdims=True)
-    )
-    far_raised = jnp.exp(tail_far - peak)
-    near_raised = jnp.exp(tail_near - peak)
-    total = jnp.sum(far_raised, axis=-1, keepdims=True) + jnp.sum(near_raised, axis=-1, keepdims=True)
-    far_share = far_raised / total
-    near_share = near_raised / total
-    prompt_mix = product("etk,kd->etd", prompt_share.astype(low), prompt_values)
-    tail_mix = product("ejtk,kd->ejtd", far_share.astype(low), prompt_values) + product(
-        "ejtk,jkd->ejtd", near_share.astype(low), tail_values
-    )
-    mixed = jnp.concatenate(
-        [prompt_mix.transpose(1, 0, 2), tail_mix.transpose(1, 2, 0, 3).reshape(prompt_total, expert_count, HEAD)],
-        axis=0,
-    )
-    mixed_low = (mixed * attn_gate[:, :, None]).astype(low).reshape(team_rows, wide)
-    hidden1 = field + deliver(times_trans(mixed_low, out_weights))
+    front, out_heads = lax.optimization_barrier((front, out_heads))
+    out_weights = deal_heads(out_heads)
+    mixed_low, query_rot, pair_rot, log_total = attend(
+        front, cosine, sine, gate_lines, units, expert_count
+    )
+    mixed_low, gate_own, up_slabs = lax.optimization_barrier((mixed_low, gate_own, up_slabs))
+    up_slabs = lax.all_to_all(up_slabs, "dp", 0, 0, tiled=True)
+    up_own = up_slabs.transpose(1, 0, 2).reshape(hidden, width)
+    up_far = across(up_own)
+    attn_sum = deliver(times_trans(mixed_low, out_weights))
+    attn_sum, up_own, gate_far = lax.optimization_barrier((attn_sum, up_own, gate_far))
+    hidden1 = field + attn_sum
     normed2 = collect((hidden1 * root_of(hidden1) * gains[1]).astype(low))
 
-    sides = ((gate_own, up_own, down_own, feed_gate_own), (gate_far, up_far, down_far, feed_gate_far))
-    feed_part = jnp.zeros((team_rows, width), jnp.float32)
-    kept = []
-    for gate_w, up_w, down_w, share_col in sides:
-        gate_pre = dot(normed2, gate_w)
-        up_pre = dot(normed2, up_w)
-        inner = (jax.nn.silu(gate_pre) * up_pre * share_col).astype(low)
-        feed_part = feed_part + dot(inner, down_w)
-        kept.append((gate_pre, up_pre, inner))
+    gate_w = jnp.concatenate([gate_own, gate_far], axis=0)
+    up_w = jnp.concatenate([up_own, up_far], axis=0)
+    down_w = jnp.concatenate([down_own, down_far], axis=0)
+    lane = jnp.arange(2 * hidden, dtype=jnp.int32)[None, :]
+    share_cols = jnp.where(lane < hidden, feed_gate_own[:, None], feed_gate_far[:, None])
+    gate_pre = times_trans(normed2, gate_w)
+    up_pre = times_trans(normed2, up_w)
+    inner = (jax.nn.silu(gate_pre) * up_pre * share_cols).astype(low)
+    feed_part = dot(inner, down_w)
     result = hidden1 + deliver(feed_part)
     layer_out = from_rows(result.astype(low))
     differ = result - goal
@@ -583,98 +824,76 @@
     grad_result = counted * differ * (2.0 * (loss_scale / (count * width)))
     grad_rows = collect(grad_result.astype(low))
 
-    grad_norm2_part = jnp.zeros((team_rows, width), jnp.float32)
-    feed_grads = []
-    for (gate_w, up_w, down_w, share_col), (gate_pre, up_pre, inner) in zip(sides, kept):
-        grad_inner = times_trans(grad_rows, down_w) * share_col
-        sigma = jax.nn.sigmoid(gate_pre)
-        grad_gate = (grad_inner * up_pre * sigma * (1.0 + gate_pre * (1.0 - sigma))).astype(low)
-        grad_up = (grad_inner * gate_pre * sigma).astype(low)
-        grad_norm2_part = grad_norm2_part + times_trans(grad_gate, gate_w) + times_trans(grad_up, up_w)
-        feed_grads.append((grad_gate, grad_up, inner))
-    grad_norm2 = deliver(grad_norm2_part)
+    grad_inner = times_trans(grad_rows, down_w) * share_cols
+    sigma = jax.nn.sigmoid(gate_pre)
+    grad_gate = (grad_inner * up_pre * sigma * (1.0 + gate_pre * (1.0 - sigma))).astype(low)
+    grad_up = (grad_inner * gate_pre * sigma).astype(low)
+    grad_norm2 = deliver(dot(grad_gate, gate_w) + dot(grad_up, up_w))
+
+    def weight_sum(left, right):
+        whole = times_rows(left, right)
+        return whole[:hidden], whole[hidden:].astype(low)
+
+    gate_near, gate_sent = weight_sum(grad_gate, normed2)
+    gate_got = across(gate_sent)
+    up_near, up_sent = weight_sum(grad_up, normed2)
+    down_near, down_sent = weight_sum(inner, grad_rows)
+    grad_norm2, gate_near, gate_got, up_near, up_sent, down_near, down_sent = (
+        lax.optimization_barrier(
+            (grad_norm2, gate_near, gate_got, up_near, up_sent, down_near, down_sent)
+        )
+    )
+    up_got = across(up_sent)
     grad_hidden_norm, grad_gain2 = norm_back(hidden1, gains[1], grad_norm2)
     grad_hidden1 = grad_result + grad_hidden_norm
     grad_hidden_rows = collect(grad_hidden1.astype(low))
 
-    (grad_gate_own, grad_up_own, inner_own), (grad_gate_far, grad_up_far, inner_far) = feed_grads
-    down_sum = times_rows(inner_own, grad_rows) + across(
-        times_rows(inner_far, grad_rows).astype(low)
-    ).astype(jnp.float32)
-    gate_sum = times_rows(normed2, grad_gate_own) + across(
-        times_rows(normed2, grad_gate_far).astype(low)
-    ).astype(jnp.float32)
-    up_sum = times_rows(normed2, grad_up_own) + across(
-        times_rows(normed2, grad_up_far).astype(low)
-    ).astype(jnp.float32)
-
-    def gather_back(value):
-        slabs = value.astype(low).reshape(units, depth, hidden)
-        got = lax.all_to_all(slabs, "dp", 0, 0, tiled=True)
-        return got.transpose(1, 0, 2).reshape(depth, units * hidden).astype(jnp.float32)
-
-    grad_gate_out = gather_back(gate_sum)
-    grad_up_out = gather_back(up_sum)
-
-    grad_mixed = (
-        dot(grad_hidden_rows, out_weights).reshape(team_rows, expert_count, HEAD) * attn_gate[:, :, None]
-    ).astype(low)
+    def rows_for_owners(value):
+        return value.astype(low).reshape(hidden, units, depth).transpose(1, 0, 2)
+
+    def own_rows(value):
+        return value.reshape(units * hidden, depth).T.astype(jnp.float32)
+
+    gate_slabs = rows_for_owners(gate_near + gate_got.astype(jnp.float32))
+    gate_slabs = lax.all_to_all(gate_slabs, "dp", 0, 0, tiled=True)
+    grad_hidden_rows, up_got, down_sent, gate_slabs = lax.optimization_barrier(
+        (grad_hidden_rows, up_got, down_sent, gate_slabs)
+    )
+    up_slabs = rows_for_owners(up_near + up_got.astype(jnp.float32))
+    up_slabs = lax.all_to_all(up_slabs, "dp", 0, 0, tiled=True)
+    down_got = across(down_sent)
+
+    front_back = attend_back(
+        dot(grad_hidden_rows, out_weights),
+        attn_gate,
+        query_rot,
+        pair_rot,
+        pair_rot[:, :HEAD].T,
+        log_total,
+        cosine,
+        sine,
+        units,
+        expert_count,
+    )
+    front_back, up_slabs, down_got = lax.optimization_barrier((front_back, up_slabs, down_got))
+    down_sum = down_near + down_got.astype(jnp.float32)
     out_grad = times_rows(grad_hidden_rows, mixed_low)
-    prompt_back = grad_mixed[:prompt_total].transpose(1, 0, 2)
-    tail_back = grad_mixed[prompt_total:].reshape(units, half, expert_count, HEAD).transpose(2, 0, 1, 3)
-    prompt_pull = product("etd,kd->etk", prompt_back, prompt_values)
-    prompt_ds = (
-        prompt_share * (prompt_pull - jnp.sum(prompt_share * prompt_pull, axis=-1, keepdims=True))
-    ).astype(low)
-    far_pull = product("ejtd,kd->ejtk", tail_back, prompt_values)
-    near_pull = product("ejtd,jkd->ejtk", tail_back, tail_values)
-    along = jnp.sum(far_share * far_pull, axis=-1, keepdims=True) + jnp.sum(
-        near_share * near_pull, axis=-1, keepdims=True
-    )
-    far_ds = (far_share * (far_pull - along)).astype(low)
-    near_ds = (near_share * (near_pull - along)).astype(low)
-    prompt_dq = product("etk,kd->etd", prompt_ds, prompt_keys)
-    tail_dq = product("ejtk,kd->ejtd", far_ds, prompt_keys) + product("ejtk,jkd->ejtd", near_ds, tail_keys)
-    prompt_dk = product("etk,etd->kd", prompt_ds, prompt_query) + product(
-        "ejtk,ejtd->kd", far_ds, tail_query
-    )
-    tail_dk = product("ejtk,ejtd->jkd", near_ds, tail_query)
-    prompt_dv = product("etk,etd->kd", prompt_share.astype(low), prompt_back) + product(
-        "ejtk,ejtd->kd", far_share.astype(low), tail_back
-    )
-    tail_dv = product("ejtk,ejtd->jkd", near_share.astype(low), tail_back)
-    grad_query = (
-        jnp.concatenate(
-            [prompt_dq.transpose(1, 0, 2), tail_dq.transpose(1, 2, 0, 3).reshape(prompt_total, expert_count, HEAD)],
-            axis=0,
-        )
-        * scale_root
-    )
-    grad_keys = jnp.concatenate([prompt_dk, tail_dk.reshape(prompt_total, HEAD)], axis=0) * scale_root
-    grad_values = jnp.concatenate([prompt_dv, tail_dv.reshape(prompt_total, HEAD)], axis=0)
-    front_back = jnp.concatenate(
-        [
-            turn(grad_query, cosine[:, None], -sine[:, None]).reshape(team_rows, wide),
-            turn(grad_keys, cosine, -sine),
-            grad_values,
-        ],
-        axis=1,
-    ).astype(low)
     grad_norm1 = deliver(times_trans(front_back, front_weights))
     front_grad = times_rows(normed1, front_back)
     grad_field_norm, grad_gain1 = norm_back(field, gains[0], grad_norm1)
     input_grad = from_rows(grad_hidden1 + grad_field_norm)
 
-    def send_back(value):
-        columns = value.shape[1]
-        halves = value.astype(low).reshape(units, 2, depth // 2, columns)
+    def undeal_heads(value):
+        halves = value.astype(low).reshape(units, 2, depth // 2, value.shape[1])
         first = lax.dynamic_index_in_dim(halves, plane, 1, keepdims=False)
         second = lax.dynamic_index_in_dim(halves, 1 - plane, 1, keepdims=False)
         both = lax.ppermute(first, QUAD, BACK_FIRST).astype(jnp.float32) + lax.ppermute(
             second, QUAD, BACK_SECOND
         ).astype(jnp.float32)
-        got = lax.all_to_all(both.astype(low), "dp", 0, 0, tiled=True)
-        got = got.reshape(2, local_heads, depth // 2, columns)
+        return both.astype(low)
+
+    def gather_heads(value):
+        got = value.reshape(2, local_heads, depth // 2, value.shape[2])
         own = lax.dynamic_index_in_dim(got, core, 0, keepdims=False)
         swapped = lax.ppermute(
             lax.dynamic_index_in_dim(got, 1 - core, 0, keepdims=False), "c", swap_pairs(2)
@@ -684,14 +903,21 @@
         )
         return rows.astype(jnp.float32)
 
-    out_back = send_back(out_grad)
-    front_out = send_back(front_grad)
+    front_heads, out_heads = undeal_heads(front_grad), undeal_heads(out_grad)
+    front_heads, out_heads = swap_all(front_heads, out_heads)
+    out_heads = lax.all_to_all(out_heads, "dp", 0, 0, tiled=True)
+    grad_gate_out, grad_up_out = own_rows(gate_slabs), own_rows(up_slabs)
+    front_out, out_back = gather_heads(front_heads), gather_heads(out_heads)
     grad_out = out_back.reshape(local_heads, depth, expert_count, HEAD).transpose(2, 0, 3, 1)
     grad_query_out = front_out[:, :, :wide].reshape(local_heads, depth, expert_count, HEAD).transpose(2, 1, 0, 3)
     grad_pair = front_out[:, :, wide:].reshape(local_heads, depth, 2, HEAD).transpose(1, 2, 0, 3)
-    gain_total, squared_total = lax.psum(
-        (jnp.stack([grad_gain1, grad_gain2]), squared), ("dp", "y", "c")
-    )
+    totals = jnp.stack([grad_gain1, grad_gain2, jnp.full((width,), squared)])
+    for axis, size in (("c", 2), ("y", 2), ("dp", units)):
+        reach = 1
+        while reach < size:
+            totals = totals + lax.ppermute(totals, axis, [(i, i ^ reach) for i in range(size)])
+            reach *= 2
+    gain_total, squared_total = totals[:2], totals[2, 0]
     return (
         layer_out,
         squared_total / (count * width),

time: 1660 us -> 1280 us (0.77)
  blocking collectives: 198 us -> 0 us
  matrix products: 366 us -> 235 us
  waiting for transfers between devices: 758 us -> 663 us
  Pallas kernels: 0 us -> 63.9 us
  local copies, waits for them, and re-layouts: 125 us -> 98.5 us
  starting transfers between devices: 96.4 us -> 115 us
    reduce_scatter x4, waiting for transfers between devices: 286 us -> 163 us  [deliver(): lax.psum_scatter(value.astype(low), TEAM, scatter_dimension=0, tiled=True)]
    all_to_all x1 -> x0, blocking collectives: 102 us -> none  [team_device(): heads = lax.all_to_all(heads, 'dp', 0, 0, tiled=True)]
    dot_general x17 -> x0, matrix products: 75.7 us -> none  [product(): return jnp.einsum(kind, left, right, preferred_element_type=jnp.float32)]
    psum x2 -> x0, blocking collectives: 65.5 us -> none  [the longest x1 44.1 us: team_device(): lax.psum((jnp.stack([grad_gain1, grad_gain2]), squared), ('dp', 'y', 'c'))]
    pallas_call x0 -> x2, Pallas kernels: none -> 63.9 us  [the longest x1 38.1 us: attend_back(): pl.pallas_call(functools.partial(attend_back_kernel, prompts, experts), g...]
    all_to_all x10 -> x8, waiting for transfers between devices: 234 us -> 187 us  [the longest x2 97.5 us: team_device(): up_slabs = lax.all_to_all(up_slabs, 'dp', 0, 0, tiled=True)]
    ppermute x6, waiting for transfers between devices: 135 us -> 180 us  [across(): return lax.ppermute(value, 'y', swap_pairs(2))]
    all_gather x1 -> x0, blocking collectives: 30.5 us -> none  [team_device(): gate_all = lax.all_gather(gate_here, 'dp', axis=0, tiled=False)]
  transfers between devices with their start and end apart: 33 -> 54, of which waited for: 15 -> 29; matrix products, arithmetic and copies ran while one was open for 22% -> 19% of each run, Pallas kernels for 0% -> 5%
where the time goes in v2:
time: 1280 us; the launch traced here: 1270 us
  waiting for transfers between devices  663 us (52%)
  matrix products  235 us (18%)
  starting transfers between devices  115 us (9%)
  local copies, waits for them, and re-layouts  98.5 us (8%)
  other arithmetic  73.3 us (6%)
  Pallas kernels  63.9 us (5%)
  between operations  18.5 us (1%)
    ppermute x6, waiting for transfers between devices, across(): return lax.ppermute(value, 'y', swap_pairs(2))  180 us
    reduce_scatter x4, waiting for transfers between devices, deliver(): lax.psum_scatter(value.astype(low), TEAM, scatter_dimension=0, tiled=True)  163 us
    all_to_all x2, waiting for transfers between devices, team_device(): up_slabs = lax.all_to_all(up_slabs, 'dp', 0, 0, tiled=True)  97.5 us
    dot_general x5, matrix products, times_trans(): lax.dot_general(left, right, TRANS_DIMS, preferred_element_type=jnp.float32)  88.4 us
    all_gather x4, waiting for transfers between devices, collect(): return lax.all_gather(value, TEAM, axis=0, tiled=True)  88.1 us
    dot_general x5, matrix products, dot(): return jnp.dot(left, right, preferred_element_type=jnp.float32)  76.9 us
    dot_general x5, matrix products, times_rows(): lax.dot_general(left, right, ROWS_DIMS, preferred_element_type=jnp.float32)  70.1 us
    all_to_all x1, waiting for transfers between devices, team_device(): gate_slabs = lax.all_to_all(gate_slabs, 'dp', 0, 0, tiled=True)  47.3 us
  transfers between devices with their start and end apart: 54, of which 29 were waited for; matrix products, arithmetic and copies ran while one was open for 19% of the time, Pallas kernels for 5%

profile of v2, /device:TPU:0, one launch (start us, length us, event | category | flops | bytes accessed | tf_op | source)
XLA Modules:
  0.0 1268.0 jit_solution(5695462474245977619)
XLA Ops:
  43.5 5.6 all-to-all-start
  54.4 49.4 %collective-permute-done.8 = bf16[704,2048]{1,0:T(8,128)(2,1)} collective-permute-done((bf16[704,2048]{1,0:T(8,128)(2,1)}, bf16[704,2048]{1,0:T(8,128)(2,1)}, u32[]{:S(2)}, u32[]{:S(2)}) %collective-permute-start.8) | collective-permute-done | bytes 2883616 | tf_op jit(solution)/shard_map/ppermute | solution.py:724
  103.8 12.8 %all-to-all-done = bf16[8,128,768]{2,1,0:T(8,128)(2,1)} async-done(((bf16[8,128,768]{2,1,0:T(8,128)(2,1)}), bf16[8,128,768]{2,1,0:T(8,128)(2,1)}, u32[]{:S(2)}, u32[]{:S(2)}) %all-to-all-start) | async-done | bytes 1572896 | tf_op jit(solution)/shard_map/all_to_all | solution.py:748
  120.9 13.3 %collective-permute-start.9 = (bf16[8,128,768]{2,1,0:T(8,128)(2,1)}, bf16[8,128,768]{2,1,0:T(8,128)(2,1)}, u32[]{:S(2)}, u32[]{:S(2)}) collective-permute-start(bf16[8,128,768]{2,1,0:T(8,128)(2,1)} %all-to-all-done), channel_id=1, source_target_pairs={{0,0},{1,2},{2,1},{3,3},{4,4},{5,6},{6,5},{7,7},{8,8},{9,10},{10,9... | collective-permute-start | bytes 4718600 | tf_op jit(solution)/shard_map/ppermute | solution.py:741
  140.6 15.7 %all-to-all-done.1 = bf16[8,128,512]{2,1,0:T(8,128)(2,1)} async-done(((bf16[8,128,512]{2,1,0:T(8,128)(2,1)}), bf16[8,128,512]{2,1,0:T(8,128)(2,1)}, u32[]{:S(2)}, u32[]{:S(2)}) %all-to-all-start.1) | async-done | bytes 1048608 | tf_op jit(solution)/shard_map/all_to_all | solution.py:748
  170.9 8.5 fusion.33.front
  179.4 9.6 collective-permute-start.11
  190.9 4.5 copy.104
  197.6 25.8 %attend.1 = (bf16[2048,512]{1,0:T(8,128)(2,1)}, bf16[2048,512]{1,0:T(8,128)(2,1)}, bf16[2048,256]{1,0:T(8,128)(2,1)}, f32[16,1,512]{2,1,0:T(1,128)}) custom-call(f32[2048,768]{1,0:T(8,128)} %fusion.33.front, f32[2048,128]{1,0:T(8,128)} %get-tuple-element.207.cosine, f32[2048,128]{1,0:T(8,128)} %get-tuple-element.208.sine, f32[16,1,512]{2,1,0:T(1,128)} %bitcast.334), custom_call_target="tpu_custom_call" | custom-call | flops 4294967296 | bytes 12582912 | tf_op jit(solution)/shard_map/attend/pallas_call | solution.py:488
  229.3 9.5 convolution_convert_fusion.2
  238.8 6.0 all-to-all-start.3
  245.9 96.8 %all-to-all-done.3 = bf16[8,704,256]{2,1,0:T(8,128)(2,1)} async-done(((bf16[8,704,256]{2,1,0:T(8,128)(2,1)}), bf16[8,704,256]{2,1,0:T(8,128)(2,1)}, u32[]{:S(2)}, u32[]{:S(2)}) %all-to-all-start.3) | async-done | bytes 2883616 | tf_op jit(solution)/shard_map/all_to_all | solution.py:803
  346.4 33.4 %reduce-scatter.5.cloned.1.call-done = bf16[128,2048]{1,0:T(8,128)(2,1)} async-done(((bf16[2048,2048]{1,0:T(8,128)(2,1)}), bf16[128,2048]{1,0:T(8,128)(2,1)}) %reduce-scatter.5.cloned.1.call-update) | async-done | bytes 524304 | tf_op jit(solution)/shard_map/reduce_scatter | solution.py:690
  390.6 57.0 %collective-permute-done.14 = bf16[704,2048]{1,0:T(8,128)(2,1)S(1)} collective-permute-done((bf16[704,2048]{1,0:T(8,128)(2,1)}, bf16[704,2048]{1,0:T(8,128)(2,1)S(1)}, u32[]{:S(2)}, u32[]{:S(2)}) %collective-permute-start.14) | collective-permute-done | bytes 2883616 | tf_op jit(solution)/shard_map/ppermute | solution.py:724
  449.4 8.2 all-gather.7.cloned.1.call-done
  457.6 18.7 %fusion.34 = f32[2048,1408]{1,0:T(8,128)} fusion(bf16[2048,2048]{1,0:T(8,128)(2,1)} %all-gather.7.cloned.1.call-done, bf16[1408,2048]{1,0:T(8,128)(2,1)} %copy-done.21), kind=kOutput, calls=%fused_computation.201 | convolution fusion | flops 11811160064 | bytes 25690112 | tf_op jit(solution)/shard_map/dot_general | solution.py:43
  476.3 23.4 %fusion = (bf16[2048,1408]{1,0:T(8,128)(2,1)}, f32[2048,1408]{1,0:T(8,128)}) fusion(f32[2048,1408]{1,0:T(8,128)} %fusion.34, f32[2048]{0:T(1024)S(1)} %get-tuple-element.74, f32[2048]{0:T(1024)S(1)} %get-tuple-element.73, pred[1408]{0:T(1024)(128)(4,1)S(1)} %iota_compare_fusion, bf16[2048,2048]{1,0:T(8,128)(2,1)} %all-gather.7.cloned.1.call-done, ...), kind=kOutput, calls=%fused_computation.3 | convolution fusion | flops 11834228736 | bytes 43009408 | tf_op jit(solution)/shard_map/dot_general | solution.py:43
  499.7 19.2 %convolution_convert_fusion.1 = bf16[2048,2048]{1,0:T(8,128)(2,1)} fusion(bf16[2048,1408]{1,0:T(8,128)(2,1)} %get-tuple-element.201, bf16[704,2048]{1,0:T(8,128)(2,1)} %collective-permute-done.8, bf16[704,2048]{1,0:T(8,128)(2,1)} %bitcast.338), kind=kOutput, calls=%fused_computation.8 | convolution fusion | flops 11826888704 | bytes 19922944 | tf_op jit(solution)/shard_map/dot_general | solution.py:393
  528.5 93.5 %reduce-scatter.7.cloned.1.call-done = bf16[128,2048]{1,0:T(8,128)(2,1)} async-done(((bf16[2048,2048]{1,0:T(8,128)(2,1)}), bf16[128,2048]{1,0:T(8,128)(2,1)}) %reduce-scatter.7.cloned.1.call-update) | async-done | bytes 524304 | tf_op jit(solution)/shard_map/reduce_scatter | solution.py:690
  624.2 75.2 %all-gather.9.cloned.1.call-done = bf16[2048,2048]{1,0:T(8,128)(2,1)} async-done(((bf16[128,2048]{1,0:T(8,128)(2,1)}), bf16[2048,2048]{1,0:T(8,128)(2,1)}) %all-gather.9.cloned.1.call-update) | async-done | bytes 8388624 | tf_op jit(solution)/shard_map/all_gather | solution.py:687
  699.4 25.5 %multiply_convert_fusion.1 = (bf16[2048,1408]{1,0:T(8,128)(2,1)}, bf16[2048,1408]{1,0:T(8,128)(2,1)}) fusion(f32[2048,1408]{1,0:T(8,128)} %fusion.34, f32[2048,1408]{1,0:T(8,128)} %get-tuple-element.202, f32[2048]{0:T(1024)S(1)} %get-tuple-element.74, f32[2048]{0:T(1024)S(1)} %copy-done.29, pred[1408]{0:T(1024)(128)(4,1)S(1)} %iota_compare_fusion, ...), kind=kOutput, calls=%fused_computation.5 | convolution fusion | flops 11865948160 | bytes 48776576 | tf_op jit(solution)/shard_map/dot_general | solution.py:43
  724.9 19.3 %fusion.35 = f32[2048,2048]{1,0:T(8,128)} fusion(bf16[2048,1408]{1,0:T(8,128)(2,1)} %get-tuple-element.142, bf16[1408,2048]{1,0:T(8,128)(2,1)} %constant_dynamic-update-slice_fusion.4), kind=kOutput, calls=%fused_computation.202 | convolution fusion | flops 11811160064 | bytes 28311552 | tf_op jit(solution)/shard_map/dot_general | solution.py:393
  744.2 19.3 %add_convert_fusion = bf16[2048,2048]{1,0:T(8,128)(2,1)} fusion(f32[2048,2048]{1,0:T(8,128)} %fusion.35, bf16[2048,1408]{1,0:T(8,128)(2,1)S(1)} %copy-done.36, bf16[1408,2048]{1,0:T(8,128)(2,1)} %copy-done.21), kind=kOutput, calls=%fused_computation | convolution fusion | flops 11819548672 | bytes 36700160 | tf_op jit(solution)/shard_map/dot_general | solution.py:393
  763.6 17.1 %fusion.36 = f32[1408,2048]{1,0:T(8,128)S(1)} fusion(bf16[2048,1408]{1,0:T(8,128)(2,1)} %get-tuple-element.141, bf16[2048,2048]{1,0:T(8,128)(2,1)} %all-gather.7.cloned.1.call-done), kind=kOutput, calls=%fused_computation.203 | convolution fusion | flops 11811160064 | bytes 25690112 | tf_op jit(solution)/shard_map/dot_general | solution.py:47
  784.0 17.0 %fusion.37 = f32[1408,2048]{1,0:T(8,128)S(1)} fusion(bf16[2048,1408]{1,0:T(8,128)(2,1)} %get-tuple-element.142, bf16[2048,2048]{1,0:T(8,128)(2,1)} %all-gather.7.cloned.1.call-done), kind=kOutput, calls=%fused_computation.204 | convolution fusion | flops 11811160064 | bytes 25690112 | tf_op jit(solution)/shard_map/dot_general | solution.py:47
  808.8 16.8 %fusion.38 = f32[1408,2048]{1,0:T(8,128)S(1)} fusion(bf16[2048,1408]{1,0:T(8,128)(2,1)} %get-tuple-element.201, bf16[2048,2048]{1,0:T(8,128)(2,1)} %all-gather.9.cloned.1.call-done), kind=kOutput, calls=%fused_computation.205 | convolution fusion | flops 11811160064 | bytes 25690112 | tf_op jit(solution)/shard_map/dot_general | solution.py:47
  830.5 36.1 %reduce-scatter.9.cloned.1.call-done = bf16[128,2048]{1,0:T(8,128)(2,1)} async-done(((bf16[2048,2048]{1,0:T(8,128)(2,1)}), bf16[128,2048]{1,0:T(8,128)(2,1)}) %reduce-scatter.9.cloned.1.call-update) | async-done | bytes 524304 | tf_op jit(solution)/shard_map/reduce_scatter | solution.py:690
  870.8 4.6 add_convert_fusion.2
  883.0 63.0 %collective-permute-done.22 = bf16[704,2048]{1,0:T(8,128)(2,1)} collective-permute-done((bf16[704,2048]{1,0:T(8,128)(2,1)}, bf16[704,2048]{1,0:T(8,128)(2,1)}, u32[]{:S(2)}, u32[]{:S(2)}) %collective-permute-start.22) | collective-permute-done | bytes 2883616 | tf_op jit(solution)/shard_map/ppermute | solution.py:724
  946.0 47.3 %all-to-all-done.4 = bf16[8,704,256]{2,1,0:T(8,128)(2,1)S(1)} async-done(((bf16[8,704,256]{2,1,0:T(8,128)(2,1)}), bf16[8,704,256]{2,1,0:T(8,128)(2,1)S(1)}, u32[]{:S(2)}, u32[]{:S(2)}) %all-to-all-start.4) | async-done | bytes 2883616 | tf_op jit(solution)/shard_map/all_to_all | solution.py:858
  993.3 4.7 all-gather.11.cloned.1.call-done
  998.0 4.6 add_convert_fusion.1
  1014.8 10.5 fusion.39.pull
  1025.3 38.1 %attend_back.1 = bf16[2048,768]{1,0:T(8,128)(2,1)} custom-call(f32[2048,512]{1,0:T(8,128)} %fusion.39.pull, f32[2048,4]{1,0:T(8,128)} %get-tuple-element.168.gate, bf16[2048,512]{1,0:T(8,128)(2,1)} %get-tuple-element.83.query_in, bf16[2048,256]{1,0:T(8,128)(2,1)} %get-tuple-element.84.pair, bf16[128,2048]{1,0:T(8,128)(2,1)} %slice_bitcast_fusion.pair_up, ...), custom_call_target="tpu_custom_call" | custom-call | flops 10737418240 | bytes 12582912 | tf_op jit(solution)/shard_map/attend_back/pallas_call | solution.py:606
  1063.4 10.5 collective-permute-done.23
  1074.6 11.3 convolution_convert_fusion
  1086.0 10.4 convolution_convert_fusion.3
  1098.3 13.4 %collective-permute-start.32 = (bf16[8,128,768]{2,1,0:T(8,128)(2,1)}, bf16[8,128,768]{2,1,0:T(8,128)(2,1)}, u32[]{:S(2)}, u32[]{:S(2)}) collective-permute-start(bf16[8,128,768]{2,1,0:T(8,128)(2,1)} %get-tuple-element.143), channel_id=1, source_target_pairs={{0,0},{2,1},{1,2},{3,3},{4,4},{6,5},{5,6},{7,7},{8,8},{10,9},{9,10... | collective-permute-start | bytes 4718600 | tf_op jit(solution)/shard_map/ppermute | solution.py:890
  1117.4 22.7 %collective-permute-done.16 = bf16[128,512]{1,0:T(8,128)(2,1)S(1)} collective-permute-done((bf16[128,512]{1,0:T(8,128)(2,1)S(1)}, bf16[128,512]{1,0:T(8,128)(2,1)S(1)}, u32[]{:S(2)}, u32[]{:S(2)}) %collective-permute-start.16) | collective-permute-done | bytes 131104 | tf_op jit(solution)/shard_map/ppermute | solution.py:674
  1144.4 4.8 all-to-all-start.6
  1149.2 8.7 convolution_convert_fusion.4
  1160.8 9.4 collective-permute-start.34
  1173.4 6.4 copy.124
  1182.6 7.6 all-to-all-done.6
  1194.5 4.8 convert_bitcast_fusion
  1199.3 6.2 copy.125
  1206.9 7.4 add_bitcast_fusion
  1227.7 6.2 all-to-all-done.7
  (301 shorter events, 209.3 us)
Async XLA Ops:
  7.2 149.1 %all-gather.5.cloned.1.call-start = ((), (), s32[]{:S(2)}) async-start(), calls=%async_computation.12 | async-start | bytes 8912896 | tf_op jit(solution)/shard_map/all_gather | solution.py:687
  8.4 15.9 %collective-permute-start.1 = (bf16[128,512]{1,0:T(8,128)(2,1)S(1)}, bf16[128,512]{1,0:T(8,128)(2,1)S(1)}, u32[]{:S(2)}, u32[]{:S(2)}) collective-permute-start(bf16[128,512]{1,0:T(8,128)(2,1)S(1)} %get-tuple-element.189), channel_id=1, source_target_pairs={{0,2},{1,3},{2,0},{3,1},{4,6},{5,7},{6,4},{7,5},{8,10},{9,11},{10,... | collective-permute-start | bytes 393224 | tf_op jit(solution)/shard_map/ppermute | solution.py:674
  11.5 12.9 %collective-permute-start.2 = (bf16[128,512]{1,0:T(8,128)(2,1)S(1)}, bf16[128,512]{1,0:T(8,128)(2,1)S(1)}, u32[]{:S(2)}, u32[]{:S(2)}) collective-permute-start(bf16[128,512]{1,0:T(8,128)(2,1)S(1)} %get-tuple-element.188), channel_id=1, source_target_pairs={{0,3},{1,2},{2,1},{3,0},{4,7},{5,6},{6,5},{7,4},{8,11},{9,10},{10,... | collective-permute-start | bytes 393224 | tf_op jit(solution)/shard_map/ppermute | solution.py:674
  11.5 12.9 %collective-permute-start = (bf16[128,512]{1,0:T(8,128)(2,1)S(1)}, bf16[128,512]{1,0:T(8,128)(2,1)S(1)}, u32[]{:S(2)}, u32[]{:S(2)}) collective-permute-start(bf16[128,512]{1,0:T(8,128)(2,1)S(1)} %get-tuple-element.187), channel_id=1, source_target_pairs={{0,1},{1,0},{2,3},{3,2},{4,5},{5,4},{6,7},{7,6},{8,9},{9,8},{10,11... | collective-permute-start | bytes 393224 | tf_op jit(solution)/shard_map/ppermute | solution.py:674
  16.7 5.8 collective-permute-start.3
  22.6 5.0 collective-permute-start.4
  27.7 7.5 collective-permute-start.5
  38.6 65.2 %collective-permute-start.8 = (bf16[704,2048]{1,0:T(8,128)(2,1)}, bf16[704,2048]{1,0:T(8,128)(2,1)}, u32[]{:S(2)}, u32[]{:S(2)}) collective-permute-start(bf16[704,2048]{1,0:T(8,128)(2,1)} %bitcast.337), channel_id=1, source_target_pairs={{0,2},{2,0},{1,3},{3,1},{4,6},{6,4},{5,7},{7,5},{8,10},{10,8},{9,1... | collective-permute-start | bytes 8650760 | tf_op jit(solution)/shard_map/ppermute | solution.py:724
  43.5 73.0 %all-to-all-start = ((bf16[8,128,768]{2,1,0:T(8,128)(2,1)}), bf16[8,128,768]{2,1,0:T(8,128)(2,1)}, u32[]{:S(2)}, u32[]{:S(2)}) async-start(bf16[8,128,768]{2,1,0:T(8,128)(2,1)} %pad_maximum_fusion.5), calls=%async_computation | async-start | bytes 3145728 | tf_op jit(solution)/shard_map/all_to_all | solution.py:748
  116.5 39.8 %all-to-all-start.1 = ((bf16[8,128,512]{2,1,0:T(8,128)(2,1)}), bf16[8,128,512]{2,1,0:T(8,128)(2,1)}, u32[]{:S(2)}, u32[]{:S(2)}) async-start(bf16[8,128,512]{2,1,0:T(8,128)(2,1)} %pad_maximum_fusion.6), calls=%async_computation.1 | async-start | bytes 2097152 | tf_op jit(solution)/shard_map/all_to_all | solution.py:748
  120.9 44.2 %collective-permute-start.9 = (bf16[8,128,768]{2,1,0:T(8,128)(2,1)}, bf16[8,128,768]{2,1,0:T(8,128)(2,1)}, u32[]{:S(2)}, u32[]{:S(2)}) collective-permute-start(bf16[8,128,768]{2,1,0:T(8,128)(2,1)} %all-to-all-done), channel_id=1, source_target_pairs={{0,0},{1,2},{2,1},{3,3},{4,4},{5,6},{6,5},{7,7},{8,8},{9,10},{10,9... | collective-permute-start | bytes 4718600 | tf_op jit(solution)/shard_map/ppermute | solution.py:741
  134.1 31.0 %collective-permute-start.10 = (bf16[8,128,768]{2,1,0:T(8,128)(2,1)}, bf16[8,128,768]{2,1,0:T(8,128)(2,1)}, u32[]{:S(2)}, u32[]{:S(2)}) collective-permute-start(bf16[8,128,768]{2,1,0:T(8,128)(2,1)} %all-to-all-done), channel_id=1, source_target_pairs={{0,2},{1,0},{2,3},{3,1},{4,6},{5,4},{6,7},{7,5},{8,10},{9,8},{10,1... | collective-permute-start | bytes 4718600 | tf_op jit(solution)/shard_map/ppermute | solution.py:742
  156.3 70.5 %all-to-all-start.2 = ((bf16[8,704,256]{2,1,0:T(8,128)(2,1)}), bf16[8,704,256]{2,1,0:T(8,128)(2,1)}, u32[]{:S(2)}, u32[]{:S(2)}) async-start(bf16[8,704,256]{2,1,0:T(8,128)(2,1)} %bitcast.283), calls=%async_computation.2 | async-start | bytes 5767168 | tf_op jit(solution)/shard_map/all_to_all | solution.py:748
  160.8 219.1 %reduce-scatter.5.cloned.1.call-start = ((), (), s32[]{:S(2)}) async-start(), calls=%async_computation.13 | async-start | bytes 8912896 | tf_op jit(solution)/shard_map/reduce_scatter | solution.py:690
  179.4 44.0 %collective-permute-start.11 = (bf16[8,128,512]{2,1,0:T(8,128)(2,1)}, bf16[8,128,512]{2,1,0:T(8,128)(2,1)}, u32[]{:S(2)}, u32[]{:S(2)}) collective-permute-start(bf16[8,128,512]{2,1,0:T(8,128)(2,1)} %all-to-all-done.1), channel_id=1, source_target_pairs={{0,0},{1,2},{2,1},{3,3},{4,4},{5,6},{6,5},{7,7},{8,8},{9,10},{10,9... | collective-permute-start | bytes 3145736 | tf_op jit(solution)/shard_map/ppermute | solution.py:741
  189.0 34.4 %collective-permute-start.12 = (bf16[8,128,512]{2,1,0:T(8,128)(2,1)}, bf16[8,128,512]{2,1,0:T(8,128)(2,1)}, u32[]{:S(2)}, u32[]{:S(2)}) collective-permute-start(bf16[8,128,512]{2,1,0:T(8,128)(2,1)} %all-to-all-done.1), channel_id=1, source_target_pairs={{0,2},{1,0},{2,3},{3,1},{4,6},{5,4},{6,7},{7,5},{8,10},{9,8},{10,1... | collective-permute-start | bytes 3145736 | tf_op jit(solution)/shard_map/ppermute | solution.py:742
  238.8 103.8 %all-to-all-start.3 = ((bf16[8,704,256]{2,1,0:T(8,128)(2,1)}), bf16[8,704,256]{2,1,0:T(8,128)(2,1)}, u32[]{:S(2)}, u32[]{:S(2)}) async-start(bf16[8,704,256]{2,1,0:T(8,128)(2,1)} %bitcast.286), calls=%async_computation.4 | async-start | bytes 5767168 | tf_op jit(solution)/shard_map/all_to_all | solution.py:803
  244.8 212.8 %all-gather.7.cloned.1.call-start = ((), (), s32[]{:S(2)}) async-start(), calls=%async_computation.14 | async-start | bytes 8912896 | tf_op jit(solution)/shard_map/all_gather | solution.py:687
  244.9 136.1 %collective-permute-start.13 = (bf16[704,2048]{1,0:T(8,128)(2,1)S(1)}, bf16[704,2048]{1,0:T(8,128)(2,1)}, u32[]{:S(2)}, u32[]{:S(2)}) collective-permute-start(bf16[704,2048]{1,0:T(8,128)(2,1)S(1)} %bitcast.284), channel_id=1, source_target_pairs={{0,2},{2,0},{1,3},{3,1},{4,6},{6,4},{5,7},{7,5},{8,10},{10,8},{9,1... | collective-permute-start | bytes 8650760 | tf_op jit(solution)/shard_map/ppermute | solution.py:724
  382.8 239.3 %reduce-scatter.7.cloned.1.call-start = ((), (), s32[]{:S(2)}) async-start(), calls=%async_computation.15 | async-start | bytes 8912896 | tf_op jit(solution)/shard_map/reduce_scatter | solution.py:690
  383.1 64.5 %collective-permute-start.14 = (bf16[704,2048]{1,0:T(8,128)(2,1)}, bf16[704,2048]{1,0:T(8,128)(2,1)S(1)}, u32[]{:S(2)}, u32[]{:S(2)}) collective-permute-start(bf16[704,2048]{1,0:T(8,128)(2,1)} %bitcast.287), channel_id=1, source_target_pairs={{0,2},{2,0},{1,3},{3,1},{4,6},{6,4},{5,7},{7,5},{8,10},{10,8},{9,1... | collective-permute-start | bytes 8650760 | tf_op jit(solution)/shard_map/ppermute | solution.py:724
  519.0 180.4 %all-gather.9.cloned.1.call-start = ((), (), s32[]{:S(2)}) async-start(), calls=%async_computation.16 | async-start | bytes 8912896 | tf_op jit(solution)/shard_map/all_gather | solution.py:687
  520.0 6.4 collective-permute-start.19
  521.6 6.3 collective-permute-start.20
  521.7 6.2 collective-permute-start.18
  624.1 242.5 %reduce-scatter.9.cloned.1.call-start = ((), (), s32[]{:S(2)}) async-start(), calls=%async_computation.17 | async-start | bytes 8912896 | tf_op jit(solution)/shard_map/reduce_scatter | solution.py:690
  763.6 234.4 %all-gather.11.cloned.1.call-start = ((), (), s32[]{:S(2)}) async-start(), calls=%async_computation.18 | async-start | bytes 8912896 | tf_op jit(solution)/shard_map/all_gather | solution.py:687
  782.8 85.0 %collective-permute-start.21 = (bf16[704,2048]{1,0:T(8,128)(2,1)}, bf16[704,2048]{1,0:T(8,128)(2,1)}, u32[]{:S(2)}, u32[]{:S(2)}) collective-permute-start(bf16[704,2048]{1,0:T(8,128)(2,1)} %slice.90), channel_id=1, source_target_pairs={{0,2},{2,0},{1,3},{3,1},{4,6},{6,4},{5,7},{7,5},{8,10},{10,8},{9,1... | collective-permute-start | bytes 8650760 | tf_op jit(solution)/shard_map/ppermute | solution.py:724
  877.2 116.1 %all-to-all-start.4 = ((bf16[8,704,256]{2,1,0:T(8,128)(2,1)}), bf16[8,704,256]{2,1,0:T(8,128)(2,1)S(1)}, u32[]{:S(2)}, u32[]{:S(2)}) async-start(bf16[8,704,256]{2,1,0:T(8,128)(2,1)} %bitcast.290), calls=%async_computation.7 | async-start | bytes 5767168 | tf_op jit(solution)/shard_map/all_to_all | solution.py:858
  881.5 64.4 %collective-permute-start.22 = (bf16[704,2048]{1,0:T(8,128)(2,1)}, bf16[704,2048]{1,0:T(8,128)(2,1)}, u32[]{:S(2)}, u32[]{:S(2)}) collective-permute-start(bf16[704,2048]{1,0:T(8,128)(2,1)} %slice.89), channel_id=1, source_target_pairs={{0,2},{2,0},{1,3},{3,1},{4,6},{6,4},{5,7},{7,5},{8,10},{10,8},{9,1... | collective-permute-start | bytes 8650760 | tf_op jit(solution)/shard_map/ppermute | solution.py:724
  1004.4 70.2 %all-to-all-start.5 = ((bf16[8,704,256]{2,1,0:T(8,128)(2,1)}), bf16[8,704,256]{2,1,0:T(8,128)(2,1)}, u32[]{:S(2)}, u32[]{:S(2)}) async-start(bf16[8,704,256]{2,1,0:T(8,128)(2,1)} %bitcast.289), calls=%async_computation.8 | async-start | bytes 5767168 | tf_op jit(solution)/shard_map/all_to_all | solution.py:863
  1008.8 226.2 %reduce-scatter.11.cloned.1.call-start = ((), (), s32[]{:S(2)}) async-start(), calls=%async_computation.19 | async-start | bytes 8912896 | tf_op jit(solution)/shard_map/reduce_scatter | solution.py:690
  1008.9 65.0 %collective-permute-start.23 = (bf16[704,2048]{1,0:T(8,128)(2,1)}, bf16[704,2048]{1,0:T(8,128)(2,1)}, u32[]{:S(2)}, u32[]{:S(2)}) collective-permute-start(bf16[704,2048]{1,0:T(8,128)(2,1)} %slice.88), channel_id=1, source_target_pairs={{0,2},{2,0},{1,3},{3,1},{4,6},{6,4},{5,7},{7,5},{8,10},{10,8},{9,1... | collective-permute-start | bytes 8650760 | tf_op jit(solution)/shard_map/ppermute | solution.py:724
  1098.3 42.7 %collective-permute-start.33 = (bf16[8,128,768]{2,1,0:T(8,128)(2,1)}, bf16[8,128,768]{2,1,0:T(8,128)(2,1)}, u32[]{:S(2)}, u32[]{:S(2)}) collective-permute-start(bf16[8,128,768]{2,1,0:T(8,128)(2,1)} %get-tuple-element.144), channel_id=1, source_target_pairs={{2,0},{0,1},{3,2},{1,3},{6,4},{4,5},{7,6},{5,7},{10,8},{8,9},{11,1... | collective-permute-start | bytes 4718600 | tf_op jit(solution)/shard_map/ppermute | solution.py:890
  1098.3 42.7 %collective-permute-start.32 = (bf16[8,128,768]{2,1,0:T(8,128)(2,1)}, bf16[8,128,768]{2,1,0:T(8,128)(2,1)}, u32[]{:S(2)}, u32[]{:S(2)}) collective-permute-start(bf16[8,128,768]{2,1,0:T(8,128)(2,1)} %get-tuple-element.143), channel_id=1, source_target_pairs={{0,0},{2,1},{1,2},{3,3},{4,4},{6,5},{5,6},{7,7},{8,8},{10,9},{9,10... | collective-permute-start | bytes 4718600 | tf_op jit(solution)/shard_map/ppermute | solution.py:890
  1114.2 25.8 %collective-permute-start.16 = (bf16[128,512]{1,0:T(8,128)(2,1)S(1)}, bf16[128,512]{1,0:T(8,128)(2,1)S(1)}, u32[]{:S(2)}, u32[]{:S(2)}) collective-permute-start(bf16[128,512]{1,0:T(8,128)(2,1)S(1)} %bitcast.331), channel_id=1, source_target_pairs={{0,2},{1,3},{2,0},{3,1},{4,6},{5,7},{6,4},{7,5},{8,10},{9,11},{10,... | collective-permute-start | bytes 393224 | tf_op jit(solution)/shard_map/ppermute | solution.py:674
  1114.4 25.7 %collective-permute-start.17 = (bf16[128,512]{1,0:T(8,128)(2,1)S(1)}, bf16[128,512]{1,0:T(8,128)(2,1)S(1)}, u32[]{:S(2)}, u32[]{:S(2)}) collective-permute-start(bf16[128,512]{1,0:T(8,128)(2,1)S(1)} %bitcast.332), channel_id=1, source_target_pairs={{0,3},{1,2},{2,1},{3,0},{4,7},{5,6},{6,5},{7,4},{8,11},{9,10},{10,... | collective-permute-start | bytes 393224 | tf_op jit(solution)/shard_map/ppermute | solution.py:674
  1115.9 24.2 %collective-permute-start.15 = (bf16[128,512]{1,0:T(8,128)(2,1)S(1)}, bf16[128,512]{1,0:T(8,128)(2,1)S(1)}, u32[]{:S(2)}, u32[]{:S(2)}) collective-permute-start(bf16[128,512]{1,0:T(8,128)(2,1)S(1)} %bitcast.333), channel_id=1, source_target_pairs={{0,1},{1,0},{2,3},{3,2},{4,5},{5,4},{6,7},{7,6},{8,9},{9,8},{10,11... | collective-permute-start | bytes 393224 | tf_op jit(solution)/shard_map/ppermute | solution.py:674
  1144.4 45.8 %all-to-all-start.6 = ((bf16[8,128,768]{2,1,0:T(8,128)(2,1)}), bf16[8,128,768]{2,1,0:T(8,128)(2,1)}, u32[]{:S(2)}, u32[]{:S(2)}) async-start(bf16[8,128,768]{2,1,0:T(8,128)(2,1)} %add_convert_fusion.3), calls=%async_computation.10 | async-start | bytes 3145728 | tf_op jit(solution)/shard_map/all_to_all | solution.py:748
  1159.4 20.4 %collective-permute-start.35 = (bf16[8,128,512]{2,1,0:T(8,128)(2,1)}, bf16[8,128,512]{2,1,0:T(8,128)(2,1)}, u32[]{:S(2)}, u32[]{:S(2)}) collective-permute-start(bf16[8,128,512]{2,1,0:T(8,128)(2,1)} %get-tuple-element.152), channel_id=1, source_target_pairs={{2,0},{0,1},{3,2},{1,3},{6,4},{4,5},{7,6},{5,7},{10,8},{8,9},{11,1... | collective-permute-start | bytes 3145736 | tf_op jit(solution)/shard_map/ppermute | solution.py:890
  1160.8 19.1 %collective-permute-start.34 = (bf16[8,128,512]{2,1,0:T(8,128)(2,1)}, bf16[8,128,512]{2,1,0:T(8,128)(2,1)}, u32[]{:S(2)}, u32[]{:S(2)}) collective-permute-start(bf16[8,128,512]{2,1,0:T(8,128)(2,1)} %get-tuple-element.151), channel_id=1, source_target_pairs={{0,0},{2,1},{1,2},{3,3},{4,4},{6,5},{5,6},{7,7},{8,8},{10,9},{9,10... | collective-permute-start | bytes 3145736 | tf_op jit(solution)/shard_map/ppermute | solution.py:890
  1190.3 43.6 %all-to-all-start.7 = ((bf16[8,128,512]{2,1,0:T(8,128)(2,1)}), bf16[8,128,512]{2,1,0:T(8,128)(2,1)}, u32[]{:S(2)}, u32[]{:S(2)}) async-start(bf16[8,128,512]{2,1,0:T(8,128)(2,1)} %add_convert_fusion.4), calls=%async_computation.11 | async-start | bytes 2097152 | tf_op jit(solution)/shard_map/all_to_all | solution.py:908
  1206.7 7.6 collective-permute-start.36
  1234.9 12.0 collective-permute-start.37
  1244.4 13.1 %collective-permute-start.30 = (f32[128,512]{1,0:T(8,128)S(1)}, f32[128,512]{1,0:T(8,128)S(1)}, u32[]{:S(2)}, u32[]{:S(2)}) collective-permute-start(f32[128,512]{1,0:T(8,128)S(1)} %bitcast.316), channel_id=1, source_target_pairs={{0,2},{1,3},{2,0},{3,1},{4,6},{5,7},{6,4},{7,5},{8,10},{9,11},{10,... | collective-permute-start | bytes 786440 | tf_op jit(solution)/shard_map/ppermute | solution.py:674
  1246.0 11.5 collective-permute-start.31
  1246.1 11.4 collective-permute-start.29
  1250.8 4.9 collective-permute-start.28
  (45 other events, 2263.7 us)
Sparse Core Ops, SparseCore 0:
  36.1 117.2 all-gather.4
  238.9 140.9 reduce-scatter.4
  382.9 74.6 all-gather.6
  519.1 102.8 reduce-scatter.6
  624.7 74.6 all-gather.8
  763.7 102.8 reduce-scatter.8
  870.9 127.0 all-gather.10
  1086.1 139.9 reduce-scatter.10

commit v3 on v2

--- a/solution.py
+++ b/solution.py
@@ -634,6 +634,171 @@
     )(pull, gate, query, pair, pair_up, log_total, cosine, sine)
 
 
+LINE = 4
+SIDES = [(i, i ^ 1) for i in range(2 * LINE)]
+
+
+def hops(moves):
+    return [(2 * a + x, 2 * b + x) for a, b in moves for x in (0, 1)]
+
+
+def hold(*values):
+    return lax.optimization_barrier(values)
+
+
+def to_side(value):
+    return lax.ppermute(value, "dp", SIDES)
+
+
+def to_core(value):
+    return lax.ppermute(value, "c", swap_pairs(2))
+
+
+def scatter_run(make, given, fill=None):
+    spot = lax.axis_index("dp") // 2
+    low = jnp.bfloat16
+    wide = lambda value: value.astype(jnp.float32)
+
+    def rise(value, last):
+        return lax.ppermute(value, "dp", hops([(a, a + 1) for a in range(last)]))
+
+    def fall(value, last):
+        return lax.ppermute(value, "dp", hops([(LINE - 1 - a, LINE - 2 - a) for a in range(last)]))
+
+    def cut(value):
+        middle = value.shape[0] // 2
+        return value[:middle], value[middle:]
+
+    here3, there3 = cut(make(3, *given))
+    there3, *given = hold(there3, *given)
+    got3, part2 = hold(to_core(there3), make(2, *given))
+    here2, there2 = cut(part2)
+    mine3, other3 = cut(here3 + got3)
+    other3, there2, *given = hold(other3, there2, *given)
+    side3, both2, part1 = hold(to_side(other3), here2 + to_core(there2), make(1, *given))
+    here1, there1 = cut(part1)
+    mine2, other2 = cut(both2)
+    row3 = wide(mine3) + wide(side3)
+    send3, other2, there1, *given = hold(row3.astype(low), other2, there1, *given)
+    side2, up, down, both1, part0 = hold(
+        to_side(other2), rise(send3, 1), fall(send3, 1), here1 + to_core(there1), make(0, *given)
+    )
+    here0, there0 = cut(part0)
+    mine1, other1 = cut(both1)
+    row2 = wide(mine2) + wide(side2)
+    send_up = (jnp.where(spot == 0, row2, row3) + wide(up)).astype(low)
+    send_down = (jnp.where(spot == LINE - 1, row2, row3) + wide(down)).astype(low)
+    send_up, send_down, other1, there0, *given = hold(send_up, send_down, other1, there0, *given)
+    side1, up, down, both0 = hold(
+        to_side(other1), rise(send_up, 2), fall(send_down, 2), here0 + to_core(there0)
+    )
+    mine0, other0 = cut(both0)
+    row1 = wide(mine1) + wide(side1)
+    send_up = (jnp.where(spot == 1, row2, row1) + wide(up)).astype(low)
+    send_down = (jnp.where(spot == LINE - 2, row2, row1) + wide(down)).astype(low)
+    send_up, send_down, other0, *given = hold(send_up, send_down, other0, *given)
+    filled = fill(*given) if fill else ()
+    side0, up, down, filled = hold(to_side(other0), rise(send_up, 3), fall(send_down, 3), filled)
+    total = wide(mine0) + wide(side0) + wide(up) + wide(down)
+    return (total, filled) if fill else total
+
+
+LANE_STEP = 512
+
+
+def product_kernel(terms, places, *refs):
+    lefts, rights, out = refs[: 4 * terms], refs[4 * terms : 5 * terms], refs[-1]
+    total = None
+    for term in range(terms):
+        rows = jnp.concatenate([lefts[4 * term + j][...] for j in range(4)], axis=0)
+        part = jnp.dot(rows, rights[term][...], preferred_element_type=jnp.float32)
+        total = part if total is None else total + part
+    out[...] = total.astype(out.dtype)
+
+
+def slot_product(places, lefts, rights):
+    width = rights[0].shape[1]
+    block = lambda j: (lambda i, places: (places[j], 0))
+    return pl.pallas_call(
+        functools.partial(product_kernel, len(lefts)),
+        grid_spec=pltpu.PrefetchScalarGridSpec(
+            num_scalar_prefetch=1,
+            grid=(width // LANE_STEP,),
+            in_specs=[
+                pl.BlockSpec((BLOCK, left.shape[1]), block(j)) for left in lefts for j in range(4)
+            ]
+            + [
+                pl.BlockSpec((right.shape[0], LANE_STEP), lambda i, places: (0, i))
+                for right in rights
+            ],
+            out_specs=pl.BlockSpec((4 * BLOCK, LANE_STEP), lambda i, places: (0, i)),
+        ),
+        out_shape=jax.ShapeDtypeStruct((4 * BLOCK, width), jnp.bfloat16),
+        compiler_params=pltpu.CompilerParams(
+            dimension_semantics=("arbitrary",), vmem_limit_bytes=ROOM
+        ),
+        cost_estimate=pl.CostEstimate(
+            flops=sum(8 * BLOCK * right.shape[0] * width for right in rights),
+            transcendentals=0,
+            bytes_accessed=sum(2 * right.size + 8 * BLOCK * right.shape[0] for right in rights),
+        ),
+        name="slot_product",
+    )(places, *[left for left in lefts for _ in range(4)], *rights)
+
+
+ROW_STEP = 256
+
+
+def share_lanes(share, columns):
+    lane = lax.broadcasted_iota(jnp.int32, (share.shape[0], columns), 1)
+    return jnp.where(lane < columns // 2, share[:, 0:1], share[:, 1:2])
+
+
+def open_kernel(rows, gate_w, up_w, share, gate_out, up_out, inner_out):
+    gate = nt(rows[...], gate_w[...])
+    up = nt(rows[...], up_w[...])
+    gate_out[...] = gate
+    up_out[...] = up
+    inner_out[...] = (
+        gate / (1.0 + jnp.exp(-gate)) * up * share_lanes(share[...], gate.shape[1])
+    ).astype(jnp.bfloat16)
+
+
+def close_kernel(rows, down_w, share, gate_in, up_in, gate_out, up_out):
+    gate = gate_in[...]
+    pull = nt(rows[...], down_w[...]) * share_lanes(share[...], gate.shape[1])
+    sigma = 1.0 / (1.0 + jnp.exp(-gate))
+    gate_out[...] = (pull * up_in[...] * sigma * (1.0 + gate * (1.0 - sigma))).astype(jnp.bfloat16)
+    up_out[...] = (pull * gate * sigma).astype(jnp.bfloat16)
+
+
+def row_call(kernel, rows, weights, others, kinds, name):
+    count, width = rows.shape
+    columns = weights[0].shape[0]
+    tile = lambda lanes: pl.BlockSpec((ROW_STEP, lanes), lambda i: (i, 0))
+    return pl.pallas_call(
+        kernel,
+        grid=(count // ROW_STEP,),
+        in_specs=[tile(width)]
+        + [
+            pl.BlockSpec(weight.shape, lambda i: (0, 0), pipeline_mode=pl.Buffered(1))
+            for weight in weights
+        ]
+        + [tile(other.shape[1]) for other in others],
+        out_specs=[tile(columns) for _ in kinds],
+        out_shape=[jax.ShapeDtypeStruct((count, columns), kind) for kind in kinds],
+        compiler_params=pltpu.CompilerParams(
+            dimension_semantics=("arbitrary",), vmem_limit_bytes=ROOM
+        ),
+        cost_estimate=pl.CostEstimate(
+            flops=2 * len(weights) * count * width * columns,
+            transcendentals=count * columns,
+            bytes_accessed=2 * len(weights) * width * columns + 10 * count * columns,
+        ),
+        name=name,
+    )(rows, *weights, *others)
+
+
 def team_device(
     tokens_in,
     teacher,
@@ -705,15 +870,13 @@
     )
     tokens_here = jnp.full((1, row_count), jnp.sum(valid).astype(jnp.float32))
     gate_here = jnp.concatenate([gate_here, tokens_here], axis=0)
-    slots = jnp.arange(units, dtype=jnp.int32)[:, None, None] == lax.axis_index("dp")
-    gate_all = jnp.where(slots, gate_here[None], 0.0)
-    reach = 1
-    while reach < units:
-        gate_all = gate_all + lax.ppermute(gate_all, "dp", [(i, i ^ reach) for i in range(units)])
-        reach *= 2
+    slots = jnp.arange(units, dtype=jnp.int32)[:, None, None]
+    gate_all = jnp.where(slots == lax.axis_index("dp"), gate_here[None], 0.0)
+    for shift in range(1, units):
+        got = lax.ppermute(gate_here, "dp", [(i, (i + shift) % units) for i in range(units)])
+        gate_all = jnp.where(slots == (lax.axis_index("dp") - shift) % units, got[None], gate_all)
     count = jnp.sum(gate_all[:, -1, 0])
     normed1 = (field * root_of(field) * gains[0]).astype(low)
-    normed1, gate_all = lax.optimization_barrier((normed1, gate_all))
     normed1 = collect(normed1)
 
     query_part = w_query.reshape(expert_count, depth, local_heads, HEAD).transpose(1, 2, 0, 3)
@@ -764,6 +927,7 @@
     )
     out_heads = scatter_heads(out_part.reshape(depth, local_heads, wide))
     gate_slabs, up_slabs = slabs_of(w_gate[0]), slabs_of(w_up[0])
+    front_heads, gate_all, count = hold(front_heads, gate_all, count)
     front_heads, out_heads, down_far = swap_all(front_heads, out_heads, down_far)
     out_heads, gate_slabs = swap_all(out_heads, gate_slabs)
     front_weights = deal_heads(front_heads)
@@ -793,6 +957,15 @@
     cosine = jnp.concatenate([cosine, cosine], axis=1)
     sine = jnp.concatenate([-sine, sine], axis=1)
 
+    unit = lax.axis_index("dp")
+    order = jnp.asarray([[0, 1, 2, 3], [1, 0, 2, 3], [2, 3, 1, 0], [3, 2, 1, 0]], jnp.int32)
+    block = jnp.arange(blocks, dtype=jnp.int32)
+    owners = (
+        ((block // 2 % 2) ^ core) * units
+        + lax.dynamic_index_in_dim(order, unit // 2, 0, False)[block // 4] * 2
+        + ((block % 2) ^ (unit % 2))
+    )
+
     front = dot(normed1, front_weights)
     front, out_heads = lax.optimization_barrier((front, out_heads))
     out_weights = deal_heads(out_heads)
@@ -811,37 +984,45 @@
     gate_w = jnp.concatenate([gate_own, gate_far], axis=0)
     up_w = jnp.concatenate([up_own, up_far], axis=0)
     down_w = jnp.concatenate([down_own, down_far], axis=0)
-    lane = jnp.arange(2 * hidden, dtype=jnp.int32)[None, :]
-    share_cols = jnp.where(lane < hidden, feed_gate_own[:, None], feed_gate_far[:, None])
-    gate_pre = times_trans(normed2, gate_w)
-    up_pre = times_trans(normed2, up_w)
-    inner = (jax.nn.silu(gate_pre) * up_pre * share_cols).astype(low)
-    feed_part = dot(inner, down_w)
-    result = hidden1 + deliver(feed_part)
-    layer_out = from_rows(result.astype(low))
+    feed_share = jnp.stack([feed_gate_own, feed_gate_far], axis=1)
+    gate_pre, up_pre, inner = row_call(
+        open_kernel,
+        normed2,
+        [gate_w, up_w],
+        [feed_share],
+        [jnp.float32, jnp.float32, low],
+        "open_rows",
+    )
+    result = hidden1 + scatter_run(
+        lambda k, left: slot_product(owners[4 * k : 4 * k + 4], [left], [down_w]), (inner,)
+    )
+    layer_low = result.astype(low)
     differ = result - goal
     squared = jnp.sum(counted * differ * differ)
     grad_result = counted * differ * (2.0 * (loss_scale / (count * width)))
     grad_rows = collect(grad_result.astype(low))
-
-    grad_inner = times_trans(grad_rows, down_w) * share_cols
-    sigma = jax.nn.sigmoid(gate_pre)
-    grad_gate = (grad_inner * up_pre * sigma * (1.0 + gate_pre * (1.0 - sigma))).astype(low)
-    grad_up = (grad_inner * gate_pre * sigma).astype(low)
-    grad_norm2 = deliver(dot(grad_gate, gate_w) + dot(grad_up, up_w))
+    grad_rows, layer_low = hold(grad_rows, layer_low)
+    layer_out = from_rows(layer_low)
+
+    grad_gate, grad_up = row_call(
+        close_kernel, grad_rows, [down_w], [feed_share, gate_pre, up_pre], [low, low], "close_rows"
+    )
 
     def weight_sum(left, right):
         whole = times_rows(left, right)
         return whole[:hidden], whole[hidden:].astype(low)
 
-    gate_near, gate_sent = weight_sum(grad_gate, normed2)
+    grad_norm2, (gate_near, gate_sent) = scatter_run(
+        lambda k, one, two: slot_product(owners[4 * k : 4 * k + 4], [one, two], [gate_w, up_w]),
+        (grad_gate, grad_up),
+        lambda one, two: weight_sum(one, normed2),
+    )
     gate_got = across(gate_sent)
+    grad_norm2, grad_up, inner = hold(grad_norm2, grad_up, inner)
     up_near, up_sent = weight_sum(grad_up, normed2)
     down_near, down_sent = weight_sum(inner, grad_rows)
-    grad_norm2, gate_near, gate_got, up_near, up_sent, down_near, down_sent = (
-        lax.optimization_barrier(
-            (grad_norm2, gate_near, gate_got, up_near, up_sent, down_near, down_sent)
-        )
+    gate_got, up_near, up_sent, down_near, down_sent = hold(
+        gate_got, up_near, up_sent, down_near, down_sent
     )
     up_got = across(up_sent)
     grad_hidden_norm, grad_gain2 = norm_back(hidden1, gains[1], grad_norm2)
@@ -856,13 +1037,6 @@
 
     gate_slabs = rows_for_owners(gate_near + gate_got.astype(jnp.float32))
     gate_slabs = lax.all_to_all(gate_slabs, "dp", 0, 0, tiled=True)
-    grad_hidden_rows, up_got, down_sent, gate_slabs = lax.optimization_barrier(
-        (grad_hidden_rows, up_got, down_sent, gate_slabs)
-    )
-    up_slabs = rows_for_owners(up_near + up_got.astype(jnp.float32))
-    up_slabs = lax.all_to_all(up_slabs, "dp", 0, 0, tiled=True)
-    down_got = across(down_sent)
-
     front_back = attend_back(
         dot(grad_hidden_rows, out_weights),
         attn_gate,
@@ -875,13 +1049,14 @@
         units,
         expert_count,
     )
-    front_back, up_slabs, down_got = lax.optimization_barrier((front_back, up_slabs, down_got))
-    down_sum = down_near + down_got.astype(jnp.float32)
+    front_back, gate_slabs, up_got = hold(front_back, gate_slabs, up_got)
+    up_slabs = rows_for_owners(up_near + up_got.astype(jnp.float32))
+    up_slabs = lax.all_to_all(up_slabs, "dp", 0, 0, tiled=True)
     out_grad = times_rows(grad_hidden_rows, mixed_low)
     grad_norm1 = deliver(times_trans(front_back, front_weights))
     front_grad = times_rows(normed1, front_back)
     grad_field_norm, grad_gain1 = norm_back(field, gains[0], grad_norm1)
-    input_grad = from_rows(grad_hidden1 + grad_field_norm)
+    grad_field = grad_hidden1 + grad_field_norm
 
     def undeal_heads(value):
         halves = value.astype(low).reshape(units, 2, depth // 2, value.shape[1])
@@ -903,8 +1078,15 @@
         )
         return rows.astype(jnp.float32)
 
-    front_heads, out_heads = undeal_heads(front_grad), undeal_heads(out_grad)
+    front_heads = undeal_heads(front_grad)
+    front_heads, out_grad = hold(front_heads, out_grad)
+    out_heads = undeal_heads(out_grad)
+    out_heads, down_sent = hold(out_heads, down_sent)
+    down_sum = down_near + across(down_sent).astype(jnp.float32)
+    front_heads, up_slabs = hold(front_heads, up_slabs)
     front_heads, out_heads = swap_all(front_heads, out_heads)
+    out_heads, grad_field, grad_gain1 = hold(out_heads, grad_field, grad_gain1)
+    input_grad = from_rows(grad_field)
     out_heads = lax.all_to_all(out_heads, "dp", 0, 0, tiled=True)
     grad_gate_out, grad_up_out = own_rows(gate_slabs), own_rows(up_slabs)
     front_out, out_back = gather_heads(front_heads), gather_heads(out_heads)
@@ -975,7 +1157,8 @@
             and w_query.shape[2] // HEAD == 2 * units
             and w_query.shape[0] == 4
             and tokens_in.shape[1] == units * 2 * PROMPT_DEV
-            and PROMPT_DEV == CLEN
+            and PROMPT_DEV == CLEN == BLOCK
+            and units == 2 * LINE
         )
         if team:
             grid = Mesh(mesh.devices.reshape(units, 2, 2), ("dp", "y", "c"))

time: 1280 us -> 1200 us (0.938)
  waiting for transfers between devices: 663 us -> 492 us
  Pallas kernels: 63.9 us -> 202 us
  matrix products: 235 us -> 99.5 us
  starting transfers between devices: 115 us -> 165 us
  local copies, waits for them, and re-layouts: 98.5 us -> 127 us
  other arithmetic: 73.3 us -> 89.6 us
    pallas_call x0 -> x10, Pallas kernels: none -> 138 us  [the longest x8 78.8 us: slot_product(): pl.pallas_call(functools.partial(product_kernel, len(lefts)), grid_spec=p...]
    reduce_scatter x4 -> x2, waiting for transfers between devices: 163 us -> 33.4 us  [deliver(): lax.psum_scatter(value.astype(low), TEAM, scatter_dimension=0, tiled=True)]
    dot_general x5 -> x2, matrix products: 88.4 us -> 18.5 us  [times_trans(): lax.dot_general(left, right, TRANS_DIMS, preferred_element_type=jnp.float32)]
    dot_general x5 -> x2, matrix products: 76.9 us -> 19 us  [dot(): return jnp.dot(left, right, preferred_element_type=jnp.float32)]
    ppermute x6, waiting for transfers between devices: 180 us -> 133 us  [across(): return lax.ppermute(value, 'y', swap_pairs(2))]
    all_to_all x1, waiting for transfers between devices: 47.3 us -> 2.8 us  [team_device(): gate_slabs = lax.all_to_all(gate_slabs, 'dp', 0, 0, tiled=True)]
    ppermute x3 -> x35, starting transfers between devices: 6.5 us -> 48.9 us  [the longest x6 22.2 us: rise(): return lax.ppermute(value, 'dp', hops([(a, a + 1) for a in range(last)]))]
    all_to_all x2, waiting for transfers between devices: 97.5 us -> 132 us  [team_device(): up_slabs = lax.all_to_all(up_slabs, 'dp', 0, 0, tiled=True)]
  transfers between devices with their start and end apart: 54 -> 84, of which waited for: 29 -> 31; matrix products, arithmetic and copies ran while one was open for 19% -> 21% of each run, Pallas kernels for 5% -> 10%
where the time goes in v3:
time: 1200 us; the launch traced here: 1190 us
  waiting for transfers between devices  492 us (41%)
  Pallas kernels  202 us (17%)
  starting transfers between devices  165 us (14%)
  local copies, waits for them, and re-layouts  127 us (11%)
  matrix products  99.5 us (8%)
  other arithmetic  89.6 us (7%)
  between operations  19.4 us (2%)
    ppermute x6, waiting for transfers between devices, across(): return lax.ppermute(value, 'y', swap_pairs(2))  133 us
    all_to_all x2, waiting for transfers between devices, team_device(): up_slabs = lax.all_to_all(up_slabs, 'dp', 0, 0, tiled=True)  132 us
    pallas_call x8, Pallas kernels, slot_product(): pl.pallas_call(functools.partial(product_kernel, len(lefts)), grid_spec=p...  78.8 us
    all_gather x4, waiting for transfers between devices, collect(): return lax.all_gather(value, TEAM, axis=0, tiled=True)  78.2 us
    dot_general x5, matrix products, times_rows(): lax.dot_general(left, right, ROWS_DIMS, preferred_element_type=jnp.float32)  61.9 us
    pallas_call x2, Pallas kernels, row_call(): pl.pallas_call(kernel, grid=(count // ROW_STEP,), in_specs=[tile(width)]...  59.1 us
    unnamed x157, local copies, waits for them, and re-layouts  47.6 us
    all_to_all x4, waiting for transfers between devices, swap_all(): got = lax.all_to_all(value, 'dp', 0, 0, tiled=True)  46.5 us
  transfers between devices with their start and end apart: 84, of which 31 were waited for; matrix products, arithmetic and copies ran while one was open for 21% of the time, Pallas kernels for 10%

profile of v3, /device:TPU:0, one launch (start us, length us, event | category | flops | bytes accessed | tf_op | source)
XLA Modules:
  0.0 1193.3 jit_solution(9146798709458393133)
XLA Ops:
  42.4 6.0 all-to-all-start
  52.7 48.4 %collective-permute-done.12 = bf16[704,2048]{1,0:T(8,128)(2,1)} collective-permute-done((bf16[704,2048]{1,0:T(8,128)(2,1)}, bf16[704,2048]{1,0:T(8,128)(2,1)}, u32[]{:S(2)}, u32[]{:S(2)}) %collective-permute-start.12) | collective-permute-done | bytes 2883616 | tf_op jit(solution)/shard_map/ppermute | solution.py:887
  101.1 10.4 all-to-all-done
  115.7 13.3 %collective-permute-start.13 = (bf16[8,128,768]{2,1,0:T(8,128)(2,1)}, bf16[8,128,768]{2,1,0:T(8,128)(2,1)}, u32[]{:S(2)}, u32[]{:S(2)}) collective-permute-start(bf16[8,128,768]{2,1,0:T(8,128)(2,1)} %all-to-all-done), channel_id=1, source_target_pairs={{0,0},{1,2},{2,1},{3,3},{4,4},{5,6},{6,5},{7,7},{8,8},{9,10},{10,9... | collective-permute-start | bytes 4718600 | tf_op jit(solution)/shard_map/ppermute | solution.py:904
  135.1 7.5 all-to-all-done.1
  159.0 8.5 fusion.39.front
  167.5 9.7 collective-permute-start.15
  185.7 25.8 %attend.1 = (bf16[2048,512]{1,0:T(8,128)(2,1)}, bf16[2048,512]{1,0:T(8,128)(2,1)}, bf16[2048,256]{1,0:T(8,128)(2,1)}, f32[16,1,512]{2,1,0:T(1,128)}) custom-call(f32[2048,768]{1,0:T(8,128)} %fusion.39.front, f32[2048,128]{1,0:T(8,128)} %get-tuple-element.408.cosine, f32[2048,128]{1,0:T(8,128)} %get-tuple-element.409.sine, f32[16,1,512]{2,1,0:T(1,128)} %bitcast.334), custom_call_target="tpu_custom_call" | custom-call | flops 4294967296 | bytes 12582912 | tf_op jit(solution)/shard_map/attend/pallas_call | solution.py:488
  218.1 6.9 convolution_convert_fusion.1
  225.0 6.0 all-to-all-start.3
  231.8 97.0 %all-to-all-done.3 = bf16[8,704,256]{2,1,0:T(8,128)(2,1)} async-done(((bf16[8,704,256]{2,1,0:T(8,128)(2,1)}), bf16[8,704,256]{2,1,0:T(8,128)(2,1)}, u32[]{:S(2)}, u32[]{:S(2)}) %all-to-all-start.3) | async-done | bytes 2883616 | tf_op jit(solution)/shard_map/all_to_all | solution.py:976
  332.7 33.4 %reduce-scatter.3.cloned.1.call-done = bf16[128,2048]{1,0:T(8,128)(2,1)} async-done(((bf16[2048,2048]{1,0:T(8,128)(2,1)}), bf16[128,2048]{1,0:T(8,128)(2,1)}) %reduce-scatter.3.cloned.1.call-update) | async-done | bytes 524304 | tf_op jit(solution)/shard_map/reduce_scatter | solution.py:855
  373.2 6.1 pad_maximum_fusion.refs_4_.down_w
  390.2 44.0 %collective-permute-done.18 = bf16[704,2048]{1,0:T(8,128)(2,1)} collective-permute-done((bf16[704,2048]{1,0:T(8,128)(2,1)}, bf16[704,2048]{1,0:T(8,128)(2,1)}, u32[]{:S(2)}, u32[]{:S(2)}) %collective-permute-start.18) | collective-permute-done | bytes 2883616 | tf_op jit(solution)/shard_map/ppermute | solution.py:887
  438.1 5.8 all-gather.7.cloned.1.call-done.rows
  443.9 34.3 %open_rows.1 = (f32[2048,1408]{1,0:T(8,128)}, f32[2048,1408]{1,0:T(8,128)}, bf16[2048,1408]{1,0:T(8,128)(2,1)}) custom-call(bf16[2048,2048]{1,0:T(8,128)(2,1)} %all-gather.7.cloned.1.call-done.rows, bf16[1408,2048]{1,0:T(8,128)(2,1)} %constant_dynamic-update-slice_fusion.2.gate_w.refs_8_, ...), custom_call_target="tpu_custom_call" | custom-call | flops 23622320128 | bytes 40370176 | tf_op jit(solution)/shard_map/open_rows/pallas_call | solution.py:779
  478.2 7.9 slot_product.8
  488.7 8.1 slot_product.9
  499.7 7.9 slot_product.10
  520.9 8.0 slot_product.11
  543.8 9.9 collective-permute-done.26
  556.7 7.1 collective-permute-start.31
  583.4 72.3 %all-gather.9.cloned.1.call-done.rows = bf16[2048,2048]{1,0:T(8,128)(2,1)} async-done(((bf16[128,2048]{1,0:T(8,128)(2,1)}), bf16[2048,2048]{1,0:T(8,128)(2,1)}) %all-gather.9.cloned.1.call-update) | async-done | bytes 8388624 | tf_op jit(solution)/shard_map/all_gather | solution.py:852
  655.8 24.8 %close_rows.1 = (bf16[2048,1408]{1,0:T(8,128)(2,1)}, bf16[2048,1408]{1,0:T(8,128)(2,1)}) custom-call(bf16[2048,2048]{1,0:T(8,128)(2,1)} %all-gather.9.cloned.1.call-done.rows, bf16[1408,2048]{1,0:T(8,128)(2,1)} %pad_maximum_fusion.refs_4_.down_w, f32[2048,2]{1,0:T(8,128)} %copy.152.share, f32[2048,1408]{1,0:T(8,128)} %get-tuple-element.201.gate_in, ...), custom_call_target="tpu_custom_call" | custom-call | flops 11811160064 | bytes 34603008 | tf_op jit(solution)/shard_map/close_rows/pallas_call | solution.py:779
  680.5 11.7 slot_product.12
  694.9 11.8 slot_product.13
  709.6 11.6 slot_product.14
  730.5 11.6 slot_product.15
  749.4 11.1 collective-permute-done.46
  762.1 6.5 collective-permute-start.51
  769.9 14.8 %fusion.40 = f32[1408,2048]{1,0:T(8,128)S(1)} fusion(bf16[2048,1408]{1,0:T(8,128)(2,1)S(1)} %bitcast.278, bf16[2048,2048]{1,0:T(8,128)(2,1)} %all-gather.7.cloned.1.call-done.rows), kind=kOutput, calls=%fused_computation.245 | convolution fusion | flops 11811160064 | bytes 25690112 | tf_op jit(solution)/shard_map/dot_general | solution.py:47
  795.5 17.1 %fusion.42 = f32[1408,2048]{1,0:T(8,128)S(1)} fusion(bf16[2048,1408]{1,0:T(8,128)(2,1)} %get-tuple-element.249.refs_4_.refs_5_.refs_6_.refs_7_, bf16[2048,2048]{1,0:T(8,128)(2,1)} %all-gather.7.cloned.1.call-done.rows), kind=kOutput, calls=%fused_computation.247 | convolution fusion | flops 11811160064 | bytes 25690112 | tf_op jit(solution)/shard_map/dot_general | solution.py:47
  817.5 14.8 %fusion.43 = f32[1408,2048]{1,0:T(8,128)S(1)} fusion(bf16[2048,1408]{1,0:T(8,128)(2,1)S(1)} %bitcast.280, bf16[2048,2048]{1,0:T(8,128)(2,1)} %all-gather.9.cloned.1.call-done.rows), kind=kOutput, calls=%fused_computation.248 | convolution fusion | flops 11811160064 | bytes 25690112 | tf_op jit(solution)/shard_map/dot_general | solution.py:47
  837.5 19.5 %collective-permute-done.53 = bf16[704,2048]{1,0:T(8,128)(2,1)S(1)} collective-permute-done((bf16[704,2048]{1,0:T(8,128)(2,1)}, bf16[704,2048]{1,0:T(8,128)(2,1)S(1)}, u32[]{:S(2)}, u32[]{:S(2)}) %collective-permute-start.53) | collective-permute-done | bytes 2883616 | tf_op jit(solution)/shard_map/ppermute | solution.py:887
  870.1 10.5 fusion.41.pull
  880.6 38.1 %attend_back.1 = bf16[2048,768]{1,0:T(8,128)(2,1)} custom-call(f32[2048,512]{1,0:T(8,128)} %fusion.41.pull, f32[2048,4]{1,0:T(8,128)} %get-tuple-element.359.gate, bf16[2048,512]{1,0:T(8,128)(2,1)} %get-tuple-element.244.query_in, bf16[2048,256]{1,0:T(8,128)(2,1)} %get-tuple-element.245.pair, bf16[128,2048]{1,0:T(8,128)(2,1)} %slice_bitcast_fusion.pair_up, ...), custom_call_target="tpu_custom_call" | custom-call | flops 10737418240 | bytes 12582912 | tf_op jit(solution)/shard_map/attend_back/pallas_call | solution.py:606
  918.7 7.4 collective-permute-done.54
  928.9 11.6 convolution_convert_fusion
  963.1 10.5 convolution_convert_fusion.2
  979.9 14.4 %collective-permute-done.56 = bf16[8,128,768]{2,1,0:T(8,128)(2,1)S(1)} collective-permute-done((bf16[8,128,768]{2,1,0:T(8,128)(2,1)S(1)}, bf16[8,128,768]{2,1,0:T(8,128)(2,1)S(1)}, u32[]{:S(2)}, u32[]{:S(2)}) %collective-permute-start.56) | collective-permute-done | bytes 1572896 | tf_op jit(solution)/shard_map/ppermute | solution.py:1065
  997.3 17.1 %collective-permute-start.58 = (bf16[8,128,512]{2,1,0:T(8,128)(2,1)}, bf16[8,128,512]{2,1,0:T(8,128)(2,1)}, u32[]{:S(2)}, u32[]{:S(2)}) collective-permute-start(bf16[8,128,512]{2,1,0:T(8,128)(2,1)} %get-tuple-element.344), channel_id=1, source_target_pairs={{2,0},{0,1},{3,2},{1,3},{6,4},{4,5},{7,6},{5,7},{10,8},{8,9},{11,1... | collective-permute-start | bytes 3145736 | tf_op jit(solution)/shard_map/ppermute | solution.py:1065
  1014.4 9.4 collective-permute-start.57
  1023.8 34.9 %all-to-all-done.5 = bf16[8,704,256]{2,1,0:T(8,128)(2,1)} async-done(((bf16[8,704,256]{2,1,0:T(8,128)(2,1)}), bf16[8,704,256]{2,1,0:T(8,128)(2,1)}, u32[]{:S(2)}, u32[]{:S(2)}) %all-to-all-start.5) | async-done | bytes 2883616 | tf_op jit(solution)/shard_map/all_to_all | solution.py:1054
  1066.5 6.3 copy.170
  1082.0 6.3 copy.171
  1088.3 28.6 %all-to-all-done.6 = bf16[8,128,768]{2,1,0:T(8,128)(2,1)} async-done(((bf16[8,128,768]{2,1,0:T(8,128)(2,1)}), bf16[8,128,768]{2,1,0:T(8,128)(2,1)}, u32[]{:S(2)}, u32[]{:S(2)}) %all-to-all-start.6) | async-done | bytes 1572896 | tf_op jit(solution)/shard_map/all_to_all | solution.py:911
  1125.9 13.6 %collective-permute-done.69 = bf16[704,2048]{1,0:T(8,128)(2,1)} collective-permute-done((bf16[704,2048]{1,0:T(8,128)(2,1)}, bf16[704,2048]{1,0:T(8,128)(2,1)}, u32[]{:S(2)}, u32[]{:S(2)}) %collective-permute-start.69) | collective-permute-done | bytes 2883616 | tf_op jit(solution)/shard_map/ppermute | solution.py:887
  1139.5 7.4 add_bitcast_fusion
  (471 shorter events, 318.2 us)
Async XLA Ops:
  7.3 135.3 %all-gather.5.cloned.1.call-start = ((), (), s32[]{:S(2)}) async-start(), calls=%async_computation.10 | async-start | bytes 8912896 | tf_op jit(solution)/shard_map/all_gather | solution.py:852
  36.8 64.3 %collective-permute-start.12 = (bf16[704,2048]{1,0:T(8,128)(2,1)}, bf16[704,2048]{1,0:T(8,128)(2,1)}, u32[]{:S(2)}, u32[]{:S(2)}) collective-permute-start(bf16[704,2048]{1,0:T(8,128)(2,1)} %bitcast.303), channel_id=1, source_target_pairs={{0,2},{2,0},{1,3},{3,1},{4,6},{6,4},{5,7},{7,5},{8,10},{10,8},{9,1... | collective-permute-start | bytes 8650760 | tf_op jit(solution)/shard_map/ppermute | solution.py:887
  42.4 69.0 %all-to-all-start = ((bf16[8,128,768]{2,1,0:T(8,128)(2,1)}), bf16[8,128,768]{2,1,0:T(8,128)(2,1)}, u32[]{:S(2)}, u32[]{:S(2)}) async-start(bf16[8,128,768]{2,1,0:T(8,128)(2,1)} %pad_maximum_fusion.3), calls=%async_computation | async-start | bytes 3145728 | tf_op jit(solution)/shard_map/all_to_all | solution.py:911
  111.4 31.2 %all-to-all-start.1 = ((bf16[8,128,512]{2,1,0:T(8,128)(2,1)}), bf16[8,128,512]{2,1,0:T(8,128)(2,1)}, u32[]{:S(2)}, u32[]{:S(2)}) async-start(bf16[8,128,512]{2,1,0:T(8,128)(2,1)} %pad_maximum_fusion.4), calls=%async_computation.1 | async-start | bytes 2097152 | tf_op jit(solution)/shard_map/all_to_all | solution.py:911
  115.7 35.4 %collective-permute-start.13 = (bf16[8,128,768]{2,1,0:T(8,128)(2,1)}, bf16[8,128,768]{2,1,0:T(8,128)(2,1)}, u32[]{:S(2)}, u32[]{:S(2)}) collective-permute-start(bf16[8,128,768]{2,1,0:T(8,128)(2,1)} %all-to-all-done), channel_id=1, source_target_pairs={{0,0},{1,2},{2,1},{3,3},{4,4},{5,6},{6,5},{7,7},{8,8},{9,10},{10,9... | collective-permute-start | bytes 4718600 | tf_op jit(solution)/shard_map/ppermute | solution.py:904
  129.0 24.2 %collective-permute-start.14 = (bf16[8,128,768]{2,1,0:T(8,128)(2,1)}, bf16[8,128,768]{2,1,0:T(8,128)(2,1)}, u32[]{:S(2)}, u32[]{:S(2)}) collective-permute-start(bf16[8,128,768]{2,1,0:T(8,128)(2,1)} %all-to-all-done), channel_id=1, source_target_pairs={{0,2},{1,0},{2,3},{3,1},{4,6},{5,4},{6,7},{7,5},{8,10},{9,8},{10,1... | collective-permute-start | bytes 4718600 | tf_op jit(solution)/shard_map/ppermute | solution.py:905
  142.6 72.4 %all-to-all-start.2 = ((bf16[8,704,256]{2,1,0:T(8,128)(2,1)}), bf16[8,704,256]{2,1,0:T(8,128)(2,1)}, u32[]{:S(2)}, u32[]{:S(2)}) async-start(bf16[8,704,256]{2,1,0:T(8,128)(2,1)} %bitcast.287), calls=%async_computation.2 | async-start | bytes 5767168 | tf_op jit(solution)/shard_map/all_to_all | solution.py:911
  147.0 219.1 %reduce-scatter.3.cloned.1.call-start = ((), (), s32[]{:S(2)}) async-start(), calls=%async_computation.11 | async-start | bytes 8912896 | tf_op jit(solution)/shard_map/reduce_scatter | solution.py:855
  167.5 44.0 %collective-permute-start.15 = (bf16[8,128,512]{2,1,0:T(8,128)(2,1)}, bf16[8,128,512]{2,1,0:T(8,128)(2,1)}, u32[]{:S(2)}, u32[]{:S(2)}) collective-permute-start(bf16[8,128,512]{2,1,0:T(8,128)(2,1)} %all-to-all-done.1), channel_id=1, source_target_pairs={{0,0},{1,2},{2,1},{3,3},{4,4},{5,6},{6,5},{7,7},{8,8},{9,10},{10,9... | collective-permute-start | bytes 3145736 | tf_op jit(solution)/shard_map/ppermute | solution.py:904
  177.2 34.3 %collective-permute-start.16 = (bf16[8,128,512]{2,1,0:T(8,128)(2,1)}, bf16[8,128,512]{2,1,0:T(8,128)(2,1)}, u32[]{:S(2)}, u32[]{:S(2)}) collective-permute-start(bf16[8,128,512]{2,1,0:T(8,128)(2,1)} %all-to-all-done.1), channel_id=1, source_target_pairs={{0,2},{1,0},{2,3},{3,1},{4,6},{5,4},{6,7},{7,5},{8,10},{9,8},{10,1... | collective-permute-start | bytes 3145736 | tf_op jit(solution)/shard_map/ppermute | solution.py:905
  225.0 103.8 %all-to-all-start.3 = ((bf16[8,704,256]{2,1,0:T(8,128)(2,1)}), bf16[8,704,256]{2,1,0:T(8,128)(2,1)}, u32[]{:S(2)}, u32[]{:S(2)}) async-start(bf16[8,704,256]{2,1,0:T(8,128)(2,1)} %bitcast.289), calls=%async_computation.4 | async-start | bytes 5767168 | tf_op jit(solution)/shard_map/all_to_all | solution.py:976
  231.0 212.9 %all-gather.7.cloned.1.call-start = ((), (), s32[]{:S(2)}) async-start(), calls=%async_computation.12 | async-start | bytes 8912896 | tf_op jit(solution)/shard_map/all_gather | solution.py:852
  231.1 136.2 %collective-permute-start.17 = (bf16[704,2048]{1,0:T(8,128)(2,1)S(1)}, bf16[704,2048]{1,0:T(8,128)(2,1)}, u32[]{:S(2)}, u32[]{:S(2)}) collective-permute-start(bf16[704,2048]{1,0:T(8,128)(2,1)S(1)} %bitcast.283), channel_id=1, source_target_pairs={{0,2},{2,0},{1,3},{3,1},{4,6},{6,4},{5,7},{7,5},{8,10},{10,8},{9,1... | collective-permute-start | bytes 8650760 | tf_op jit(solution)/shard_map/ppermute | solution.py:887
  369.1 286.7 %all-gather.9.cloned.1.call-start = ((), (), s32[]{:S(2)}) async-start(), calls=%async_computation.13 | async-start | bytes 8912896 | tf_op jit(solution)/shard_map/all_gather | solution.py:852
  369.6 64.6 %collective-permute-start.18 = (bf16[704,2048]{1,0:T(8,128)(2,1)}, bf16[704,2048]{1,0:T(8,128)(2,1)}, u32[]{:S(2)}, u32[]{:S(2)}) collective-permute-start(bf16[704,2048]{1,0:T(8,128)(2,1)} %bitcast.285), channel_id=1, source_target_pairs={{0,2},{2,0},{1,3},{3,1},{4,6},{6,4},{5,7},{7,5},{8,10},{10,8},{9,1... | collective-permute-start | bytes 8650760 | tf_op jit(solution)/shard_map/ppermute | solution.py:887
  516.1 18.6 %collective-permute-start.23 = (bf16[128,2048]{1,0:T(8,128)(2,1)}, bf16[128,2048]{1,0:T(8,128)(2,1)S(1)}, u32[]{:S(2)}, u32[]{:S(2)}) collective-permute-start(bf16[128,2048]{1,0:T(8,128)(2,1)} %fusion.11), channel_id=1, source_target_pairs={{0,8},{4,12},{1,9},{5,13},{2,10},{6,14},{3,11},{7,15}} | collective-permute-start | bytes 1572872 | tf_op jit(solution)/shard_map/ppermute | solution.py:663
  518.9 15.7 %collective-permute-start.24 = (bf16[128,2048]{1,0:T(8,128)(2,1)}, bf16[128,2048]{1,0:T(8,128)(2,1)}, u32[]{:S(2)}, u32[]{:S(2)}) collective-permute-start(bf16[128,2048]{1,0:T(8,128)(2,1)} %fusion.11), channel_id=1, source_target_pairs={{24,16},{28,20},{25,17},{29,21},{26,18},{30,22},{27,19},{31,23}} | collective-permute-start | bytes 1572872 | tf_op jit(solution)/shard_map/ppermute | solution.py:666
  539.1 14.5 %collective-permute-start.26 = (bf16[128,2048]{1,0:T(8,128)(2,1)}, bf16[128,2048]{1,0:T(8,128)(2,1)S(1)}, u32[]{:S(2)}, u32[]{:S(2)}) collective-permute-start(bf16[128,2048]{1,0:T(8,128)(2,1)} %slice.185), channel_id=1, source_target_pairs={{0,4},{4,0},{8,12},{12,8},{16,20},{20,16},{24,28},{28,24},{1,5},{5... | collective-permute-start | bytes 1572872 | tf_op jit(solution)/shard_map/ppermute | solution.py:650
  555.8 18.4 %collective-permute-start.30 = (bf16[128,2048]{1,0:T(8,128)(2,1)}, bf16[128,2048]{1,0:T(8,128)(2,1)S(1)}, u32[]{:S(2)}, u32[]{:S(2)}) collective-permute-start(bf16[128,2048]{1,0:T(8,128)(2,1)} %slice.190), channel_id=1, source_target_pairs={{0,4},{4,0},{8,12},{12,8},{16,20},{20,16},{24,28},{28,24},{1,5},{5... | collective-permute-start | bytes 1572872 | tf_op jit(solution)/shard_map/ppermute | solution.py:650
  556.7 17.5 %collective-permute-start.31 = (bf16[128,2048]{1,0:T(8,128)(2,1)}, bf16[128,2048]{1,0:T(8,128)(2,1)S(1)}, u32[]{:S(2)}, u32[]{:S(2)}) collective-permute-start(bf16[128,2048]{1,0:T(8,128)(2,1)} %get-tuple-element.193), channel_id=1, source_target_pairs={{0,8},{4,12},{8,16},{12,20},{16,24},{20,28},{1,9},{5,13},{9,17},{1... | collective-permute-start | bytes 1572872 | tf_op jit(solution)/shard_map/ppermute | solution.py:663
  583.2 286.9 %all-gather.11.cloned.1.call-start = ((), (), s32[]{:S(2)}) async-start(), calls=%async_computation.14 | async-start | bytes 8912896 | tf_op jit(solution)/shard_map/all_gather | solution.py:852
  725.0 17.1 %collective-permute-start.45 = (bf16[256,2048]{1,0:T(8,128)(2,1)S(1)}, bf16[256,2048]{1,0:T(8,128)(2,1)}, u32[]{:S(2)}, u32[]{:S(2)}) collective-permute-start(bf16[256,2048]{1,0:T(8,128)(2,1)S(1)} %slice.199), channel_id=1, source_target_pairs={{0,1},{1,0},{2,3},{3,2},{4,5},{5,4},{6,7},{7,6},{8,9},{9,8},{10,11... | collective-permute-start | bytes 3145736 | tf_op jit(solution)/shard_map/ppermute | solution.py:654
  725.1 18.6 %collective-permute-start.43 = (bf16[128,2048]{1,0:T(8,128)(2,1)}, bf16[128,2048]{1,0:T(8,128)(2,1)S(1)}, u32[]{:S(2)}, u32[]{:S(2)}) collective-permute-start(bf16[128,2048]{1,0:T(8,128)(2,1)} %fusion.12), channel_id=1, source_target_pairs={{0,8},{4,12},{1,9},{5,13},{2,10},{6,14},{3,11},{7,15}} | collective-permute-start | bytes 1572872 | tf_op jit(solution)/shard_map/ppermute | solution.py:663
  727.9 15.8 %collective-permute-start.44 = (bf16[128,2048]{1,0:T(8,128)(2,1)}, bf16[128,2048]{1,0:T(8,128)(2,1)}, u32[]{:S(2)}, u32[]{:S(2)}) collective-permute-start(bf16[128,2048]{1,0:T(8,128)(2,1)} %fusion.12), channel_id=1, source_target_pairs={{24,16},{28,20},{25,17},{29,21},{26,18},{30,22},{27,19},{31,23}} | collective-permute-start | bytes 1572872 | tf_op jit(solution)/shard_map/ppermute | solution.py:666
  761.1 30.0 %collective-permute-start.50 = (bf16[128,2048]{1,0:T(8,128)(2,1)S(1)}, bf16[128,2048]{1,0:T(8,128)(2,1)S(1)}, u32[]{:S(2)}, u32[]{:S(2)}) collective-permute-start(bf16[128,2048]{1,0:T(8,128)(2,1)S(1)} %slice.206), channel_id=1, source_target_pairs={{0,4},{4,0},{8,12},{12,8},{16,20},{20,16},{24,28},{28,24},{1,5},{5... | collective-permute-start | bytes 1572872 | tf_op jit(solution)/shard_map/ppermute | solution.py:650
  762.1 29.0 %collective-permute-start.51 = (bf16[128,2048]{1,0:T(8,128)(2,1)S(1)}, bf16[128,2048]{1,0:T(8,128)(2,1)S(1)}, u32[]{:S(2)}, u32[]{:S(2)}) collective-permute-start(bf16[128,2048]{1,0:T(8,128)(2,1)S(1)} %get-tuple-element.237), channel_id=1, source_target_pairs={{0,8},{4,12},{8,16},{12,20},{16,24},{20,28},{1,9},{5,13},{9,17},{1... | collective-permute-start | bytes 1572872 | tf_op jit(solution)/shard_map/ppermute | solution.py:663
  768.6 22.5 %collective-permute-start.52 = (bf16[128,2048]{1,0:T(8,128)(2,1)S(1)}, bf16[128,2048]{1,0:T(8,128)(2,1)S(1)}, u32[]{:S(2)}, u32[]{:S(2)}) collective-permute-start(bf16[128,2048]{1,0:T(8,128)(2,1)S(1)} %get-tuple-element.238), channel_id=1, source_target_pairs={{24,16},{28,20},{16,8},{20,12},{8,0},{12,4},{25,17},{29,21},{17,9}... | collective-permute-start | bytes 1572872 | tf_op jit(solution)/shard_map/ppermute | solution.py:666
  793.9 63.1 %collective-permute-start.53 = (bf16[704,2048]{1,0:T(8,128)(2,1)}, bf16[704,2048]{1,0:T(8,128)(2,1)S(1)}, u32[]{:S(2)}, u32[]{:S(2)}) collective-permute-start(bf16[704,2048]{1,0:T(8,128)(2,1)} %slice.280), channel_id=1, source_target_pairs={{0,2},{2,0},{1,3},{3,1},{4,6},{6,4},{5,7},{7,5},{8,10},{10,8},{9,1... | collective-permute-start | bytes 8650760 | tf_op jit(solution)/shard_map/ppermute | solution.py:887
  860.0 68.9 %all-to-all-start.4 = ((bf16[8,704,256]{2,1,0:T(8,128)(2,1)}), bf16[8,704,256]{2,1,0:T(8,128)(2,1)S(1)}, u32[]{:S(2)}, u32[]{:S(2)}) async-start(bf16[8,704,256]{2,1,0:T(8,128)(2,1)} %bitcast.290), calls=%async_computation.5 | async-start | bytes 5767168 | tf_op jit(solution)/shard_map/all_to_all | solution.py:1039
  864.2 254.0 %reduce-scatter.5.cloned.1.call-start = ((), (), s32[]{:S(2)}) async-start(), calls=%async_computation.15 | async-start | bytes 8912896 | tf_op jit(solution)/shard_map/reduce_scatter | solution.py:855
  864.2 61.8 %collective-permute-start.54 = (bf16[704,2048]{1,0:T(8,128)(2,1)}, bf16[704,2048]{1,0:T(8,128)(2,1)}, u32[]{:S(2)}, u32[]{:S(2)}) collective-permute-start(bf16[704,2048]{1,0:T(8,128)(2,1)} %slice.279), channel_id=1, source_target_pairs={{0,2},{2,0},{1,3},{3,1},{4,6},{6,4},{5,7},{7,5},{8,10},{10,8},{9,1... | collective-permute-start | bytes 8650760 | tf_op jit(solution)/shard_map/ppermute | solution.py:887
  943.7 17.3 %collective-permute-start.37 = (bf16[128,512]{1,0:T(8,128)(2,1)S(1)}, bf16[128,512]{1,0:T(8,128)(2,1)S(1)}, u32[]{:S(2)}, u32[]{:S(2)}) collective-permute-start(bf16[128,512]{1,0:T(8,128)(2,1)S(1)} %bitcast.331), channel_id=1, source_target_pairs={{0,2},{1,3},{2,0},{3,1},{4,6},{5,7},{6,4},{7,5},{8,10},{9,11},{10,... | collective-permute-start | bytes 393224 | tf_op jit(solution)/shard_map/ppermute | solution.py:839
  946.0 15.1 %collective-permute-start.38 = (bf16[128,512]{1,0:T(8,128)(2,1)}, bf16[128,512]{1,0:T(8,128)(2,1)S(1)}, u32[]{:S(2)}, u32[]{:S(2)}) collective-permute-start(bf16[128,512]{1,0:T(8,128)(2,1)} %bitcast.274), channel_id=1, source_target_pairs={{0,3},{1,2},{2,1},{3,0},{4,7},{5,6},{6,5},{7,4},{8,11},{9,10},{10,... | collective-permute-start | bytes 393224 | tf_op jit(solution)/shard_map/ppermute | solution.py:839
  954.4 104.4 %all-to-all-start.5 = ((bf16[8,704,256]{2,1,0:T(8,128)(2,1)}), bf16[8,704,256]{2,1,0:T(8,128)(2,1)}, u32[]{:S(2)}, u32[]{:S(2)}) async-start(bf16[8,704,256]{2,1,0:T(8,128)(2,1)} %bitcast.288), calls=%async_computation.6 | async-start | bytes 5767168 | tf_op jit(solution)/shard_map/all_to_all | solution.py:1054
  973.9 20.4 %collective-permute-start.56 = (bf16[8,128,768]{2,1,0:T(8,128)(2,1)S(1)}, bf16[8,128,768]{2,1,0:T(8,128)(2,1)S(1)}, u32[]{:S(2)}, u32[]{:S(2)}) collective-permute-start(bf16[8,128,768]{2,1,0:T(8,128)(2,1)S(1)} %get-tuple-element.328), channel_id=1, source_target_pairs={{2,0},{0,1},{3,2},{1,3},{6,4},{4,5},{7,6},{5,7},{10,8},{8,9},{11,1... | collective-permute-start | bytes 4718600 | tf_op jit(solution)/shard_map/ppermute | solution.py:1065
  973.9 20.4 %collective-permute-start.55 = (bf16[8,128,768]{2,1,0:T(8,128)(2,1)S(1)}, bf16[8,128,768]{2,1,0:T(8,128)(2,1)S(1)}, u32[]{:S(2)}, u32[]{:S(2)}) collective-permute-start(bf16[8,128,768]{2,1,0:T(8,128)(2,1)S(1)} %get-tuple-element.327), channel_id=1, source_target_pairs={{0,0},{2,1},{1,2},{3,3},{4,4},{6,5},{5,6},{7,7},{8,8},{10,9},{9,10... | collective-permute-start | bytes 4718600 | tf_op jit(solution)/shard_map/ppermute | solution.py:1065
  997.3 75.4 %collective-permute-start.58 = (bf16[8,128,512]{2,1,0:T(8,128)(2,1)}, bf16[8,128,512]{2,1,0:T(8,128)(2,1)}, u32[]{:S(2)}, u32[]{:S(2)}) collective-permute-start(bf16[8,128,512]{2,1,0:T(8,128)(2,1)} %get-tuple-element.344), channel_id=1, source_target_pairs={{2,0},{0,1},{3,2},{1,3},{6,4},{4,5},{7,6},{5,7},{10,8},{8,9},{11,1... | collective-permute-start | bytes 3145736 | tf_op jit(solution)/shard_map/ppermute | solution.py:1065
  1014.4 58.4 %collective-permute-start.57 = (bf16[8,128,512]{2,1,0:T(8,128)(2,1)}, bf16[8,128,512]{2,1,0:T(8,128)(2,1)}, u32[]{:S(2)}, u32[]{:S(2)}) collective-permute-start(bf16[8,128,512]{2,1,0:T(8,128)(2,1)} %get-tuple-element.343), channel_id=1, source_target_pairs={{0,0},{2,1},{1,2},{3,3},{4,4},{6,5},{5,6},{7,7},{8,8},{10,9},{9,10... | collective-permute-start | bytes 3145736 | tf_op jit(solution)/shard_map/ppermute | solution.py:1065
  1058.8 58.1 %all-to-all-start.6 = ((bf16[8,128,768]{2,1,0:T(8,128)(2,1)}), bf16[8,128,768]{2,1,0:T(8,128)(2,1)}, u32[]{:S(2)}, u32[]{:S(2)}) async-start(bf16[8,128,768]{2,1,0:T(8,128)(2,1)} %add_convert_fusion.2), calls=%async_computation.7 | async-start | bytes 3145728 | tf_op jit(solution)/shard_map/all_to_all | solution.py:911
  1075.6 63.9 %collective-permute-start.69 = (bf16[704,2048]{1,0:T(8,128)(2,1)}, bf16[704,2048]{1,0:T(8,128)(2,1)}, u32[]{:S(2)}, u32[]{:S(2)}) collective-permute-start(bf16[704,2048]{1,0:T(8,128)(2,1)} %slice.278), channel_id=1, source_target_pairs={{0,2},{2,0},{1,3},{3,1},{4,6},{6,4},{5,7},{7,5},{8,10},{10,8},{9,1... | collective-permute-start | bytes 8650760 | tf_op jit(solution)/shard_map/ppermute | solution.py:887
  1118.1 30.4 %collective-permute-start.67 = (bf16[4,128,768]{2,1,0:T(8,128)(2,1)S(1)}, bf16[4,128,768]{2,1,0:T(8,128)(2,1)}, u32[]{:S(2)}, u32[]{:S(2)}) collective-permute-start(bf16[4,128,768]{2,1,0:T(8,128)(2,1)S(1)} %dynamic-slice_bitcast_fusion.4), channel_id=1, source_target_pairs={{0,1},{1,0},{2,3},{3,2},{4,5},{5,4},{6,7},{7,6},{8,9},{9,8},{10,11... | collective-permute-start | bytes 2359304 | tf_op jit(solution)/shard_map/ppermute | solution.py:1073
  1121.2 25.6 %collective-permute-start.59 = (f32[3,2048]{1,0:T(4,128)S(1)}, f32[3,2048]{1,0:T(4,128)S(1)}, u32[]{:S(2)}, u32[]{:S(2)}) collective-permute-start(f32[3,2048]{1,0:T(4,128)S(1)} %maximum_maximum_fusion), channel_id=1, source_target_pairs={{0,1},{1,0},{2,3},{3,2},{4,5},{5,4},{6,7},{7,6},{8,9},{9,8},{10,11... | collective-permute-start | bytes 73736 | tf_op jit(solution)/shard_map/ppermute | solution.py:1100
  1121.7 43.1 %all-to-all-start.7 = ((bf16[8,128,512]{2,1,0:T(8,128)(2,1)}), bf16[8,128,512]{2,1,0:T(8,128)(2,1)}, u32[]{:S(2)}, u32[]{:S(2)}) async-start(bf16[8,128,512]{2,1,0:T(8,128)(2,1)} %add_convert_fusion.3), calls=%async_computation.9 | async-start | bytes 2097152 | tf_op jit(solution)/shard_map/all_to_all | solution.py:1090
  1159.4 19.7 %collective-permute-start.65 = (f32[128,512]{1,0:T(8,128)}, f32[128,512]{1,0:T(8,128)}, u32[]{:S(2)}, u32[]{:S(2)}) collective-permute-start(f32[128,512]{1,0:T(8,128)} %bitcast.272), channel_id=1, source_target_pairs={{0,2},{1,3},{2,0},{3,1},{4,6},{5,7},{6,4},{7,5},{8,10},{9,11},{10,... | collective-permute-start | bytes 786440 | tf_op jit(solution)/shard_map/ppermute | solution.py:839
  1161.7 17.4 %collective-permute-start.66 = (f32[128,512]{1,0:T(8,128)}, f32[128,512]{1,0:T(8,128)}, u32[]{:S(2)}, u32[]{:S(2)}) collective-permute-start(f32[128,512]{1,0:T(8,128)} %bitcast.271), channel_id=1, source_target_pairs={{0,3},{1,2},{2,1},{3,0},{4,7},{5,6},{6,5},{7,4},{8,11},{9,10},{10,... | collective-permute-start | bytes 786440 | tf_op jit(solution)/shard_map/ppermute | solution.py:839
  1161.7 17.4 %collective-permute-start.64 = (f32[128,512]{1,0:T(8,128)S(1)}, f32[128,512]{1,0:T(8,128)}, u32[]{:S(2)}, u32[]{:S(2)}) collective-permute-start(f32[128,512]{1,0:T(8,128)S(1)} %bitcast.318), channel_id=1, source_target_pairs={{0,1},{1,0},{2,3},{3,2},{4,5},{5,4},{6,7},{7,6},{8,9},{9,8},{10,11... | collective-permute-start | bytes 786440 | tf_op jit(solution)/shard_map/ppermute | solution.py:839
  1162.4 14.9 %collective-permute-start.63 = (f32[3,2048]{1,0:T(4,128)S(1)}, f32[3,2048]{1,0:T(4,128)S(1)}, u32[]{:S(2)}, u32[]{:S(2)}) collective-permute-start(f32[3,2048]{1,0:T(4,128)S(1)} %add.417), channel_id=1, source_target_pairs={{0,16},{4,20},{8,24},{12,28},{16,0},{20,4},{24,8},{28,12},{1,17},{... | collective-permute-start | bytes 73736 | tf_op jit(solution)/shard_map/ppermute | solution.py:1100
  1166.7 14.7 %collective-permute-start.68 = (bf16[4,128,512]{2,1,0:T(8,128)(2,1)}, bf16[4,128,512]{2,1,0:T(8,128)(2,1)}, u32[]{:S(2)}, u32[]{:S(2)}) collective-permute-start(bf16[4,128,512]{2,1,0:T(8,128)(2,1)} %dynamic-slice_bitcast_fusion.6), channel_id=1, source_target_pairs={{0,1},{1,0},{2,3},{3,2},{4,5},{5,4},{6,7},{7,6},{8,9},{9,8},{10,11... | collective-permute-start | bytes 1572872 | tf_op jit(solution)/shard_map/ppermute | solution.py:1073
  (109 other events, 1941.0 us)
Sparse Core Ops, SparseCore 0:
  20.3 104.3 all-gather.4
  225.1 140.9 reduce-scatter.2
  369.2 74.6 all-gather.6
  583.3 72.3 all-gather.8
  794.0 75.7 all-gather.10
  940.6 173.0 reduce-scatter.4

commit v4 on v3

--- a/solution.py
+++ b/solution.py
@@ -345,9 +345,8 @@
     return [(i, i ^ 1) for i in range(size)]
 
 
-DEAL_FIRST = [(0, 0), (1, 2), (2, 1), (3, 3)]
+DEAL_FIRST = [(1, 2), (2, 1)]
 DEAL_SECOND = [(0, 2), (1, 0), (2, 3), (3, 1)]
-BACK_FIRST = [(b, a) for a, b in DEAL_FIRST]
 BACK_SECOND = [(b, a) for a, b in DEAL_SECOND]
 QUAD = ("y", "c")
 TEAM = ("c", "dp")
@@ -669,34 +668,34 @@
         middle = value.shape[0] // 2
         return value[:middle], value[middle:]
 
-    here3, there3 = cut(make(3, *given))
+    here3, there3 = make(3, *given)
     there3, *given = hold(there3, *given)
-    got3, part2 = hold(to_core(there3), make(2, *given))
-    here2, there2 = cut(part2)
+    got3, (here2, there2) = hold(to_core(there3), make(2, *given))
     mine3, other3 = cut(here3 + got3)
     other3, there2, *given = hold(other3, there2, *given)
-    side3, both2, part1 = hold(to_side(other3), here2 + to_core(there2), make(1, *given))
-    here1, there1 = cut(part1)
+    side3, both2, (here1, there1) = hold(
+        to_side(other3), here2 + to_core(there2), make(1, *given)
+    )
     mine2, other2 = cut(both2)
+    other2, there1, *given = hold(other2, there1, *given)
     row3 = wide(mine3) + wide(side3)
-    send3, other2, there1, *given = hold(row3.astype(low), other2, there1, *given)
-    side2, up, down, both1, part0 = hold(
+    send3 = row3.astype(low)
+    side2, up, down, both1, (here0, there0) = hold(
         to_side(other2), rise(send3, 1), fall(send3, 1), here1 + to_core(there1), make(0, *given)
     )
-    here0, there0 = cut(part0)
     mine1, other1 = cut(both1)
+    other1, there0, *given = hold(other1, there0, *given)
     row2 = wide(mine2) + wide(side2)
     send_up = (jnp.where(spot == 0, row2, row3) + wide(up)).astype(low)
     send_down = (jnp.where(spot == LINE - 1, row2, row3) + wide(down)).astype(low)
-    send_up, send_down, other1, there0, *given = hold(send_up, send_down, other1, there0, *given)
     side1, up, down, both0 = hold(
         to_side(other1), rise(send_up, 2), fall(send_down, 2), here0 + to_core(there0)
     )
     mine0, other0 = cut(both0)
+    other0, *given = hold(other0, *given)
     row1 = wide(mine1) + wide(side1)
     send_up = (jnp.where(spot == 1, row2, row1) + wide(up)).astype(low)
     send_down = (jnp.where(spot == LINE - 2, row2, row1) + wide(down)).astype(low)
-    send_up, send_down, other0, *given = hold(send_up, send_down, other0, *given)
     filled = fill(*given) if fill else ()
     side0, up, down, filled = hold(to_side(other0), rise(send_up, 3), fall(send_down, 3), filled)
     total = wide(mine0) + wide(side0) + wide(up) + wide(down)
@@ -707,13 +706,16 @@
 
 
 def product_kernel(terms, places, *refs):
-    lefts, rights, out = refs[: 4 * terms], refs[4 * terms : 5 * terms], refs[-1]
+    lefts, rights, out = refs[: 4 * terms], refs[4 * terms : 5 * terms], refs[-2]
+    far_out = refs[-1]
     total = None
     for term in range(terms):
         rows = jnp.concatenate([lefts[4 * term + j][...] for j in range(4)], axis=0)
         part = jnp.dot(rows, rights[term][...], preferred_element_type=jnp.float32)
         total = part if total is None else total + part
-    out[...] = total.astype(out.dtype)
+    middle = out.shape[0]
+    out[...] = total[:middle].astype(out.dtype)
+    far_out[...] = total[middle:].astype(out.dtype)
 
 
 def slot_product(places, lefts, rights):
@@ -731,9 +733,9 @@
                 pl.BlockSpec((right.shape[0], LANE_STEP), lambda i, places: (0, i))
                 for right in rights
             ],
-            out_specs=pl.BlockSpec((4 * BLOCK, LANE_STEP), lambda i, places: (0, i)),
+            out_specs=[pl.BlockSpec((2 * BLOCK, LANE_STEP), lambda i, places: (0, i))] * 2,
         ),
-        out_shape=jax.ShapeDtypeStruct((4 * BLOCK, width), jnp.bfloat16),
+        out_shape=[jax.ShapeDtypeStruct((2 * BLOCK, width), jnp.bfloat16)] * 2,
         compiler_params=pltpu.CompilerParams(
             dimension_semantics=("arbitrary",), vmem_limit_bytes=ROOM
         ),
@@ -901,7 +903,7 @@
         )
 
     def deal_heads(heads):
-        first = lax.ppermute(heads, QUAD, DEAL_FIRST)
+        first = jnp.where(plane == core, heads, lax.ppermute(heads, QUAD, DEAL_FIRST))
         second = lax.ppermute(heads, QUAD, DEAL_SECOND)
         return jnp.stack(
             [jnp.where(plane == 0, first, second), jnp.where(plane == 0, second, first)], axis=1
@@ -928,7 +930,9 @@
     out_heads = scatter_heads(out_part.reshape(depth, local_heads, wide))
     gate_slabs, up_slabs = slabs_of(w_gate[0]), slabs_of(w_up[0])
     front_heads, gate_all, count = hold(front_heads, gate_all, count)
-    front_heads, out_heads, down_far = swap_all(front_heads, out_heads, down_far)
+    front_heads, out_heads, down_far, gate_slabs, up_slabs = swap_all(
+        front_heads, out_heads, down_far, gate_slabs, up_slabs
+    )
     out_heads, gate_slabs = swap_all(out_heads, gate_slabs)
     front_weights = deal_heads(front_heads)
     gate_all = (
@@ -1062,9 +1066,10 @@
         halves = value.astype(low).reshape(units, 2, depth // 2, value.shape[1])
         first = lax.dynamic_index_in_dim(halves, plane, 1, keepdims=False)
         second = lax.dynamic_index_in_dim(halves, 1 - plane, 1, keepdims=False)
-        both = lax.ppermute(first, QUAD, BACK_FIRST).astype(jnp.float32) + lax.ppermute(
-            second, QUAD, BACK_SECOND
-        ).astype(jnp.float32)
+        first = jnp.where(plane == core, first, lax.ppermute(first, QUAD, DEAL_FIRST))
+        both = first.astype(jnp.float32) + lax.ppermute(second, QUAD, BACK_SECOND).astype(
+            jnp.float32
+        )
         return both.astype(low)
 
     def gather_heads(value):

time: 1200 us -> 1190 us (level)
  starting transfers between devices: 165 us -> 147 us
  waiting for transfers between devices: 492 us -> 505 us
    ppermute x4, starting transfers between devices: 33.3 us -> 6.22 us  [the longest x2 3.69 us: deal_heads(): lax.ppermute(heads, QUAD, DEAL_FIRST)]
    all_to_all x4, waiting for transfers between devices: 46.5 us -> 69.3 us  [swap_all(): got = lax.all_to_all(value, 'dp', 0, 0, tiled=True)]
    ppermute x8, waiting for transfers between devices: 31 us -> 18.9 us  [to_side(): return lax.ppermute(value, 'dp', SIDES)]
    unnamed x157 -> x153, local copies, waits for them, and re-layouts: 47.6 us -> 45.2 us
  transfers between devices with their start and end apart: 84 -> 84, of which waited for: 31 -> 32; matrix products, arithmetic and copies ran while one was open for 21% -> 22% of each run, Pallas kernels for 10% -> 10%
where the time goes in v4:
time: 1190 us; the launch traced here: 1180 us
  waiting for transfers between devices  505 us (42%)
  Pallas kernels  200 us (17%)
  starting transfers between devices  147 us (12%)
  local copies, waits for them, and re-layouts  120 us (10%)
  matrix products  99.4 us (8%)
  other arithmetic  91.4 us (8%)
  between operations  19.3 us (2%)
    all_to_all x2, waiting for transfers between devices, team_device(): up_slabs = lax.all_to_all(up_slabs, 'dp', 0, 0, tiled=True)  140 us
    ppermute x6, waiting for transfers between devices, across(): return lax.ppermute(value, 'y', swap_pairs(2))  124 us
    all_gather x4, waiting for transfers between devices, collect(): return lax.all_gather(value, TEAM, axis=0, tiled=True)  78.9 us
    pallas_call x8, Pallas kernels, slot_product(): pl.pallas_call(functools.partial(product_kernel, len(lefts)), grid_spec=p...  77.5 us
    all_to_all x4, waiting for transfers between devices, swap_all(): got = lax.all_to_all(value, 'dp', 0, 0, tiled=True)  69.3 us
    dot_general x5, matrix products, times_rows(): lax.dot_general(left, right, ROWS_DIMS, preferred_element_type=jnp.float32)  61.9 us
    pallas_call x2, Pallas kernels, row_call(): pl.pallas_call(kernel, grid=(count // ROW_STEP,), in_specs=[tile(width)]...  59.1 us
    unnamed x153, local copies, waits for them, and re-layouts  45.2 us
  transfers between devices with their start and end apart: 84, of which 32 were waited for; matrix products, arithmetic and copies ran while one was open for 22% of the time, Pallas kernels for 10%

profile of v4, /device:TPU:0, one launch (start us, length us, event | category | flops | bytes accessed | tf_op | source)
XLA Modules:
  0.0 1183.3 jit_solution(6471460643743428428)
XLA Ops:
  42.3 5.8 all-to-all-start
  63.5 37.5 %collective-permute-done.12 = bf16[704,2048]{1,0:T(8,128)(2,1)} collective-permute-done((bf16[704,2048]{1,0:T(8,128)(2,1)}, bf16[704,2048]{1,0:T(8,128)(2,1)}, u32[]{:S(2)}, u32[]{:S(2)}) %collective-permute-start.12) | collective-permute-done | bytes 2883616 | tf_op jit(solution)/shard_map/ppermute | solution.py:889
  101.1 9.6 all-to-all-done
  120.0 22.6 %all-to-all-done.1 = bf16[8,128,512]{2,1,0:T(8,128)(2,1)} async-done(((bf16[8,128,512]{2,1,0:T(8,128)(2,1)}), bf16[8,128,512]{2,1,0:T(8,128)(2,1)}, u32[]{:S(2)}, u32[]{:S(2)}) %all-to-all-start.1) | async-done | bytes 1048608 | tf_op jit(solution)/shard_map/all_to_all | solution.py:913
  156.4 8.5 fusion.39.front
  174.3 25.8 %attend.1 = (bf16[2048,512]{1,0:T(8,128)(2,1)}, bf16[2048,512]{1,0:T(8,128)(2,1)}, bf16[2048,256]{1,0:T(8,128)(2,1)}, f32[16,1,512]{2,1,0:T(1,128)}) custom-call(f32[2048,768]{1,0:T(8,128)} %fusion.39.front, f32[2048,128]{1,0:T(8,128)} %get-tuple-element.434.cosine, f32[2048,128]{1,0:T(8,128)} %get-tuple-element.435.sine, f32[16,1,512]{2,1,0:T(1,128)} %bitcast.333), custom_call_target="tpu_custom_call" | custom-call | flops 4294967296 | bytes 12582912 | tf_op jit(solution)/shard_map/attend/pallas_call | solution.py:487
  203.6 8.5 all-to-all-done.2
  215.2 6.9 convolution_convert_fusion.1
  228.1 96.2 %all-to-all-done.3 = bf16[8,704,256]{2,1,0:T(8,128)(2,1)} async-done(((bf16[8,704,256]{2,1,0:T(8,128)(2,1)}), bf16[8,704,256]{2,1,0:T(8,128)(2,1)}, u32[]{:S(2)}, u32[]{:S(2)}) %all-to-all-start.3) | async-done | bytes 2883616 | tf_op jit(solution)/shard_map/all_to_all | solution.py:980
  328.2 32.8 %reduce-scatter.3.cloned.1.call-done = bf16[128,2048]{1,0:T(8,128)(2,1)} async-done(((bf16[2048,2048]{1,0:T(8,128)(2,1)}), bf16[128,2048]{1,0:T(8,128)(2,1)}) %reduce-scatter.3.cloned.1.call-update) | async-done | bytes 524304 | tf_op jit(solution)/shard_map/reduce_scatter | solution.py:857
  368.0 6.1 pad_maximum_fusion.refs_4_.down_w
  385.1 44.0 %collective-permute-done.18 = bf16[704,2048]{1,0:T(8,128)(2,1)} collective-permute-done((bf16[704,2048]{1,0:T(8,128)(2,1)}, bf16[704,2048]{1,0:T(8,128)(2,1)}, u32[]{:S(2)}, u32[]{:S(2)}) %collective-permute-start.18) | collective-permute-done | bytes 2883616 | tf_op jit(solution)/shard_map/ppermute | solution.py:889
  432.9 5.8 all-gather.7.cloned.1.call-done.rows
  438.7 34.3 %open_rows.1 = (f32[2048,1408]{1,0:T(8,128)}, f32[2048,1408]{1,0:T(8,128)}, bf16[2048,1408]{1,0:T(8,128)(2,1)}) custom-call(bf16[2048,2048]{1,0:T(8,128)(2,1)} %all-gather.7.cloned.1.call-done.rows, bf16[1408,2048]{1,0:T(8,128)(2,1)} %constant_dynamic-update-slice_fusion.2.gate_w.refs_8_, ...), custom_call_target="tpu_custom_call" | custom-call | flops 23622320128 | bytes 40370176 | tf_op jit(solution)/shard_map/open_rows/pallas_call | solution.py:781
  473.0 7.8 slot_product.8
  481.1 7.9 slot_product.9
  491.0 8.0 slot_product.10
  499.4 5.2 collective-permute-done.20
  511.9 7.9 slot_product.11
  536.6 6.4 collective-permute-done.27
  547.3 8.6 collective-permute-start.31
  575.6 73.1 %all-gather.9.cloned.1.call-done.rows = bf16[2048,2048]{1,0:T(8,128)(2,1)} async-done(((bf16[128,2048]{1,0:T(8,128)(2,1)}), bf16[2048,2048]{1,0:T(8,128)(2,1)}) %all-gather.9.cloned.1.call-update) | async-done | bytes 8388624 | tf_op jit(solution)/shard_map/all_gather | solution.py:854
  648.7 24.8 %close_rows.1 = (bf16[2048,1408]{1,0:T(8,128)(2,1)}, bf16[2048,1408]{1,0:T(8,128)(2,1)}) custom-call(bf16[2048,2048]{1,0:T(8,128)(2,1)} %all-gather.9.cloned.1.call-done.rows, bf16[1408,2048]{1,0:T(8,128)(2,1)} %pad_maximum_fusion.refs_4_.down_w, f32[2048,2]{1,0:T(8,128)} %copy.152.share, f32[2048,1408]{1,0:T(8,128)} %get-tuple-element.221.gate_in, ...), custom_call_target="tpu_custom_call" | custom-call | flops 11811160064 | bytes 34603008 | tf_op jit(solution)/shard_map/close_rows/pallas_call | solution.py:781
  673.5 11.5 slot_product.12
  685.3 11.5 slot_product.13
  698.9 11.5 slot_product.14
  719.2 11.5 slot_product.15
  738.1 8.1 collective-permute-done.46
  750.8 7.3 collective-permute-start.51
  759.7 14.8 %fusion.40 = f32[1408,2048]{1,0:T(8,128)S(1)} fusion(bf16[2048,1408]{1,0:T(8,128)(2,1)S(1)} %bitcast.278, bf16[2048,2048]{1,0:T(8,128)(2,1)} %all-gather.7.cloned.1.call-done.rows), kind=kOutput, calls=%fused_computation.239 | convolution fusion | flops 11811160064 | bytes 25690112 | tf_op jit(solution)/shard_map/dot_general | solution.py:47
  785.2 17.1 %fusion.42 = f32[1408,2048]{1,0:T(8,128)S(1)} fusion(bf16[2048,1408]{1,0:T(8,128)(2,1)} %get-tuple-element.275.refs_4_.refs_5_.refs_6_.refs_7_, bf16[2048,2048]{1,0:T(8,128)(2,1)} %all-gather.7.cloned.1.call-done.rows), kind=kOutput, calls=%fused_computation.241 | convolution fusion | flops 11811160064 | bytes 25690112 | tf_op jit(solution)/shard_map/dot_general | solution.py:47
  807.2 14.8 %fusion.43 = f32[1408,2048]{1,0:T(8,128)S(1)} fusion(bf16[2048,1408]{1,0:T(8,128)(2,1)S(1)} %bitcast.280, bf16[2048,2048]{1,0:T(8,128)(2,1)} %all-gather.9.cloned.1.call-done.rows), kind=kOutput, calls=%fused_computation.242 | convolution fusion | flops 11811160064 | bytes 25690112 | tf_op jit(solution)/shard_map/dot_general | solution.py:47
  827.3 19.9 %collective-permute-done.53 = bf16[704,2048]{1,0:T(8,128)(2,1)S(1)} collective-permute-done((bf16[704,2048]{1,0:T(8,128)(2,1)}, bf16[704,2048]{1,0:T(8,128)(2,1)S(1)}, u32[]{:S(2)}, u32[]{:S(2)}) %collective-permute-start.53) | collective-permute-done | bytes 2883616 | tf_op jit(solution)/shard_map/ppermute | solution.py:889
  859.5 10.5 fusion.41.pull
  870.0 38.1 %attend_back.1 = bf16[2048,768]{1,0:T(8,128)(2,1)} custom-call(f32[2048,512]{1,0:T(8,128)} %fusion.41.pull, f32[2048,4]{1,0:T(8,128)} %get-tuple-element.385.gate, bf16[2048,512]{1,0:T(8,128)(2,1)} %get-tuple-element.270.query_in, bf16[2048,256]{1,0:T(8,128)(2,1)} %get-tuple-element.271.pair, bf16[128,2048]{1,0:T(8,128)(2,1)} %slice_bitcast_fusion.pair_up, ...), custom_call_target="tpu_custom_call" | custom-call | flops 10737418240 | bytes 12582912 | tf_op jit(solution)/shard_map/attend_back/pallas_call | solution.py:605
  908.1 8.5 collective-permute-done.54
  918.0 11.6 convolution_convert_fusion
  937.6 5.4 add_convert_fusion
  951.5 10.4 convolution_convert_fusion.2
  968.3 14.4 %collective-permute-done.56 = bf16[8,128,768]{2,1,0:T(8,128)(2,1)S(1)} collective-permute-done((bf16[8,128,768]{2,1,0:T(8,128)(2,1)S(1)}, bf16[8,128,768]{2,1,0:T(8,128)(2,1)S(1)}, u32[]{:S(2)}, u32[]{:S(2)}) %collective-permute-start.56) | collective-permute-done | bytes 1572896 | tf_op jit(solution)/shard_map/ppermute | solution.py:1070
  985.9 17.1 %collective-permute-start.58 = (bf16[8,128,512]{2,1,0:T(8,128)(2,1)}, bf16[8,128,512]{2,1,0:T(8,128)(2,1)}, u32[]{:S(2)}, u32[]{:S(2)}) collective-permute-start(bf16[8,128,512]{2,1,0:T(8,128)(2,1)} %get-tuple-element.372), channel_id=1, source_target_pairs={{2,0},{0,1},{3,2},{1,3},{6,4},{4,5},{7,6},{5,7},{10,8},{8,9},{11,1... | collective-permute-start | bytes 3145736 | tf_op jit(solution)/shard_map/ppermute | solution.py:1070
  1004.6 44.0 %all-to-all-done.5 = bf16[8,704,256]{2,1,0:T(8,128)(2,1)} async-done(((bf16[8,704,256]{2,1,0:T(8,128)(2,1)}), bf16[8,704,256]{2,1,0:T(8,128)(2,1)}, u32[]{:S(2)}, u32[]{:S(2)}) %all-to-all-start.5) | async-done | bytes 2883616 | tf_op jit(solution)/shard_map/all_to_all | solution.py:1058
  1056.4 6.3 copy.170
  1067.0 4.8 convert_bitcast_fusion
  1071.9 6.3 copy.171
  1078.2 28.5 %all-to-all-done.6 = bf16[8,128,768]{2,1,0:T(8,128)(2,1)} async-done(((bf16[8,128,768]{2,1,0:T(8,128)(2,1)}), bf16[8,128,768]{2,1,0:T(8,128)(2,1)}, u32[]{:S(2)}, u32[]{:S(2)}) %all-to-all-start.6) | async-done | bytes 1572896 | tf_op jit(solution)/shard_map/all_to_all | solution.py:913
  1115.8 13.7 %collective-permute-done.69 = bf16[704,2048]{1,0:T(8,128)(2,1)} collective-permute-done((bf16[704,2048]{1,0:T(8,128)(2,1)}, bf16[704,2048]{1,0:T(8,128)(2,1)}, u32[]{:S(2)}, u32[]{:S(2)}) %collective-permute-start.69) | collective-permute-done | bytes 2883616 | tf_op jit(solution)/shard_map/ppermute | solution.py:889
  1129.5 7.4 add_bitcast_fusion
  (459 shorter events, 314.7 us)
Async XLA Ops:
  7.3 135.4 %all-gather.5.cloned.1.call-start = ((), (), s32[]{:S(2)}) async-start(), calls=%async_computation.10 | async-start | bytes 8912896 | tf_op jit(solution)/shard_map/all_gather | solution.py:854
  36.8 64.3 %collective-permute-start.12 = (bf16[704,2048]{1,0:T(8,128)(2,1)}, bf16[704,2048]{1,0:T(8,128)(2,1)}, u32[]{:S(2)}, u32[]{:S(2)}) collective-permute-start(bf16[704,2048]{1,0:T(8,128)(2,1)} %bitcast.302), channel_id=1, source_target_pairs={{0,2},{2,0},{1,3},{3,1},{4,6},{6,4},{5,7},{7,5},{8,10},{10,8},{9,1... | collective-permute-start | bytes 8650760 | tf_op jit(solution)/shard_map/ppermute | solution.py:889
  42.3 68.4 %all-to-all-start = ((bf16[8,128,768]{2,1,0:T(8,128)(2,1)}), bf16[8,128,768]{2,1,0:T(8,128)(2,1)S(1)}, u32[]{:S(2)}, u32[]{:S(2)}) async-start(bf16[8,128,768]{2,1,0:T(8,128)(2,1)} %pad_maximum_fusion.3), calls=%async_computation | async-start | bytes 3145728 | tf_op jit(solution)/shard_map/all_to_all | solution.py:913
  110.7 31.9 %all-to-all-start.1 = ((bf16[8,128,512]{2,1,0:T(8,128)(2,1)}), bf16[8,128,512]{2,1,0:T(8,128)(2,1)}, u32[]{:S(2)}, u32[]{:S(2)}) async-start(bf16[8,128,512]{2,1,0:T(8,128)(2,1)} %pad_maximum_fusion.4), calls=%async_computation.1 | async-start | bytes 2097152 | tf_op jit(solution)/shard_map/all_to_all | solution.py:913
  115.0 36.0 %collective-permute-start.14 = (bf16[8,128,768]{2,1,0:T(8,128)(2,1)S(1)}, bf16[8,128,768]{2,1,0:T(8,128)(2,1)}, u32[]{:S(2)}, u32[]{:S(2)}) collective-permute-start(bf16[8,128,768]{2,1,0:T(8,128)(2,1)S(1)} %all-to-all-done), channel_id=1, source_target_pairs={{0,2},{1,0},{2,3},{3,1},{4,6},{5,4},{6,7},{7,5},{8,10},{9,8},{10,1... | collective-permute-start | bytes 4718600 | tf_op jit(solution)/shard_map/ppermute | solution.py:907
  116.7 34.4 %collective-permute-start.13 = (bf16[8,128,768]{2,1,0:T(8,128)(2,1)S(1)}, bf16[8,128,768]{2,1,0:T(8,128)(2,1)}, u32[]{:S(2)}, u32[]{:S(2)}) collective-permute-start(bf16[8,128,768]{2,1,0:T(8,128)(2,1)S(1)} %all-to-all-done), channel_id=1, source_target_pairs={{1,2},{2,1},{5,6},{6,5},{9,10},{10,9},{13,14},{14,13},{17,18},{18,... | collective-permute-start | bytes 4718600 | tf_op jit(solution)/shard_map/ppermute | solution.py:906
  142.6 69.5 %all-to-all-start.2 = ((bf16[8,704,256]{2,1,0:T(8,128)(2,1)}), bf16[8,704,256]{2,1,0:T(8,128)(2,1)}, u32[]{:S(2)}, u32[]{:S(2)}) async-start(bf16[8,704,256]{2,1,0:T(8,128)(2,1)} %bitcast.283), calls=%async_computation.2 | async-start | bytes 5767168 | tf_op jit(solution)/shard_map/all_to_all | solution.py:913
  147.1 213.9 %reduce-scatter.3.cloned.1.call-start = ((), (), s32[]{:S(2)}) async-start(), calls=%async_computation.11 | async-start | bytes 8912896 | tf_op jit(solution)/shard_map/reduce_scatter | solution.py:857
  165.0 35.1 %collective-permute-start.16 = (bf16[8,128,512]{2,1,0:T(8,128)(2,1)}, bf16[8,128,512]{2,1,0:T(8,128)(2,1)}, u32[]{:S(2)}, u32[]{:S(2)}) collective-permute-start(bf16[8,128,512]{2,1,0:T(8,128)(2,1)} %all-to-all-done.1), channel_id=1, source_target_pairs={{0,2},{1,0},{2,3},{3,1},{4,6},{5,4},{6,7},{7,5},{8,10},{9,8},{10,1... | collective-permute-start | bytes 3145736 | tf_op jit(solution)/shard_map/ppermute | solution.py:907
  168.4 31.7 %collective-permute-start.15 = (bf16[8,128,512]{2,1,0:T(8,128)(2,1)}, bf16[8,128,512]{2,1,0:T(8,128)(2,1)}, u32[]{:S(2)}, u32[]{:S(2)}) collective-permute-start(bf16[8,128,512]{2,1,0:T(8,128)(2,1)} %all-to-all-done.1), channel_id=1, source_target_pairs={{1,2},{2,1},{5,6},{6,5},{9,10},{10,9},{13,14},{14,13},{17,18},{18,... | collective-permute-start | bytes 3145736 | tf_op jit(solution)/shard_map/ppermute | solution.py:906
  222.2 102.2 %all-to-all-start.3 = ((bf16[8,704,256]{2,1,0:T(8,128)(2,1)}), bf16[8,704,256]{2,1,0:T(8,128)(2,1)}, u32[]{:S(2)}, u32[]{:S(2)}) async-start(bf16[8,704,256]{2,1,0:T(8,128)(2,1)} %bitcast.34), calls=%async_computation.4 | async-start | bytes 5767168 | tf_op jit(solution)/shard_map/all_to_all | solution.py:980
  226.6 212.1 %all-gather.7.cloned.1.call-start = ((), (), s32[]{:S(2)}) async-start(), calls=%async_computation.12 | async-start | bytes 8912896 | tf_op jit(solution)/shard_map/all_gather | solution.py:854
  226.6 135.5 %collective-permute-start.17 = (bf16[704,2048]{1,0:T(8,128)(2,1)S(1)}, bf16[704,2048]{1,0:T(8,128)(2,1)}, u32[]{:S(2)}, u32[]{:S(2)}) collective-permute-start(bf16[704,2048]{1,0:T(8,128)(2,1)S(1)} %bitcast.284), channel_id=1, source_target_pairs={{0,2},{2,0},{1,3},{3,1},{4,6},{6,4},{5,7},{7,5},{8,10},{10,8},{9,1... | collective-permute-start | bytes 8650760 | tf_op jit(solution)/shard_map/ppermute | solution.py:889
  363.9 284.8 %all-gather.9.cloned.1.call-start = ((), (), s32[]{:S(2)}) async-start(), calls=%async_computation.13 | async-start | bytes 8912896 | tf_op jit(solution)/shard_map/all_gather | solution.py:854
  364.4 64.7 %collective-permute-start.18 = (bf16[704,2048]{1,0:T(8,128)(2,1)}, bf16[704,2048]{1,0:T(8,128)(2,1)}, u32[]{:S(2)}, u32[]{:S(2)}) collective-permute-start(bf16[704,2048]{1,0:T(8,128)(2,1)} %bitcast.286), channel_id=1, source_target_pairs={{0,2},{2,0},{1,3},{3,1},{4,6},{6,4},{5,7},{7,5},{8,10},{10,8},{9,1... | collective-permute-start | bytes 8650760 | tf_op jit(solution)/shard_map/ppermute | solution.py:889
  505.4 16.2 %collective-permute-start.22 = (bf16[128,2048]{1,0:T(8,128)(2,1)}, bf16[128,2048]{1,0:T(8,128)(2,1)S(1)}, u32[]{:S(2)}, u32[]{:S(2)}) collective-permute-start(bf16[128,2048]{1,0:T(8,128)(2,1)} %slice.127), channel_id=1, source_target_pairs={{0,4},{4,0},{8,12},{12,8},{16,20},{20,16},{24,28},{28,24},{1,5},{5... | collective-permute-start | bytes 1572872 | tf_op jit(solution)/shard_map/ppermute | solution.py:649
  506.9 14.7 %collective-permute-start.23 = (bf16[128,2048]{1,0:T(8,128)(2,1)}, bf16[128,2048]{1,0:T(8,128)(2,1)}, u32[]{:S(2)}, u32[]{:S(2)}) collective-permute-start(bf16[128,2048]{1,0:T(8,128)(2,1)} %fusion.11), channel_id=1, source_target_pairs={{0,8},{4,12},{1,9},{5,13},{2,10},{6,14},{3,11},{7,15}} | collective-permute-start | bytes 1572872 | tf_op jit(solution)/shard_map/ppermute | solution.py:662
  526.7 16.4 %collective-permute-start.27 = (bf16[128,2048]{1,0:T(8,128)(2,1)}, bf16[128,2048]{1,0:T(8,128)(2,1)S(1)}, u32[]{:S(2)}, u32[]{:S(2)}) collective-permute-start(bf16[128,2048]{1,0:T(8,128)(2,1)} %get-tuple-element.364), channel_id=1, source_target_pairs={{0,8},{4,12},{8,16},{12,20},{1,9},{5,13},{9,17},{13,21},{2,10},{6,... | collective-permute-start | bytes 1572872 | tf_op jit(solution)/shard_map/ppermute | solution.py:662
  544.1 22.3 %collective-permute-start.30 = (bf16[128,2048]{1,0:T(8,128)(2,1)}, bf16[128,2048]{1,0:T(8,128)(2,1)}, u32[]{:S(2)}, u32[]{:S(2)}) collective-permute-start(bf16[128,2048]{1,0:T(8,128)(2,1)} %slice.133), channel_id=1, source_target_pairs={{0,4},{4,0},{8,12},{12,8},{16,20},{20,16},{24,28},{28,24},{1,5},{5... | collective-permute-start | bytes 1572872 | tf_op jit(solution)/shard_map/ppermute | solution.py:649
  547.3 19.4 %collective-permute-start.31 = (bf16[128,2048]{1,0:T(8,128)(2,1)}, bf16[128,2048]{1,0:T(8,128)(2,1)S(1)}, u32[]{:S(2)}, u32[]{:S(2)}) collective-permute-start(bf16[128,2048]{1,0:T(8,128)(2,1)} %get-tuple-element.362), channel_id=1, source_target_pairs={{0,8},{4,12},{8,16},{12,20},{16,24},{20,28},{1,9},{5,13},{9,17},{1... | collective-permute-start | bytes 1572872 | tf_op jit(solution)/shard_map/ppermute | solution.py:662
  555.9 14.6 %collective-permute-start.32 = (bf16[128,2048]{1,0:T(8,128)(2,1)S(1)}, bf16[128,2048]{1,0:T(8,128)(2,1)S(1)}, u32[]{:S(2)}, u32[]{:S(2)}) collective-permute-start(bf16[128,2048]{1,0:T(8,128)(2,1)S(1)} %get-tuple-element.361), channel_id=1, source_target_pairs={{24,16},{28,20},{16,8},{20,12},{8,0},{12,4},{25,17},{29,21},{17,9}... | collective-permute-start | bytes 1572872 | tf_op jit(solution)/shard_map/ppermute | solution.py:665
  575.5 284.0 %all-gather.11.cloned.1.call-start = ((), (), s32[]{:S(2)}) async-start(), calls=%async_computation.14 | async-start | bytes 8912896 | tf_op jit(solution)/shard_map/all_gather | solution.py:854
  713.3 17.4 %collective-permute-start.45 = (bf16[256,2048]{1,0:T(8,128)(2,1)}, bf16[256,2048]{1,0:T(8,128)(2,1)S(1)}, u32[]{:S(2)}, u32[]{:S(2)}) collective-permute-start(bf16[256,2048]{1,0:T(8,128)(2,1)} %get-tuple-element.246), channel_id=1, source_target_pairs={{0,1},{1,0},{2,3},{3,2},{4,5},{5,4},{6,7},{7,6},{8,9},{9,8},{10,11... | collective-permute-start | bytes 3145736 | tf_op jit(solution)/shard_map/ppermute | solution.py:653
  714.2 18.7 %collective-permute-start.43 = (bf16[128,2048]{1,0:T(8,128)(2,1)}, bf16[128,2048]{1,0:T(8,128)(2,1)S(1)}, u32[]{:S(2)}, u32[]{:S(2)}) collective-permute-start(bf16[128,2048]{1,0:T(8,128)(2,1)} %fusion.12), channel_id=1, source_target_pairs={{0,8},{4,12},{1,9},{5,13},{2,10},{6,14},{3,11},{7,15}} | collective-permute-start | bytes 1572872 | tf_op jit(solution)/shard_map/ppermute | solution.py:662
  717.1 15.8 %collective-permute-start.44 = (bf16[128,2048]{1,0:T(8,128)(2,1)}, bf16[128,2048]{1,0:T(8,128)(2,1)}, u32[]{:S(2)}, u32[]{:S(2)}) collective-permute-start(bf16[128,2048]{1,0:T(8,128)(2,1)} %fusion.12), channel_id=1, source_target_pairs={{24,16},{28,20},{25,17},{29,21},{26,18},{30,22},{27,19},{31,23}} | collective-permute-start | bytes 1572872 | tf_op jit(solution)/shard_map/ppermute | solution.py:665
  748.7 32.1 %collective-permute-start.50 = (bf16[128,2048]{1,0:T(8,128)(2,1)S(1)}, bf16[128,2048]{1,0:T(8,128)(2,1)S(1)}, u32[]{:S(2)}, u32[]{:S(2)}) collective-permute-start(bf16[128,2048]{1,0:T(8,128)(2,1)S(1)} %slice.141), channel_id=1, source_target_pairs={{0,4},{4,0},{8,12},{12,8},{16,20},{20,16},{24,28},{28,24},{1,5},{5... | collective-permute-start | bytes 1572872 | tf_op jit(solution)/shard_map/ppermute | solution.py:649
  750.8 30.0 %collective-permute-start.51 = (bf16[128,2048]{1,0:T(8,128)(2,1)S(1)}, bf16[128,2048]{1,0:T(8,128)(2,1)S(1)}, u32[]{:S(2)}, u32[]{:S(2)}) collective-permute-start(bf16[128,2048]{1,0:T(8,128)(2,1)S(1)} %get-tuple-element.358), channel_id=1, source_target_pairs={{0,8},{4,12},{8,16},{12,20},{16,24},{20,28},{1,9},{5,13},{9,17},{1... | collective-permute-start | bytes 1572872 | tf_op jit(solution)/shard_map/ppermute | solution.py:662
  758.2 22.7 %collective-permute-start.52 = (bf16[128,2048]{1,0:T(8,128)(2,1)S(1)}, bf16[128,2048]{1,0:T(8,128)(2,1)S(1)}, u32[]{:S(2)}, u32[]{:S(2)}) collective-permute-start(bf16[128,2048]{1,0:T(8,128)(2,1)S(1)} %get-tuple-element.357), channel_id=1, source_target_pairs={{24,16},{28,20},{16,8},{20,12},{8,0},{12,4},{25,17},{29,21},{17,9}... | collective-permute-start | bytes 1572872 | tf_op jit(solution)/shard_map/ppermute | solution.py:665
  783.7 63.5 %collective-permute-start.53 = (bf16[704,2048]{1,0:T(8,128)(2,1)}, bf16[704,2048]{1,0:T(8,128)(2,1)S(1)}, u32[]{:S(2)}, u32[]{:S(2)}) collective-permute-start(bf16[704,2048]{1,0:T(8,128)(2,1)} %slice.204), channel_id=1, source_target_pairs={{0,2},{2,0},{1,3},{3,1},{4,6},{6,4},{5,7},{7,5},{8,10},{10,8},{9,1... | collective-permute-start | bytes 8650760 | tf_op jit(solution)/shard_map/ppermute | solution.py:889
  850.1 68.0 %all-to-all-start.4 = ((bf16[8,704,256]{2,1,0:T(8,128)(2,1)}), bf16[8,704,256]{2,1,0:T(8,128)(2,1)S(1)}, u32[]{:S(2)}, u32[]{:S(2)}) async-start(bf16[8,704,256]{2,1,0:T(8,128)(2,1)} %bitcast.289), calls=%async_computation.5 | async-start | bytes 5767168 | tf_op jit(solution)/shard_map/all_to_all | solution.py:1043
  853.8 254.2 %reduce-scatter.5.cloned.1.call-start = ((), (), s32[]{:S(2)}) async-start(), calls=%async_computation.15 | async-start | bytes 8912896 | tf_op jit(solution)/shard_map/reduce_scatter | solution.py:857
  853.8 62.7 %collective-permute-start.54 = (bf16[704,2048]{1,0:T(8,128)(2,1)}, bf16[704,2048]{1,0:T(8,128)(2,1)}, u32[]{:S(2)}, u32[]{:S(2)}) collective-permute-start(bf16[704,2048]{1,0:T(8,128)(2,1)} %slice.203), channel_id=1, source_target_pairs={{0,2},{2,0},{1,3},{3,1},{4,6},{6,4},{5,7},{7,5},{8,10},{10,8},{9,1... | collective-permute-start | bytes 8650760 | tf_op jit(solution)/shard_map/ppermute | solution.py:889
  934.1 15.3 %collective-permute-start.37 = (bf16[128,512]{1,0:T(8,128)(2,1)S(1)}, bf16[128,512]{1,0:T(8,128)(2,1)S(1)}, u32[]{:S(2)}, u32[]{:S(2)}) collective-permute-start(bf16[128,512]{1,0:T(8,128)(2,1)S(1)} %bitcast.330), channel_id=1, source_target_pairs={{0,2},{1,3},{2,0},{3,1},{4,6},{5,7},{6,4},{7,5},{8,10},{9,11},{10,... | collective-permute-start | bytes 393224 | tf_op jit(solution)/shard_map/ppermute | solution.py:841
  944.8 103.8 %all-to-all-start.5 = ((bf16[8,704,256]{2,1,0:T(8,128)(2,1)}), bf16[8,704,256]{2,1,0:T(8,128)(2,1)}, u32[]{:S(2)}, u32[]{:S(2)}) async-start(bf16[8,704,256]{2,1,0:T(8,128)(2,1)} %bitcast.288), calls=%async_computation.6 | async-start | bytes 5767168 | tf_op jit(solution)/shard_map/all_to_all | solution.py:1058
  962.3 20.4 %collective-permute-start.56 = (bf16[8,128,768]{2,1,0:T(8,128)(2,1)S(1)}, bf16[8,128,768]{2,1,0:T(8,128)(2,1)S(1)}, u32[]{:S(2)}, u32[]{:S(2)}) collective-permute-start(bf16[8,128,768]{2,1,0:T(8,128)(2,1)S(1)} %get-tuple-element.356), channel_id=1, source_target_pairs={{2,0},{0,1},{3,2},{1,3},{6,4},{4,5},{7,6},{5,7},{10,8},{8,9},{11,1... | collective-permute-start | bytes 4718600 | tf_op jit(solution)/shard_map/ppermute | solution.py:1070
  962.3 20.4 %collective-permute-start.55 = (bf16[8,128,768]{2,1,0:T(8,128)(2,1)S(1)}, bf16[8,128,768]{2,1,0:T(8,128)(2,1)S(1)}, u32[]{:S(2)}, u32[]{:S(2)}) collective-permute-start(bf16[8,128,768]{2,1,0:T(8,128)(2,1)S(1)} %get-tuple-element.355), channel_id=1, source_target_pairs={{1,2},{2,1},{5,6},{6,5},{9,10},{10,9},{13,14},{14,13},{17,18},{18,... | collective-permute-start | bytes 4718600 | tf_op jit(solution)/shard_map/ppermute | solution.py:1069
  985.9 76.8 %collective-permute-start.58 = (bf16[8,128,512]{2,1,0:T(8,128)(2,1)}, bf16[8,128,512]{2,1,0:T(8,128)(2,1)}, u32[]{:S(2)}, u32[]{:S(2)}) collective-permute-start(bf16[8,128,512]{2,1,0:T(8,128)(2,1)} %get-tuple-element.372), channel_id=1, source_target_pairs={{2,0},{0,1},{3,2},{1,3},{6,4},{4,5},{7,6},{5,7},{10,8},{8,9},{11,1... | collective-permute-start | bytes 3145736 | tf_op jit(solution)/shard_map/ppermute | solution.py:1070
  1003.0 59.7 %collective-permute-start.57 = (bf16[8,128,512]{2,1,0:T(8,128)(2,1)}, bf16[8,128,512]{2,1,0:T(8,128)(2,1)}, u32[]{:S(2)}, u32[]{:S(2)}) collective-permute-start(bf16[8,128,512]{2,1,0:T(8,128)(2,1)} %get-tuple-element.371), channel_id=1, source_target_pairs={{1,2},{2,1},{5,6},{6,5},{9,10},{10,9},{13,14},{14,13},{17,18},{18,... | collective-permute-start | bytes 3145736 | tf_op jit(solution)/shard_map/ppermute | solution.py:1069
  1048.7 58.1 %all-to-all-start.6 = ((bf16[8,128,768]{2,1,0:T(8,128)(2,1)}), bf16[8,128,768]{2,1,0:T(8,128)(2,1)}, u32[]{:S(2)}, u32[]{:S(2)}) async-start(bf16[8,128,768]{2,1,0:T(8,128)(2,1)} %add_convert_fusion.2), calls=%async_computation.7 | async-start | bytes 3145728 | tf_op jit(solution)/shard_map/all_to_all | solution.py:913
  1065.6 63.8 %collective-permute-start.69 = (bf16[704,2048]{1,0:T(8,128)(2,1)}, bf16[704,2048]{1,0:T(8,128)(2,1)}, u32[]{:S(2)}, u32[]{:S(2)}) collective-permute-start(bf16[704,2048]{1,0:T(8,128)(2,1)} %slice.202), channel_id=1, source_target_pairs={{0,2},{2,0},{1,3},{3,1},{4,6},{6,4},{5,7},{7,5},{8,10},{10,8},{9,1... | collective-permute-start | bytes 8650760 | tf_op jit(solution)/shard_map/ppermute | solution.py:889
  1107.9 30.5 %collective-permute-start.67 = (bf16[4,128,768]{2,1,0:T(8,128)(2,1)S(1)}, bf16[4,128,768]{2,1,0:T(8,128)(2,1)}, u32[]{:S(2)}, u32[]{:S(2)}) collective-permute-start(bf16[4,128,768]{2,1,0:T(8,128)(2,1)S(1)} %dynamic-slice_bitcast_fusion.4), channel_id=1, source_target_pairs={{0,1},{1,0},{2,3},{3,2},{4,5},{5,4},{6,7},{7,6},{8,9},{9,8},{10,11... | collective-permute-start | bytes 2359304 | tf_op jit(solution)/shard_map/ppermute | solution.py:1078
  1111.0 25.8 %collective-permute-start.59 = (f32[3,2048]{1,0:T(4,128)S(1)}, f32[3,2048]{1,0:T(4,128)S(1)}, u32[]{:S(2)}, u32[]{:S(2)}) collective-permute-start(f32[3,2048]{1,0:T(4,128)S(1)} %maximum_maximum_fusion), channel_id=1, source_target_pairs={{0,1},{1,0},{2,3},{3,2},{4,5},{5,4},{6,7},{7,6},{8,9},{9,8},{10,11... | collective-permute-start | bytes 73736 | tf_op jit(solution)/shard_map/ppermute | solution.py:1105
  1111.5 43.2 %all-to-all-start.7 = ((bf16[8,128,512]{2,1,0:T(8,128)(2,1)}), bf16[8,128,512]{2,1,0:T(8,128)(2,1)}, u32[]{:S(2)}, u32[]{:S(2)}) async-start(bf16[8,128,512]{2,1,0:T(8,128)(2,1)} %add_convert_fusion.3), calls=%async_computation.9 | async-start | bytes 2097152 | tf_op jit(solution)/shard_map/all_to_all | solution.py:1095
  1149.3 19.7 %collective-permute-start.65 = (f32[128,512]{1,0:T(8,128)}, f32[128,512]{1,0:T(8,128)}, u32[]{:S(2)}, u32[]{:S(2)}) collective-permute-start(f32[128,512]{1,0:T(8,128)} %bitcast.272), channel_id=1, source_target_pairs={{0,2},{1,3},{2,0},{3,1},{4,6},{5,7},{6,4},{7,5},{8,10},{9,11},{10,... | collective-permute-start | bytes 786440 | tf_op jit(solution)/shard_map/ppermute | solution.py:841
  1151.5 17.5 %collective-permute-start.66 = (f32[128,512]{1,0:T(8,128)}, f32[128,512]{1,0:T(8,128)}, u32[]{:S(2)}, u32[]{:S(2)}) collective-permute-start(f32[128,512]{1,0:T(8,128)} %bitcast.271), channel_id=1, source_target_pairs={{0,3},{1,2},{2,1},{3,0},{4,7},{5,6},{6,5},{7,4},{8,11},{9,10},{10,... | collective-permute-start | bytes 786440 | tf_op jit(solution)/shard_map/ppermute | solution.py:841
  1151.6 17.5 %collective-permute-start.64 = (f32[128,512]{1,0:T(8,128)S(1)}, f32[128,512]{1,0:T(8,128)}, u32[]{:S(2)}, u32[]{:S(2)}) collective-permute-start(f32[128,512]{1,0:T(8,128)S(1)} %bitcast.317), channel_id=1, source_target_pairs={{0,1},{1,0},{2,3},{3,2},{4,5},{5,4},{6,7},{7,6},{8,9},{9,8},{10,11... | collective-permute-start | bytes 786440 | tf_op jit(solution)/shard_map/ppermute | solution.py:841
  1152.3 14.9 %collective-permute-start.63 = (f32[3,2048]{1,0:T(4,128)S(1)}, f32[3,2048]{1,0:T(4,128)S(1)}, u32[]{:S(2)}, u32[]{:S(2)}) collective-permute-start(f32[3,2048]{1,0:T(4,128)S(1)} %add.417), channel_id=1, source_target_pairs={{0,16},{4,20},{8,24},{12,28},{16,0},{20,4},{24,8},{28,12},{1,17},{... | collective-permute-start | bytes 73736 | tf_op jit(solution)/shard_map/ppermute | solution.py:1105
  1156.6 14.7 %collective-permute-start.68 = (bf16[4,128,512]{2,1,0:T(8,128)(2,1)}, bf16[4,128,512]{2,1,0:T(8,128)(2,1)}, u32[]{:S(2)}, u32[]{:S(2)}) collective-permute-start(bf16[4,128,512]{2,1,0:T(8,128)(2,1)} %dynamic-slice_bitcast_fusion.6), channel_id=1, source_target_pairs={{0,1},{1,0},{2,3},{3,2},{4,5},{5,4},{6,7},{7,6},{8,9},{9,8},{10,11... | collective-permute-start | bytes 1572872 | tf_op jit(solution)/shard_map/ppermute | solution.py:1078
  (107 other events, 1975.6 us)
Sparse Core Ops, SparseCore 0:
  20.3 104.6 all-gather.4
  222.3 138.6 reduce-scatter.2
  364.0 74.6 all-gather.6
  575.7 73.0 all-gather.8
  783.8 74.6 all-gather.10
  929.7 173.5 reduce-scatter.4

commit v5 on v4

--- a/solution.py
+++ b/solution.py
@@ -759,18 +759,19 @@
 def open_kernel(rows, gate_w, up_w, share, gate_out, up_out, inner_out):
     gate = nt(rows[...], gate_w[...])
     up = nt(rows[...], up_w[...])
-    gate_out[...] = gate
-    up_out[...] = up
+    gate_out[...] = gate.astype(gate_out.dtype)
+    up_out[...] = up.astype(up_out.dtype)
     inner_out[...] = (
         gate / (1.0 + jnp.exp(-gate)) * up * share_lanes(share[...], gate.shape[1])
     ).astype(jnp.bfloat16)
 
 
 def close_kernel(rows, down_w, share, gate_in, up_in, gate_out, up_out):
-    gate = gate_in[...]
+    gate = gate_in[...].astype(jnp.float32)
+    up = up_in[...].astype(jnp.float32)
     pull = nt(rows[...], down_w[...]) * share_lanes(share[...], gate.shape[1])
     sigma = 1.0 / (1.0 + jnp.exp(-gate))
-    gate_out[...] = (pull * up_in[...] * sigma * (1.0 + gate * (1.0 - sigma))).astype(jnp.bfloat16)
+    gate_out[...] = (pull * up * sigma * (1.0 + gate * (1.0 - sigma))).astype(jnp.bfloat16)
     up_out[...] = (pull * gate * sigma).astype(jnp.bfloat16)
 
 
@@ -994,7 +995,7 @@
         normed2,
         [gate_w, up_w],
         [feed_share],
-        [jnp.float32, jnp.float32, low],
+        [low, low, low],
         "open_rows",
     )
     result = hidden1 + scatter_run(
@@ -1053,7 +1054,7 @@
         units,
         expert_count,
     )
-    front_back, gate_slabs, up_got = hold(front_back, gate_slabs, up_got)
+    front_back, gate_slabs = hold(front_back, gate_slabs)
     up_slabs = rows_for_owners(up_near + up_got.astype(jnp.float32))
     up_slabs = lax.all_to_all(up_slabs, "dp", 0, 0, tiled=True)
     out_grad = times_rows(grad_hidden_rows, mixed_low)
@@ -1083,16 +1084,22 @@
         )
         return rows.astype(jnp.float32)
 
+    middle = hidden // 2
     front_heads = undeal_heads(front_grad)
-    front_heads, out_grad = hold(front_heads, out_grad)
+    front_heads, out_grad, down_sent = hold(front_heads, out_grad, down_sent)
+    down_first = across(down_sent[:middle])
+    front_heads, up_slabs, down_first = hold(front_heads, up_slabs, down_first)
     out_heads = undeal_heads(out_grad)
     out_heads, down_sent = hold(out_heads, down_sent)
-    down_sum = down_near + across(down_sent).astype(jnp.float32)
-    front_heads, up_slabs = hold(front_heads, up_slabs)
+    down_second = across(down_sent[middle:])
     front_heads, out_heads = swap_all(front_heads, out_heads)
-    out_heads, grad_field, grad_gain1 = hold(out_heads, grad_field, grad_gain1)
+    out_heads, grad_field, grad_gain1, down_second = hold(
+        out_heads, grad_field, grad_gain1, down_second
+    )
     input_grad = from_rows(grad_field)
     out_heads = lax.all_to_all(out_heads, "dp", 0, 0, tiled=True)
+    down_got = jnp.concatenate([down_first, down_second], axis=0)
+    down_sum = down_near + down_got.astype(jnp.float32)
     grad_gate_out, grad_up_out = own_rows(gate_slabs), own_rows(up_slabs)
     front_out, out_back = gather_heads(front_heads), gather_heads(out_heads)
     grad_out = out_back.reshape(local_heads, depth, expert_count, HEAD).transpose(2, 0, 3, 1)

time: 1190 us -> 1170 us (0.983)
  waiting for transfers between devices: 505 us -> 477 us
    all_to_all x2, waiting for transfers between devices: 140 us -> 101 us  [team_device(): up_slabs = lax.all_to_all(up_slabs, 'dp', 0, 0, tiled=True)]
    ppermute x12, waiting for transfers between devices: 10.5 us -> 43.1 us  [exchange(): got.append(lax.ppermute(part, QUAD, [(p, p ^ step) for p in range(4)]))]
    ppermute x6 -> x7, starting transfers between devices: 8.65 us -> 29.2 us  [across(): return lax.ppermute(value, 'y', swap_pairs(2))]
    ppermute x6 -> x7, waiting for transfers between devices: 124 us -> 103 us  [across(): return lax.ppermute(value, 'y', swap_pairs(2))]
    ppermute x2, starting transfers between devices: 17.1 us -> 0.02 us  [undeal_heads(): lax.ppermute(second, QUAD, BACK_SECOND).astype(jnp.float32)]
    unnamed x153 -> x151, local copies, waits for them, and re-layouts: 45.2 us -> 44.7 us
  transfers between devices with their start and end apart: 84 -> 85, of which waited for: 32 -> 33; matrix products, arithmetic and copies ran while one was open for 22% -> 24% of each run, Pallas kernels for 10% -> 11%
where the time goes in v5:
time: 1170 us; the launch traced here: 1160 us
  waiting for transfers between devices  477 us (41%)
  Pallas kernels  199 us (17%)
  starting transfers between devices  150 us (13%)
  local copies, waits for them, and re-layouts  120 us (10%)
  matrix products  105 us (9%)
  other arithmetic  90.2 us (8%)
  between operations  19.3 us (2%)
    ppermute x7, waiting for transfers between devices, across(): return lax.ppermute(value, 'y', swap_pairs(2))  103 us
    all_to_all x2, waiting for transfers between devices, team_device(): up_slabs = lax.all_to_all(up_slabs, 'dp', 0, 0, tiled=True)  101 us
    all_gather x4, waiting for transfers between devices, collect(): return lax.all_gather(value, TEAM, axis=0, tiled=True)  79 us
    pallas_call x8, Pallas kernels, slot_product(): pl.pallas_call(functools.partial(product_kernel, len(lefts)), grid_spec=p...  77.5 us
    dot_general x5, matrix products, times_rows(): lax.dot_general(left, right, ROWS_DIMS, preferred_element_type=jnp.float32)  67.1 us
    all_to_all x4, waiting for transfers between devices, swap_all(): got = lax.all_to_all(value, 'dp', 0, 0, tiled=True)  62.2 us
    pallas_call x2, Pallas kernels, row_call(): pl.pallas_call(kernel, grid=(count // ROW_STEP,), in_specs=[tile(width)]...  57.7 us
    unnamed x151, local copies, waits for them, and re-layouts  44.7 us
  transfers between devices with their start and end apart: 85, of which 33 were waited for; matrix products, arithmetic and copies ran while one was open for 24% of the time, Pallas kernels for 11%

profile of v5, /device:TPU:0, one launch (start us, length us, event | category | flops | bytes accessed | tf_op | source)
XLA Modules:
  0.0 1160.2 jit_solution(493222175678134557)
XLA Ops:
  42.4 5.8 all-to-all-start
  63.6 37.5 %collective-permute-done.12 = bf16[704,2048]{1,0:T(8,128)(2,1)} collective-permute-done((bf16[704,2048]{1,0:T(8,128)(2,1)}, bf16[704,2048]{1,0:T(8,128)(2,1)}, u32[]{:S(2)}, u32[]{:S(2)}) %collective-permute-start.12) | collective-permute-done | bytes 2883616 | tf_op jit(solution)/shard_map/ppermute | solution.py:890
  101.1 9.6 all-to-all-done
  120.1 22.5 %all-to-all-done.1 = bf16[8,128,512]{2,1,0:T(8,128)(2,1)} async-done(((bf16[8,128,512]{2,1,0:T(8,128)(2,1)}), bf16[8,128,512]{2,1,0:T(8,128)(2,1)}, u32[]{:S(2)}, u32[]{:S(2)}) %all-to-all-start.1) | async-done | bytes 1048608 | tf_op jit(solution)/shard_map/all_to_all | solution.py:914
  156.4 8.5 fusion.39.front
  174.3 25.8 %attend.1 = (bf16[2048,512]{1,0:T(8,128)(2,1)}, bf16[2048,512]{1,0:T(8,128)(2,1)}, bf16[2048,256]{1,0:T(8,128)(2,1)}, f32[16,1,512]{2,1,0:T(1,128)}) custom-call(f32[2048,768]{1,0:T(8,128)} %fusion.39.front, f32[2048,128]{1,0:T(8,128)} %get-tuple-element.438.cosine, f32[2048,128]{1,0:T(8,128)} %get-tuple-element.439.sine, f32[16,1,512]{2,1,0:T(1,128)} %bitcast.336), custom_call_target="tpu_custom_call" | custom-call | flops 4294967296 | bytes 12582912 | tf_op jit(solution)/shard_map/attend/pallas_call | solution.py:487
  203.6 8.5 all-to-all-done.2
  215.2 6.9 convolution_convert_fusion.1
  228.1 96.2 %all-to-all-done.3 = bf16[8,704,256]{2,1,0:T(8,128)(2,1)} async-done(((bf16[8,704,256]{2,1,0:T(8,128)(2,1)}), bf16[8,704,256]{2,1,0:T(8,128)(2,1)}, u32[]{:S(2)}, u32[]{:S(2)}) %all-to-all-start.3) | async-done | bytes 2883616 | tf_op jit(solution)/shard_map/all_to_all | solution.py:981
  328.2 32.8 %reduce-scatter.3.cloned.1.call-done = bf16[128,2048]{1,0:T(8,128)(2,1)} async-done(((bf16[2048,2048]{1,0:T(8,128)(2,1)}), bf16[128,2048]{1,0:T(8,128)(2,1)}) %reduce-scatter.3.cloned.1.call-update) | async-done | bytes 524304 | tf_op jit(solution)/shard_map/reduce_scatter | solution.py:858
  368.1 6.1 pad_maximum_fusion.refs_4_.down_w
  385.0 44.1 %collective-permute-done.18 = bf16[704,2048]{1,0:T(8,128)(2,1)} collective-permute-done((bf16[704,2048]{1,0:T(8,128)(2,1)}, bf16[704,2048]{1,0:T(8,128)(2,1)}, u32[]{:S(2)}, u32[]{:S(2)}) %collective-permute-start.18) | collective-permute-done | bytes 2883616 | tf_op jit(solution)/shard_map/ppermute | solution.py:890
  432.9 5.8 all-gather.7.cloned.1.call-done.rows
  438.8 34.1 %open_rows.1 = (bf16[2048,1408]{1,0:T(8,128)(2,1)}, bf16[2048,1408]{1,0:T(8,128)(2,1)}, bf16[2048,1408]{1,0:T(8,128)(2,1)}) custom-call(bf16[2048,2048]{1,0:T(8,128)(2,1)} %all-gather.7.cloned.1.call-done.rows, bf16[1408,2048]{1,0:T(8,128)(2,1)} %constant_dynamic-update-slice_fusion.2.gate_w.refs_8_, ...), custom_call_target="tpu_custom_call" | custom-call | flops 23622320128 | bytes 40370176 | tf_op jit(solution)/shard_map/open_rows/pallas_call | solution.py:782
  472.9 7.8 slot_product.8
  481.0 7.9 slot_product.9
  490.9 7.9 slot_product.10
  499.3 5.2 collective-permute-done.20
  511.8 7.9 slot_product.11
  536.5 6.5 collective-permute-done.27
  547.2 8.7 collective-permute-start.31
  575.5 73.1 %all-gather.9.cloned.1.call-done.rows = bf16[2048,2048]{1,0:T(8,128)(2,1)} async-done(((bf16[128,2048]{1,0:T(8,128)(2,1)}), bf16[2048,2048]{1,0:T(8,128)(2,1)}) %all-gather.9.cloned.1.call-update) | async-done | bytes 8388624 | tf_op jit(solution)/shard_map/all_gather | solution.py:855
  648.7 23.6 %close_rows.1 = (bf16[2048,1408]{1,0:T(8,128)(2,1)}, bf16[2048,1408]{1,0:T(8,128)(2,1)}) custom-call(bf16[2048,2048]{1,0:T(8,128)(2,1)} %all-gather.9.cloned.1.call-done.rows, bf16[1408,2048]{1,0:T(8,128)(2,1)} %pad_maximum_fusion.refs_4_.down_w, f32[2048,2]{1,0:T(8,128)} %copy.152.share, bf16[2048,1408]{1,0:T(8,128)(2,1)} %get-tuple-element.223.gate_in, ...), custom_call_target="tpu_custom_call" | custom-call | flops 11811160064 | bytes 34603008 | tf_op jit(solution)/shard_map/close_rows/pallas_call | solution.py:782
  672.2 11.5 slot_product.12
  684.1 11.5 slot_product.13
  697.6 11.5 slot_product.14
  717.9 11.5 slot_product.15
  736.8 8.1 collective-permute-done.46
  749.6 7.3 collective-permute-start.51
  758.4 14.8 %fusion.40 = f32[1408,2048]{1,0:T(8,128)S(1)} fusion(bf16[2048,1408]{1,0:T(8,128)(2,1)S(1)} %bitcast.278, bf16[2048,2048]{1,0:T(8,128)(2,1)} %all-gather.7.cloned.1.call-done.rows), kind=kOutput, calls=%fused_computation.239 | convolution fusion | flops 11811160064 | bytes 25690112 | tf_op jit(solution)/shard_map/dot_general | solution.py:47
  783.9 17.1 %fusion.42 = f32[1408,2048]{1,0:T(8,128)S(1)} fusion(bf16[2048,1408]{1,0:T(8,128)(2,1)} %get-tuple-element.277.refs_4_.refs_5_.refs_6_.refs_7_, bf16[2048,2048]{1,0:T(8,128)(2,1)} %all-gather.7.cloned.1.call-done.rows), kind=kOutput, calls=%fused_computation.241 | convolution fusion | flops 11811160064 | bytes 25690112 | tf_op jit(solution)/shard_map/dot_general | solution.py:47
  805.9 14.8 %fusion.43 = f32[1408,2048]{1,0:T(8,128)S(1)} fusion(bf16[2048,1408]{1,0:T(8,128)(2,1)S(1)} %bitcast.280, bf16[2048,2048]{1,0:T(8,128)(2,1)} %all-gather.9.cloned.1.call-done.rows), kind=kOutput, calls=%fused_computation.242 | convolution fusion | flops 11811160064 | bytes 25690112 | tf_op jit(solution)/shard_map/dot_general | solution.py:47
  824.4 21.5 %collective-permute-done.53 = bf16[704,2048]{1,0:T(8,128)(2,1)S(1)} collective-permute-done((bf16[704,2048]{1,0:T(8,128)(2,1)}, bf16[704,2048]{1,0:T(8,128)(2,1)S(1)}, u32[]{:S(2)}, u32[]{:S(2)}) %collective-permute-start.53) | collective-permute-done | bytes 2883616 | tf_op jit(solution)/shard_map/ppermute | solution.py:890
  859.0 10.5 fusion.41.pull
  869.5 38.1 %attend_back.1 = bf16[2048,768]{1,0:T(8,128)(2,1)} custom-call(f32[2048,512]{1,0:T(8,128)} %fusion.41.pull, f32[2048,4]{1,0:T(8,128)} %get-tuple-element.389.gate, bf16[2048,512]{1,0:T(8,128)(2,1)} %get-tuple-element.272.query_in, bf16[2048,256]{1,0:T(8,128)(2,1)} %get-tuple-element.273.pair, bf16[128,2048]{1,0:T(8,128)(2,1)} %slice_bitcast_fusion.pair_up, ...), custom_call_target="tpu_custom_call" | custom-call | flops 10737418240 | bytes 12582912 | tf_op jit(solution)/shard_map/attend_back/pallas_call | solution.py:605
  907.6 9.3 all-to-all-done.4
  916.9 11.6 convolution_convert_fusion
  939.3 11.0 convolution_convert_fusion.2
  952.0 9.4 fusion.44
  961.4 9.7 collective-permute-done.55
  974.0 16.4 %collective-permute-start.57 = (bf16[352,2048]{1,0:T(8,128)(2,1)}, bf16[352,2048]{1,0:T(8,128)(2,1)}, u32[]{:S(2)}, u32[]{:S(2)}) collective-permute-start(bf16[352,2048]{1,0:T(8,128)(2,1)} %slice.156), channel_id=1, source_target_pairs={{0,2},{2,0},{1,3},{3,1},{4,6},{6,4},{5,7},{7,5},{8,10},{10,8},{9,1... | collective-permute-start | bytes 4325384 | tf_op jit(solution)/shard_map/ppermute | solution.py:890
  996.1 29.3 %collective-permute-done.37 = bf16[128,512]{1,0:T(8,128)(2,1)S(1)} collective-permute-done((bf16[128,512]{1,0:T(8,128)(2,1)S(1)}, bf16[128,512]{1,0:T(8,128)(2,1)S(1)}, u32[]{:S(2)}, u32[]{:S(2)}) %collective-permute-start.37) | collective-permute-done | bytes 131104 | tf_op jit(solution)/shard_map/ppermute | solution.py:842
  1042.1 4.8 convert_bitcast_fusion.1
  1046.9 6.3 copy.170
  1057.3 5.6 collective-permute-start.60
  1067.8 6.3 copy.171
  1074.1 21.5 %all-to-all-done.6 = bf16[8,128,768]{2,1,0:T(8,128)(2,1)} async-done(((bf16[8,128,768]{2,1,0:T(8,128)(2,1)}), bf16[8,128,768]{2,1,0:T(8,128)(2,1)}, u32[]{:S(2)}, u32[]{:S(2)}) %all-to-all-start.6) | async-done | bytes 1572896 | tf_op jit(solution)/shard_map/all_to_all | solution.py:914
  1136.0 6.9 add_bitcast_fusion
  (459 shorter events, 321.5 us)
Async XLA Ops:
  7.3 135.3 %all-gather.5.cloned.1.call-start = ((), (), s32[]{:S(2)}) async-start(), calls=%async_computation.10 | async-start | bytes 8912896 | tf_op jit(solution)/shard_map/all_gather | solution.py:855
  36.8 64.3 %collective-permute-start.12 = (bf16[704,2048]{1,0:T(8,128)(2,1)}, bf16[704,2048]{1,0:T(8,128)(2,1)}, u32[]{:S(2)}, u32[]{:S(2)}) collective-permute-start(bf16[704,2048]{1,0:T(8,128)(2,1)} %bitcast.302), channel_id=1, source_target_pairs={{0,2},{2,0},{1,3},{3,1},{4,6},{6,4},{5,7},{7,5},{8,10},{10,8},{9,1... | collective-permute-start | bytes 8650760 | tf_op jit(solution)/shard_map/ppermute | solution.py:890
  42.4 68.3 %all-to-all-start = ((bf16[8,128,768]{2,1,0:T(8,128)(2,1)}), bf16[8,128,768]{2,1,0:T(8,128)(2,1)S(1)}, u32[]{:S(2)}, u32[]{:S(2)}) async-start(bf16[8,128,768]{2,1,0:T(8,128)(2,1)} %pad_maximum_fusion.3), calls=%async_computation | async-start | bytes 3145728 | tf_op jit(solution)/shard_map/all_to_all | solution.py:914
  110.7 31.9 %all-to-all-start.1 = ((bf16[8,128,512]{2,1,0:T(8,128)(2,1)}), bf16[8,128,512]{2,1,0:T(8,128)(2,1)}, u32[]{:S(2)}, u32[]{:S(2)}) async-start(bf16[8,128,512]{2,1,0:T(8,128)(2,1)} %pad_maximum_fusion.4), calls=%async_computation.1 | async-start | bytes 2097152 | tf_op jit(solution)/shard_map/all_to_all | solution.py:914
  115.0 36.0 %collective-permute-start.14 = (bf16[8,128,768]{2,1,0:T(8,128)(2,1)S(1)}, bf16[8,128,768]{2,1,0:T(8,128)(2,1)}, u32[]{:S(2)}, u32[]{:S(2)}) collective-permute-start(bf16[8,128,768]{2,1,0:T(8,128)(2,1)S(1)} %all-to-all-done), channel_id=1, source_target_pairs={{0,2},{1,0},{2,3},{3,1},{4,6},{5,4},{6,7},{7,5},{8,10},{9,8},{10,1... | collective-permute-start | bytes 4718600 | tf_op jit(solution)/shard_map/ppermute | solution.py:908
  116.7 34.4 %collective-permute-start.13 = (bf16[8,128,768]{2,1,0:T(8,128)(2,1)S(1)}, bf16[8,128,768]{2,1,0:T(8,128)(2,1)}, u32[]{:S(2)}, u32[]{:S(2)}) collective-permute-start(bf16[8,128,768]{2,1,0:T(8,128)(2,1)S(1)} %all-to-all-done), channel_id=1, source_target_pairs={{1,2},{2,1},{5,6},{6,5},{9,10},{10,9},{13,14},{14,13},{17,18},{18,... | collective-permute-start | bytes 4718600 | tf_op jit(solution)/shard_map/ppermute | solution.py:907
  142.6 69.5 %all-to-all-start.2 = ((bf16[8,704,256]{2,1,0:T(8,128)(2,1)}), bf16[8,704,256]{2,1,0:T(8,128)(2,1)}, u32[]{:S(2)}, u32[]{:S(2)}) async-start(bf16[8,704,256]{2,1,0:T(8,128)(2,1)} %bitcast.283), calls=%async_computation.2 | async-start | bytes 5767168 | tf_op jit(solution)/shard_map/all_to_all | solution.py:914
  147.0 214.0 %reduce-scatter.3.cloned.1.call-start = ((), (), s32[]{:S(2)}) async-start(), calls=%async_computation.11 | async-start | bytes 8912896 | tf_op jit(solution)/shard_map/reduce_scatter | solution.py:858
  164.9 35.1 %collective-permute-start.16 = (bf16[8,128,512]{2,1,0:T(8,128)(2,1)}, bf16[8,128,512]{2,1,0:T(8,128)(2,1)}, u32[]{:S(2)}, u32[]{:S(2)}) collective-permute-start(bf16[8,128,512]{2,1,0:T(8,128)(2,1)} %all-to-all-done.1), channel_id=1, source_target_pairs={{0,2},{1,0},{2,3},{3,1},{4,6},{5,4},{6,7},{7,5},{8,10},{9,8},{10,1... | collective-permute-start | bytes 3145736 | tf_op jit(solution)/shard_map/ppermute | solution.py:908
  168.4 31.7 %collective-permute-start.15 = (bf16[8,128,512]{2,1,0:T(8,128)(2,1)}, bf16[8,128,512]{2,1,0:T(8,128)(2,1)}, u32[]{:S(2)}, u32[]{:S(2)}) collective-permute-start(bf16[8,128,512]{2,1,0:T(8,128)(2,1)} %all-to-all-done.1), channel_id=1, source_target_pairs={{1,2},{2,1},{5,6},{6,5},{9,10},{10,9},{13,14},{14,13},{17,18},{18,... | collective-permute-start | bytes 3145736 | tf_op jit(solution)/shard_map/ppermute | solution.py:907
  222.1 102.2 %all-to-all-start.3 = ((bf16[8,704,256]{2,1,0:T(8,128)(2,1)}), bf16[8,704,256]{2,1,0:T(8,128)(2,1)}, u32[]{:S(2)}, u32[]{:S(2)}) async-start(bf16[8,704,256]{2,1,0:T(8,128)(2,1)} %bitcast.34), calls=%async_computation.4 | async-start | bytes 5767168 | tf_op jit(solution)/shard_map/all_to_all | solution.py:981
  226.6 212.2 %all-gather.7.cloned.1.call-start = ((), (), s32[]{:S(2)}) async-start(), calls=%async_computation.12 | async-start | bytes 8912896 | tf_op jit(solution)/shard_map/all_gather | solution.py:855
  226.6 135.6 %collective-permute-start.17 = (bf16[704,2048]{1,0:T(8,128)(2,1)S(1)}, bf16[704,2048]{1,0:T(8,128)(2,1)}, u32[]{:S(2)}, u32[]{:S(2)}) collective-permute-start(bf16[704,2048]{1,0:T(8,128)(2,1)S(1)} %bitcast.284), channel_id=1, source_target_pairs={{0,2},{2,0},{1,3},{3,1},{4,6},{6,4},{5,7},{7,5},{8,10},{10,8},{9,1... | collective-permute-start | bytes 8650760 | tf_op jit(solution)/shard_map/ppermute | solution.py:890
  364.0 284.7 %all-gather.9.cloned.1.call-start = ((), (), s32[]{:S(2)}) async-start(), calls=%async_computation.13 | async-start | bytes 8912896 | tf_op jit(solution)/shard_map/all_gather | solution.py:855
  364.5 64.6 %collective-permute-start.18 = (bf16[704,2048]{1,0:T(8,128)(2,1)}, bf16[704,2048]{1,0:T(8,128)(2,1)}, u32[]{:S(2)}, u32[]{:S(2)}) collective-permute-start(bf16[704,2048]{1,0:T(8,128)(2,1)} %bitcast.287), channel_id=1, source_target_pairs={{0,2},{2,0},{1,3},{3,1},{4,6},{6,4},{5,7},{7,5},{8,10},{10,8},{9,1... | collective-permute-start | bytes 8650760 | tf_op jit(solution)/shard_map/ppermute | solution.py:890
  505.3 14.4 %collective-permute-start.25 = (bf16[256,2048]{1,0:T(8,128)(2,1)}, bf16[256,2048]{1,0:T(8,128)(2,1)}, u32[]{:S(2)}, u32[]{:S(2)}) collective-permute-start(bf16[256,2048]{1,0:T(8,128)(2,1)} %get-tuple-element.201), channel_id=1, source_target_pairs={{0,1},{1,0},{2,3},{3,2},{4,5},{5,4},{6,7},{7,6},{8,9},{9,8},{10,11... | collective-permute-start | bytes 3145736 | tf_op jit(solution)/shard_map/ppermute | solution.py:653
  505.3 16.2 %collective-permute-start.22 = (bf16[128,2048]{1,0:T(8,128)(2,1)}, bf16[128,2048]{1,0:T(8,128)(2,1)S(1)}, u32[]{:S(2)}, u32[]{:S(2)}) collective-permute-start(bf16[128,2048]{1,0:T(8,128)(2,1)} %slice.133), channel_id=1, source_target_pairs={{0,4},{4,0},{8,12},{12,8},{16,20},{20,16},{24,28},{28,24},{1,5},{5... | collective-permute-start | bytes 1572872 | tf_op jit(solution)/shard_map/ppermute | solution.py:649
  506.8 14.7 %collective-permute-start.23 = (bf16[128,2048]{1,0:T(8,128)(2,1)}, bf16[128,2048]{1,0:T(8,128)(2,1)}, u32[]{:S(2)}, u32[]{:S(2)}) collective-permute-start(bf16[128,2048]{1,0:T(8,128)(2,1)} %fusion.11), channel_id=1, source_target_pairs={{0,8},{4,12},{1,9},{5,13},{2,10},{6,14},{3,11},{7,15}} | collective-permute-start | bytes 1572872 | tf_op jit(solution)/shard_map/ppermute | solution.py:662
  526.6 16.4 %collective-permute-start.27 = (bf16[128,2048]{1,0:T(8,128)(2,1)}, bf16[128,2048]{1,0:T(8,128)(2,1)S(1)}, u32[]{:S(2)}, u32[]{:S(2)}) collective-permute-start(bf16[128,2048]{1,0:T(8,128)(2,1)} %get-tuple-element.368), channel_id=1, source_target_pairs={{0,8},{4,12},{8,16},{12,20},{1,9},{5,13},{9,17},{13,21},{2,10},{6,... | collective-permute-start | bytes 1572872 | tf_op jit(solution)/shard_map/ppermute | solution.py:662
  543.9 22.4 %collective-permute-start.30 = (bf16[128,2048]{1,0:T(8,128)(2,1)}, bf16[128,2048]{1,0:T(8,128)(2,1)}, u32[]{:S(2)}, u32[]{:S(2)}) collective-permute-start(bf16[128,2048]{1,0:T(8,128)(2,1)} %slice.139), channel_id=1, source_target_pairs={{0,4},{4,0},{8,12},{12,8},{16,20},{20,16},{24,28},{28,24},{1,5},{5... | collective-permute-start | bytes 1572872 | tf_op jit(solution)/shard_map/ppermute | solution.py:649
  547.2 19.4 %collective-permute-start.31 = (bf16[128,2048]{1,0:T(8,128)(2,1)}, bf16[128,2048]{1,0:T(8,128)(2,1)S(1)}, u32[]{:S(2)}, u32[]{:S(2)}) collective-permute-start(bf16[128,2048]{1,0:T(8,128)(2,1)} %get-tuple-element.366), channel_id=1, source_target_pairs={{0,8},{4,12},{8,16},{12,20},{16,24},{20,28},{1,9},{5,13},{9,17},{1... | collective-permute-start | bytes 1572872 | tf_op jit(solution)/shard_map/ppermute | solution.py:662
  555.9 14.6 %collective-permute-start.32 = (bf16[128,2048]{1,0:T(8,128)(2,1)S(1)}, bf16[128,2048]{1,0:T(8,128)(2,1)S(1)}, u32[]{:S(2)}, u32[]{:S(2)}) collective-permute-start(bf16[128,2048]{1,0:T(8,128)(2,1)S(1)} %get-tuple-element.365), channel_id=1, source_target_pairs={{24,16},{28,20},{16,8},{20,12},{8,0},{12,4},{25,17},{29,21},{17,9}... | collective-permute-start | bytes 1572872 | tf_op jit(solution)/shard_map/ppermute | solution.py:665
  575.5 283.5 %all-gather.11.cloned.1.call-start = ((), (), s32[]{:S(2)}) async-start(), calls=%async_computation.14 | async-start | bytes 8912896 | tf_op jit(solution)/shard_map/all_gather | solution.py:855
  712.0 17.4 %collective-permute-start.45 = (bf16[256,2048]{1,0:T(8,128)(2,1)}, bf16[256,2048]{1,0:T(8,128)(2,1)S(1)}, u32[]{:S(2)}, u32[]{:S(2)}) collective-permute-start(bf16[256,2048]{1,0:T(8,128)(2,1)} %get-tuple-element.248), channel_id=1, source_target_pairs={{0,1},{1,0},{2,3},{3,2},{4,5},{5,4},{6,7},{7,6},{8,9},{9,8},{10,11... | collective-permute-start | bytes 3145736 | tf_op jit(solution)/shard_map/ppermute | solution.py:653
  712.9 18.7 %collective-permute-start.43 = (bf16[128,2048]{1,0:T(8,128)(2,1)}, bf16[128,2048]{1,0:T(8,128)(2,1)S(1)}, u32[]{:S(2)}, u32[]{:S(2)}) collective-permute-start(bf16[128,2048]{1,0:T(8,128)(2,1)} %fusion.12), channel_id=1, source_target_pairs={{0,8},{4,12},{1,9},{5,13},{2,10},{6,14},{3,11},{7,15}} | collective-permute-start | bytes 1572872 | tf_op jit(solution)/shard_map/ppermute | solution.py:662
  715.8 15.7 %collective-permute-start.44 = (bf16[128,2048]{1,0:T(8,128)(2,1)}, bf16[128,2048]{1,0:T(8,128)(2,1)}, u32[]{:S(2)}, u32[]{:S(2)}) collective-permute-start(bf16[128,2048]{1,0:T(8,128)(2,1)} %fusion.12), channel_id=1, source_target_pairs={{24,16},{28,20},{25,17},{29,21},{26,18},{30,22},{27,19},{31,23}} | collective-permute-start | bytes 1572872 | tf_op jit(solution)/shard_map/ppermute | solution.py:665
  747.5 32.1 %collective-permute-start.50 = (bf16[128,2048]{1,0:T(8,128)(2,1)S(1)}, bf16[128,2048]{1,0:T(8,128)(2,1)S(1)}, u32[]{:S(2)}, u32[]{:S(2)}) collective-permute-start(bf16[128,2048]{1,0:T(8,128)(2,1)S(1)} %slice.147), channel_id=1, source_target_pairs={{0,4},{4,0},{8,12},{12,8},{16,20},{20,16},{24,28},{28,24},{1,5},{5... | collective-permute-start | bytes 1572872 | tf_op jit(solution)/shard_map/ppermute | solution.py:649
  749.6 30.0 %collective-permute-start.51 = (bf16[128,2048]{1,0:T(8,128)(2,1)S(1)}, bf16[128,2048]{1,0:T(8,128)(2,1)S(1)}, u32[]{:S(2)}, u32[]{:S(2)}) collective-permute-start(bf16[128,2048]{1,0:T(8,128)(2,1)S(1)} %get-tuple-element.362), channel_id=1, source_target_pairs={{0,8},{4,12},{8,16},{12,20},{16,24},{20,28},{1,9},{5,13},{9,17},{1... | collective-permute-start | bytes 1572872 | tf_op jit(solution)/shard_map/ppermute | solution.py:662
  756.9 22.7 %collective-permute-start.52 = (bf16[128,2048]{1,0:T(8,128)(2,1)S(1)}, bf16[128,2048]{1,0:T(8,128)(2,1)S(1)}, u32[]{:S(2)}, u32[]{:S(2)}) collective-permute-start(bf16[128,2048]{1,0:T(8,128)(2,1)S(1)} %get-tuple-element.361), channel_id=1, source_target_pairs={{24,16},{28,20},{16,8},{20,12},{8,0},{12,4},{25,17},{29,21},{17,9}... | collective-permute-start | bytes 1572872 | tf_op jit(solution)/shard_map/ppermute | solution.py:665
  782.4 63.5 %collective-permute-start.53 = (bf16[704,2048]{1,0:T(8,128)(2,1)}, bf16[704,2048]{1,0:T(8,128)(2,1)S(1)}, u32[]{:S(2)}, u32[]{:S(2)}) collective-permute-start(bf16[704,2048]{1,0:T(8,128)(2,1)} %slice.212), channel_id=1, source_target_pairs={{0,2},{2,0},{1,3},{3,1},{4,6},{6,4},{5,7},{7,5},{8,10},{10,8},{9,1... | collective-permute-start | bytes 8650760 | tf_op jit(solution)/shard_map/ppermute | solution.py:890
  848.8 68.1 %all-to-all-start.4 = ((bf16[8,704,256]{2,1,0:T(8,128)(2,1)}), bf16[8,704,256]{2,1,0:T(8,128)(2,1)}, u32[]{:S(2)}, u32[]{:S(2)}) async-start(bf16[8,704,256]{2,1,0:T(8,128)(2,1)} %bitcast.289), calls=%async_computation.5 | async-start | bytes 5767168 | tf_op jit(solution)/shard_map/all_to_all | solution.py:1044
  853.3 244.4 %reduce-scatter.5.cloned.1.call-start = ((), (), s32[]{:S(2)}) async-start(), calls=%async_computation.15 | async-start | bytes 8912896 | tf_op jit(solution)/shard_map/reduce_scatter | solution.py:858
  857.5 71.0 %collective-permute-start.56 = (bf16[704,2048]{1,0:T(8,128)(2,1)}, bf16[704,2048]{1,0:T(8,128)(2,1)}, u32[]{:S(2)}, u32[]{:S(2)}) collective-permute-start(bf16[704,2048]{1,0:T(8,128)(2,1)} %slice.211), channel_id=1, source_target_pairs={{0,2},{2,0},{1,3},{3,1},{4,6},{6,4},{5,7},{7,5},{8,10},{10,8},{9,1... | collective-permute-start | bytes 8650760 | tf_op jit(solution)/shard_map/ppermute | solution.py:890
  934.9 102.7 %all-to-all-start.5 = ((bf16[8,704,256]{2,1,0:T(8,128)(2,1)}), bf16[8,704,256]{2,1,0:T(8,128)(2,1)}, u32[]{:S(2)}, u32[]{:S(2)}) async-start(bf16[8,704,256]{2,1,0:T(8,128)(2,1)} %bitcast.286), calls=%async_computation.6 | async-start | bytes 5767168 | tf_op jit(solution)/shard_map/all_to_all | solution.py:1059
  950.6 20.4 %collective-permute-start.55 = (bf16[8,128,768]{2,1,0:T(8,128)(2,1)S(1)}, bf16[8,128,768]{2,1,0:T(8,128)(2,1)S(1)}, u32[]{:S(2)}, u32[]{:S(2)}) collective-permute-start(bf16[8,128,768]{2,1,0:T(8,128)(2,1)S(1)} %get-tuple-element.360), channel_id=1, source_target_pairs={{2,0},{0,1},{3,2},{1,3},{6,4},{4,5},{7,6},{5,7},{10,8},{8,9},{11,1... | collective-permute-start | bytes 4718600 | tf_op jit(solution)/shard_map/ppermute | solution.py:1071
  950.7 20.4 %collective-permute-start.54 = (bf16[8,128,768]{2,1,0:T(8,128)(2,1)S(1)}, bf16[8,128,768]{2,1,0:T(8,128)(2,1)S(1)}, u32[]{:S(2)}, u32[]{:S(2)}) collective-permute-start(bf16[8,128,768]{2,1,0:T(8,128)(2,1)S(1)} %get-tuple-element.359), channel_id=1, source_target_pairs={{1,2},{2,1},{5,6},{6,5},{9,10},{10,9},{13,14},{14,13},{17,18},{18,... | collective-permute-start | bytes 4718600 | tf_op jit(solution)/shard_map/ppermute | solution.py:1070
  974.0 63.5 %collective-permute-start.57 = (bf16[352,2048]{1,0:T(8,128)(2,1)}, bf16[352,2048]{1,0:T(8,128)(2,1)}, u32[]{:S(2)}, u32[]{:S(2)}) collective-permute-start(bf16[352,2048]{1,0:T(8,128)(2,1)} %slice.156), channel_id=1, source_target_pairs={{0,2},{2,0},{1,3},{3,1},{4,6},{6,4},{5,7},{7,5},{8,10},{10,8},{9,1... | collective-permute-start | bytes 4325384 | tf_op jit(solution)/shard_map/ppermute | solution.py:890
  993.0 32.4 %collective-permute-start.37 = (bf16[128,512]{1,0:T(8,128)(2,1)S(1)}, bf16[128,512]{1,0:T(8,128)(2,1)S(1)}, u32[]{:S(2)}, u32[]{:S(2)}) collective-permute-start(bf16[128,512]{1,0:T(8,128)(2,1)S(1)} %bitcast.331), channel_id=1, source_target_pairs={{0,2},{1,3},{2,0},{3,1},{4,6},{5,7},{6,4},{7,5},{8,10},{9,11},{10,... | collective-permute-start | bytes 393224 | tf_op jit(solution)/shard_map/ppermute | solution.py:842
  993.1 35.6 %collective-permute-start.38 = (bf16[128,512]{1,0:T(8,128)(2,1)S(1)}, bf16[128,512]{1,0:T(8,128)(2,1)S(1)}, u32[]{:S(2)}, u32[]{:S(2)}) collective-permute-start(bf16[128,512]{1,0:T(8,128)(2,1)S(1)} %bitcast.332), channel_id=1, source_target_pairs={{0,3},{1,2},{2,1},{3,0},{4,7},{5,6},{6,5},{7,4},{8,11},{9,10},{10,... | collective-permute-start | bytes 393224 | tf_op jit(solution)/shard_map/ppermute | solution.py:842
  995.2 33.5 %collective-permute-start.36 = (bf16[128,512]{1,0:T(8,128)(2,1)S(1)}, bf16[128,512]{1,0:T(8,128)(2,1)S(1)}, u32[]{:S(2)}, u32[]{:S(2)}) collective-permute-start(bf16[128,512]{1,0:T(8,128)(2,1)S(1)} %bitcast.333), channel_id=1, source_target_pairs={{0,1},{1,0},{2,3},{3,2},{4,5},{5,4},{6,7},{7,6},{8,9},{9,8},{10,11... | collective-permute-start | bytes 393224 | tf_op jit(solution)/shard_map/ppermute | solution.py:842
  1031.2 22.0 %collective-permute-start.59 = (bf16[8,128,512]{2,1,0:T(8,128)(2,1)}, bf16[8,128,512]{2,1,0:T(8,128)(2,1)}, u32[]{:S(2)}, u32[]{:S(2)}) collective-permute-start(bf16[8,128,512]{2,1,0:T(8,128)(2,1)} %get-tuple-element.376), channel_id=1, source_target_pairs={{2,0},{0,1},{3,2},{1,3},{6,4},{4,5},{7,6},{5,7},{10,8},{8,9},{11,1... | collective-permute-start | bytes 3145736 | tf_op jit(solution)/shard_map/ppermute | solution.py:1071
  1031.2 22.0 %collective-permute-start.58 = (bf16[8,128,512]{2,1,0:T(8,128)(2,1)}, bf16[8,128,512]{2,1,0:T(8,128)(2,1)}, u32[]{:S(2)}, u32[]{:S(2)}) collective-permute-start(bf16[8,128,512]{2,1,0:T(8,128)(2,1)} %get-tuple-element.375), channel_id=1, source_target_pairs={{1,2},{2,1},{5,6},{6,5},{9,10},{10,9},{13,14},{14,13},{17,18},{18,... | collective-permute-start | bytes 3145736 | tf_op jit(solution)/shard_map/ppermute | solution.py:1070
  1037.6 58.0 %all-to-all-start.6 = ((bf16[8,128,768]{2,1,0:T(8,128)(2,1)}), bf16[8,128,768]{2,1,0:T(8,128)(2,1)}, u32[]{:S(2)}, u32[]{:S(2)}) async-start(bf16[8,128,768]{2,1,0:T(8,128)(2,1)} %add_convert_fusion.2), calls=%async_computation.7 | async-start | bytes 3145728 | tf_op jit(solution)/shard_map/all_to_all | solution.py:914
  1057.3 44.3 %collective-permute-start.60 = (bf16[352,2048]{1,0:T(8,128)(2,1)}, bf16[352,2048]{1,0:T(8,128)(2,1)S(1)}, u32[]{:S(2)}, u32[]{:S(2)}) collective-permute-start(bf16[352,2048]{1,0:T(8,128)(2,1)} %slice.157), channel_id=1, source_target_pairs={{0,2},{2,0},{1,3},{3,1},{4,6},{6,4},{5,7},{7,5},{8,10},{10,8},{9,1... | collective-permute-start | bytes 4325384 | tf_op jit(solution)/shard_map/ppermute | solution.py:890
  1101.6 33.1 %all-to-all-start.7 = ((bf16[8,128,512]{2,1,0:T(8,128)(2,1)}), bf16[8,128,512]{2,1,0:T(8,128)(2,1)}, u32[]{:S(2)}, u32[]{:S(2)}) async-start(bf16[8,128,512]{2,1,0:T(8,128)(2,1)} %add_convert_fusion.3), calls=%async_computation.9 | async-start | bytes 2097152 | tf_op jit(solution)/shard_map/all_to_all | solution.py:1100
  1128.8 16.7 %collective-permute-start.67 = (f32[128,512]{1,0:T(8,128)S(1)}, f32[128,512]{1,0:T(8,128)}, u32[]{:S(2)}, u32[]{:S(2)}) collective-permute-start(f32[128,512]{1,0:T(8,128)S(1)} %bitcast.317), channel_id=1, source_target_pairs={{0,2},{1,3},{2,0},{3,1},{4,6},{5,7},{6,4},{7,5},{8,10},{9,11},{10,... | collective-permute-start | bytes 786440 | tf_op jit(solution)/shard_map/ppermute | solution.py:842
  1131.0 14.4 %collective-permute-start.68 = (f32[128,512]{1,0:T(8,128)}, f32[128,512]{1,0:T(8,128)}, u32[]{:S(2)}, u32[]{:S(2)}) collective-permute-start(f32[128,512]{1,0:T(8,128)} %bitcast.271), channel_id=1, source_target_pairs={{0,3},{1,2},{2,1},{3,0},{4,7},{5,6},{6,5},{7,4},{8,11},{9,10},{10,... | collective-permute-start | bytes 786440 | tf_op jit(solution)/shard_map/ppermute | solution.py:842
  1131.0 14.4 %collective-permute-start.66 = (f32[128,512]{1,0:T(8,128)S(1)}, f32[128,512]{1,0:T(8,128)S(1)}, u32[]{:S(2)}, u32[]{:S(2)}) collective-permute-start(f32[128,512]{1,0:T(8,128)S(1)} %bitcast.318), channel_id=1, source_target_pairs={{0,1},{1,0},{2,3},{3,2},{4,5},{5,4},{6,7},{7,6},{8,9},{9,8},{10,11... | collective-permute-start | bytes 786440 | tf_op jit(solution)/shard_map/ppermute | solution.py:842
  (106 other events, 1916.7 us)
Sparse Core Ops, SparseCore 0:
  20.3 104.5 all-gather.4
  222.2 138.7 reduce-scatter.2
  364.1 74.6 all-gather.6
  575.6 73.0 all-gather.8
  782.5 74.2 all-gather.10
  928.6 164.8 reduce-scatter.4

commit v6 on v5

--- a/solution.py
+++ b/solution.py
@@ -1082,7 +1082,7 @@
         rows = jnp.concatenate(
             [jnp.where(core == 0, own, swapped), jnp.where(core == 0, swapped, own)], axis=1
         )
-        return rows.astype(jnp.float32)
+        return rows
 
     middle = hidden // 2
     front_heads = undeal_heads(front_grad)
@@ -1105,6 +1105,14 @@
     grad_out = out_back.reshape(local_heads, depth, expert_count, HEAD).transpose(2, 0, 3, 1)
     grad_query_out = front_out[:, :, :wide].reshape(local_heads, depth, expert_count, HEAD).transpose(2, 1, 0, 3)
     grad_pair = front_out[:, :, wide:].reshape(local_heads, depth, 2, HEAD).transpose(1, 2, 0, 3)
+    grad_out, grad_query_out, grad_pair = (
+        hold(value)[0].astype(jnp.float32)
+        for value in (
+            grad_out.reshape(w_out.shape),
+            grad_query_out.reshape(w_query.shape),
+            grad_pair.reshape(w_keyval.shape),
+        )
+    )
     totals = jnp.stack([grad_gain1, grad_gain2, jnp.full((width,), squared)])
     for axis, size in (("c", 2), ("y", 2), ("dp", units)):
         reach = 1

time: 1170 us -> 1160 us (level)
    unnamed x151 -> x143, local copies, waits for them, and re-layouts: 44.7 us -> 42.1 us
  transfers between devices with their start and end apart: 85 -> 85, of which waited for: 33 -> 33; matrix products, arithmetic and copies ran while one was open for 24% -> 23% of each run, Pallas kernels for 11% -> 11%
where the time goes in v6:
time: 1160 us
  waiting for transfers between devices  476 us (41%)
  Pallas kernels  199 us (17%)
  starting transfers between devices  157 us (14%)
  local copies, waits for them, and re-layouts  111 us (10%)
  matrix products  105 us (9%)
  other arithmetic  87.6 us (8%)
  between operations  19.5 us (2%)
    ppermute x7, waiting for transfers between devices, across(): return lax.ppermute(value, 'y', swap_pairs(2))  103 us
    all_to_all x2, waiting for transfers between devices, team_device(): up_slabs = lax.all_to_all(up_slabs, 'dp', 0, 0, tiled=True)  101 us
    all_gather x4, waiting for transfers between devices, collect(): return lax.all_gather(value, TEAM, axis=0, tiled=True)  78.9 us
    pallas_call x8, Pallas kernels, slot_product(): pl.pallas_call(functools.partial(product_kernel, len(lefts)), grid_spec=p...  77.5 us
    dot_general x5, matrix products, times_rows(): lax.dot_general(left, right, ROWS_DIMS, preferred_element_type=jnp.float32)  67.1 us
    all_to_all x4, waiting for transfers between devices, swap_all(): got = lax.all_to_all(value, 'dp', 0, 0, tiled=True)  62.3 us
    pallas_call x2, Pallas kernels, row_call(): pl.pallas_call(kernel, grid=(count // ROW_STEP,), in_specs=[tile(width)]...  57.7 us
    ppermute x12, waiting for transfers between devices, exchange(): got.append(lax.ppermute(part, QUAD, [(p, p ^ step) for p in range(4)]))  43.1 us
  transfers between devices with their start and end apart: 85, of which 33 were waited for; matrix products, arithmetic and copies ran while one was open for 23% of the time, Pallas kernels for 11%

profile of v6, /device:TPU:0, one launch (start us, length us, event | category | flops | bytes accessed | tf_op | source)
XLA Modules:
  0.0 1155.0 jit_solution(6963581480471413449)
XLA Ops:
  42.4 5.8 all-to-all-start
  63.7 37.4 %collective-permute-done.12 = bf16[704,2048]{1,0:T(8,128)(2,1)} collective-permute-done((bf16[704,2048]{1,0:T(8,128)(2,1)}, bf16[704,2048]{1,0:T(8,128)(2,1)}, u32[]{:S(2)}, u32[]{:S(2)}) %collective-permute-start.12) | collective-permute-done | bytes 2883616 | tf_op jit(solution)/shard_map/ppermute | solution.py:890
  101.1 9.7 all-to-all-done
  120.1 22.5 %all-to-all-done.1 = bf16[8,128,512]{2,1,0:T(8,128)(2,1)} async-done(((bf16[8,128,512]{2,1,0:T(8,128)(2,1)}), bf16[8,128,512]{2,1,0:T(8,128)(2,1)}, u32[]{:S(2)}, u32[]{:S(2)}) %all-to-all-start.1) | async-done | bytes 1048608 | tf_op jit(solution)/shard_map/all_to_all | solution.py:914
  156.4 8.5 fusion.40.front
  174.3 25.8 %attend.1 = (bf16[2048,512]{1,0:T(8,128)(2,1)}, bf16[2048,512]{1,0:T(8,128)(2,1)}, bf16[2048,256]{1,0:T(8,128)(2,1)}, f32[16,1,512]{2,1,0:T(1,128)}) custom-call(f32[2048,768]{1,0:T(8,128)} %fusion.40.front, f32[2048,128]{1,0:T(8,128)} %get-tuple-element.438.cosine, f32[2048,128]{1,0:T(8,128)} %get-tuple-element.439.sine, f32[16,1,512]{2,1,0:T(1,128)} %bitcast.335), custom_call_target="tpu_custom_call" | custom-call | flops 4294967296 | bytes 12582912 | tf_op jit(solution)/shard_map/attend/pallas_call | solution.py:487
  203.6 8.5 all-to-all-done.2
  215.2 6.9 convolution_convert_fusion.1
  228.1 96.2 %all-to-all-done.3 = bf16[8,704,256]{2,1,0:T(8,128)(2,1)} async-done(((bf16[8,704,256]{2,1,0:T(8,128)(2,1)}), bf16[8,704,256]{2,1,0:T(8,128)(2,1)}, u32[]{:S(2)}, u32[]{:S(2)}) %all-to-all-start.3) | async-done | bytes 2883616 | tf_op jit(solution)/shard_map/all_to_all | solution.py:981
  328.2 32.8 %reduce-scatter.3.cloned.1.call-done = bf16[128,2048]{1,0:T(8,128)(2,1)} async-done(((bf16[2048,2048]{1,0:T(8,128)(2,1)}), bf16[128,2048]{1,0:T(8,128)(2,1)}) %reduce-scatter.3.cloned.1.call-update) | async-done | bytes 524304 | tf_op jit(solution)/shard_map/reduce_scatter | solution.py:858
  368.1 6.1 pad_maximum_fusion.refs_4_.down_w
  385.1 44.1 %collective-permute-done.18 = bf16[704,2048]{1,0:T(8,128)(2,1)} collective-permute-done((bf16[704,2048]{1,0:T(8,128)(2,1)}, bf16[704,2048]{1,0:T(8,128)(2,1)}, u32[]{:S(2)}, u32[]{:S(2)}) %collective-permute-start.18) | collective-permute-done | bytes 2883616 | tf_op jit(solution)/shard_map/ppermute | solution.py:890
  433.0 5.8 all-gather.7.cloned.1.call-done.rows
  438.8 34.1 %open_rows.1 = (bf16[2048,1408]{1,0:T(8,128)(2,1)}, bf16[2048,1408]{1,0:T(8,128)(2,1)}, bf16[2048,1408]{1,0:T(8,128)(2,1)}) custom-call(bf16[2048,2048]{1,0:T(8,128)(2,1)} %all-gather.7.cloned.1.call-done.rows, bf16[1408,2048]{1,0:T(8,128)(2,1)} %constant_dynamic-update-slice_fusion.2.gate_w.refs_8_, ...), custom_call_target="tpu_custom_call" | custom-call | flops 23622320128 | bytes 40370176 | tf_op jit(solution)/shard_map/open_rows/pallas_call | solution.py:782
  473.0 7.8 slot_product.8
  481.0 7.9 slot_product.9
  491.0 7.9 slot_product.10
  499.3 5.2 collective-permute-done.20
  511.9 7.9 slot_product.11
  536.6 6.4 collective-permute-done.27
  547.3 8.7 collective-permute-start.31
  575.7 73.1 %all-gather.9.cloned.1.call-done.rows = bf16[2048,2048]{1,0:T(8,128)(2,1)} async-done(((bf16[128,2048]{1,0:T(8,128)(2,1)}), bf16[2048,2048]{1,0:T(8,128)(2,1)}) %all-gather.9.cloned.1.call-update) | async-done | bytes 8388624 | tf_op jit(solution)/shard_map/all_gather | solution.py:855
  648.8 23.6 %close_rows.1 = (bf16[2048,1408]{1,0:T(8,128)(2,1)}, bf16[2048,1408]{1,0:T(8,128)(2,1)}) custom-call(bf16[2048,2048]{1,0:T(8,128)(2,1)} %all-gather.9.cloned.1.call-done.rows, bf16[1408,2048]{1,0:T(8,128)(2,1)} %pad_maximum_fusion.refs_4_.down_w, f32[2048,2]{1,0:T(8,128)} %copy.149.share, bf16[2048,1408]{1,0:T(8,128)(2,1)} %get-tuple-element.223.gate_in, ...), custom_call_target="tpu_custom_call" | custom-call | flops 11811160064 | bytes 34603008 | tf_op jit(solution)/shard_map/close_rows/pallas_call | solution.py:782
  672.4 11.5 slot_product.12
  684.2 11.5 slot_product.13
  697.7 11.5 slot_product.14
  718.1 11.5 slot_product.15
  737.0 8.1 collective-permute-done.46
  749.7 7.3 collective-permute-start.51
  758.6 14.8 %fusion.41 = f32[1408,2048]{1,0:T(8,128)S(1)} fusion(bf16[2048,1408]{1,0:T(8,128)(2,1)S(1)} %bitcast.277, bf16[2048,2048]{1,0:T(8,128)(2,1)} %all-gather.7.cloned.1.call-done.rows), kind=kOutput, calls=%fused_computation.241 | convolution fusion | flops 11811160064 | bytes 25690112 | tf_op jit(solution)/shard_map/dot_general | solution.py:47
  784.1 17.1 %fusion.43 = f32[1408,2048]{1,0:T(8,128)S(1)} fusion(bf16[2048,1408]{1,0:T(8,128)(2,1)} %get-tuple-element.277.refs_4_.refs_5_.refs_6_.refs_7_, bf16[2048,2048]{1,0:T(8,128)(2,1)} %all-gather.7.cloned.1.call-done.rows), kind=kOutput, calls=%fused_computation.243 | convolution fusion | flops 11811160064 | bytes 25690112 | tf_op jit(solution)/shard_map/dot_general | solution.py:47
  806.1 14.8 %fusion.44 = f32[1408,2048]{1,0:T(8,128)S(1)} fusion(bf16[2048,1408]{1,0:T(8,128)(2,1)S(1)} %bitcast.279, bf16[2048,2048]{1,0:T(8,128)(2,1)} %all-gather.9.cloned.1.call-done.rows), kind=kOutput, calls=%fused_computation.244 | convolution fusion | flops 11811160064 | bytes 25690112 | tf_op jit(solution)/shard_map/dot_general | solution.py:47
  824.6 21.5 %collective-permute-done.53 = bf16[704,2048]{1,0:T(8,128)(2,1)S(1)} collective-permute-done((bf16[704,2048]{1,0:T(8,128)(2,1)}, bf16[704,2048]{1,0:T(8,128)(2,1)S(1)}, u32[]{:S(2)}, u32[]{:S(2)}) %collective-permute-start.53) | collective-permute-done | bytes 2883616 | tf_op jit(solution)/shard_map/ppermute | solution.py:890
  859.2 10.5 fusion.42.pull
  869.7 38.1 %attend_back.1 = bf16[2048,768]{1,0:T(8,128)(2,1)} custom-call(f32[2048,512]{1,0:T(8,128)} %fusion.42.pull, f32[2048,4]{1,0:T(8,128)} %get-tuple-element.389.gate, bf16[2048,512]{1,0:T(8,128)(2,1)} %get-tuple-element.272.query_in, bf16[2048,256]{1,0:T(8,128)(2,1)} %get-tuple-element.273.pair, bf16[128,2048]{1,0:T(8,128)(2,1)} %slice_bitcast_fusion.pair_up, ...), custom_call_target="tpu_custom_call" | custom-call | flops 10737418240 | bytes 12582912 | tf_op jit(solution)/shard_map/attend_back/pallas_call | solution.py:605
  907.8 9.3 all-to-all-done.4
  917.0 11.6 %convolution_convert_fusion = bf16[2048,2048]{1,0:T(8,128)(2,1)} fusion(bf16[2048,768]{1,0:T(8,128)(2,1)} %attend_back.1, bf16[2048,768]{1,0:T(8,128)(2,1)} %bitcast.299), kind=kOutput, calls=%fused_computation.1 | convolution fusion | flops 6446645248 | bytes 14680064 | tf_op jit(solution)/shard_map/dot_general | solution.py:43
  939.5 11.0 convolution_convert_fusion.2
  952.1 9.4 fusion.45
  961.5 9.7 collective-permute-done.55
  974.2 16.4 %collective-permute-start.57 = (bf16[352,2048]{1,0:T(8,128)(2,1)}, bf16[352,2048]{1,0:T(8,128)(2,1)}, u32[]{:S(2)}, u32[]{:S(2)}) collective-permute-start(bf16[352,2048]{1,0:T(8,128)(2,1)} %slice.156), channel_id=1, source_target_pairs={{0,2},{2,0},{1,3},{3,1},{4,6},{6,4},{5,7},{7,5},{8,10},{10,8},{9,1... | collective-permute-start | bytes 4325384 | tf_op jit(solution)/shard_map/ppermute | solution.py:890
  996.3 29.3 %collective-permute-done.37 = bf16[128,512]{1,0:T(8,128)(2,1)S(1)} collective-permute-done((bf16[128,512]{1,0:T(8,128)(2,1)S(1)}, bf16[128,512]{1,0:T(8,128)(2,1)S(1)}, u32[]{:S(2)}, u32[]{:S(2)}) %collective-permute-start.37) | collective-permute-done | bytes 131104 | tf_op jit(solution)/shard_map/ppermute | solution.py:842
  1047.1 6.3 copy.166
  1057.5 5.6 collective-permute-start.60
  1067.9 6.3 copy.167
  1074.3 21.5 %all-to-all-done.6 = bf16[8,128,768]{2,1,0:T(8,128)(2,1)} async-done(((bf16[8,128,768]{2,1,0:T(8,128)(2,1)}), bf16[8,128,768]{2,1,0:T(8,128)(2,1)}, u32[]{:S(2)}, u32[]{:S(2)}) %all-to-all-start.6) | async-done | bytes 1572896 | tf_op jit(solution)/shard_map/all_to_all | solution.py:914
  1124.1 7.6 collective-permute-start.65
  1132.9 7.3 add_bitcast_fusion
  (450 shorter events, 313.1 us)
Async XLA Ops:
  7.3 135.3 %all-gather.5.cloned.1.call-start = ((), (), s32[]{:S(2)}) async-start(), calls=%async_computation.10 | async-start | bytes 8912896 | tf_op jit(solution)/shard_map/all_gather | solution.py:855
  36.8 64.3 %collective-permute-start.12 = (bf16[704,2048]{1,0:T(8,128)(2,1)}, bf16[704,2048]{1,0:T(8,128)(2,1)}, u32[]{:S(2)}, u32[]{:S(2)}) collective-permute-start(bf16[704,2048]{1,0:T(8,128)(2,1)} %bitcast.301), channel_id=1, source_target_pairs={{0,2},{2,0},{1,3},{3,1},{4,6},{6,4},{5,7},{7,5},{8,10},{10,8},{9,1... | collective-permute-start | bytes 8650760 | tf_op jit(solution)/shard_map/ppermute | solution.py:890
  42.4 68.4 %all-to-all-start = ((bf16[8,128,768]{2,1,0:T(8,128)(2,1)}), bf16[8,128,768]{2,1,0:T(8,128)(2,1)S(1)}, u32[]{:S(2)}, u32[]{:S(2)}) async-start(bf16[8,128,768]{2,1,0:T(8,128)(2,1)} %pad_maximum_fusion.3), calls=%async_computation | async-start | bytes 3145728 | tf_op jit(solution)/shard_map/all_to_all | solution.py:914
  110.8 31.8 %all-to-all-start.1 = ((bf16[8,128,512]{2,1,0:T(8,128)(2,1)}), bf16[8,128,512]{2,1,0:T(8,128)(2,1)}, u32[]{:S(2)}, u32[]{:S(2)}) async-start(bf16[8,128,512]{2,1,0:T(8,128)(2,1)} %pad_maximum_fusion.4), calls=%async_computation.1 | async-start | bytes 2097152 | tf_op jit(solution)/shard_map/all_to_all | solution.py:914
  115.1 35.9 %collective-permute-start.14 = (bf16[8,128,768]{2,1,0:T(8,128)(2,1)S(1)}, bf16[8,128,768]{2,1,0:T(8,128)(2,1)}, u32[]{:S(2)}, u32[]{:S(2)}) collective-permute-start(bf16[8,128,768]{2,1,0:T(8,128)(2,1)S(1)} %all-to-all-done), channel_id=1, source_target_pairs={{0,2},{1,0},{2,3},{3,1},{4,6},{5,4},{6,7},{7,5},{8,10},{9,8},{10,1... | collective-permute-start | bytes 4718600 | tf_op jit(solution)/shard_map/ppermute | solution.py:908
  116.7 34.4 %collective-permute-start.13 = (bf16[8,128,768]{2,1,0:T(8,128)(2,1)S(1)}, bf16[8,128,768]{2,1,0:T(8,128)(2,1)}, u32[]{:S(2)}, u32[]{:S(2)}) collective-permute-start(bf16[8,128,768]{2,1,0:T(8,128)(2,1)S(1)} %all-to-all-done), channel_id=1, source_target_pairs={{1,2},{2,1},{5,6},{6,5},{9,10},{10,9},{13,14},{14,13},{17,18},{18,... | collective-permute-start | bytes 4718600 | tf_op jit(solution)/shard_map/ppermute | solution.py:907
  142.6 69.5 %all-to-all-start.2 = ((bf16[8,704,256]{2,1,0:T(8,128)(2,1)}), bf16[8,704,256]{2,1,0:T(8,128)(2,1)}, u32[]{:S(2)}, u32[]{:S(2)}) async-start(bf16[8,704,256]{2,1,0:T(8,128)(2,1)} %bitcast.282), calls=%async_computation.2 | async-start | bytes 5767168 | tf_op jit(solution)/shard_map/all_to_all | solution.py:914
  147.0 214.0 %reduce-scatter.3.cloned.1.call-start = ((), (), s32[]{:S(2)}) async-start(), calls=%async_computation.11 | async-start | bytes 8912896 | tf_op jit(solution)/shard_map/reduce_scatter | solution.py:858
  164.9 35.1 %collective-permute-start.16 = (bf16[8,128,512]{2,1,0:T(8,128)(2,1)}, bf16[8,128,512]{2,1,0:T(8,128)(2,1)}, u32[]{:S(2)}, u32[]{:S(2)}) collective-permute-start(bf16[8,128,512]{2,1,0:T(8,128)(2,1)} %all-to-all-done.1), channel_id=1, source_target_pairs={{0,2},{1,0},{2,3},{3,1},{4,6},{5,4},{6,7},{7,5},{8,10},{9,8},{10,1... | collective-permute-start | bytes 3145736 | tf_op jit(solution)/shard_map/ppermute | solution.py:908
  168.4 31.7 %collective-permute-start.15 = (bf16[8,128,512]{2,1,0:T(8,128)(2,1)}, bf16[8,128,512]{2,1,0:T(8,128)(2,1)}, u32[]{:S(2)}, u32[]{:S(2)}) collective-permute-start(bf16[8,128,512]{2,1,0:T(8,128)(2,1)} %all-to-all-done.1), channel_id=1, source_target_pairs={{1,2},{2,1},{5,6},{6,5},{9,10},{10,9},{13,14},{14,13},{17,18},{18,... | collective-permute-start | bytes 3145736 | tf_op jit(solution)/shard_map/ppermute | solution.py:907
  222.1 102.2 %all-to-all-start.3 = ((bf16[8,704,256]{2,1,0:T(8,128)(2,1)}), bf16[8,704,256]{2,1,0:T(8,128)(2,1)}, u32[]{:S(2)}, u32[]{:S(2)}) async-start(bf16[8,704,256]{2,1,0:T(8,128)(2,1)} %bitcast.34), calls=%async_computation.4 | async-start | bytes 5767168 | tf_op jit(solution)/shard_map/all_to_all | solution.py:981
  226.6 212.3 %all-gather.7.cloned.1.call-start = ((), (), s32[]{:S(2)}) async-start(), calls=%async_computation.12 | async-start | bytes 8912896 | tf_op jit(solution)/shard_map/all_gather | solution.py:855
  226.6 135.5 %collective-permute-start.17 = (bf16[704,2048]{1,0:T(8,128)(2,1)S(1)}, bf16[704,2048]{1,0:T(8,128)(2,1)}, u32[]{:S(2)}, u32[]{:S(2)}) collective-permute-start(bf16[704,2048]{1,0:T(8,128)(2,1)S(1)} %bitcast.283), channel_id=1, source_target_pairs={{0,2},{2,0},{1,3},{3,1},{4,6},{6,4},{5,7},{7,5},{8,10},{10,8},{9,1... | collective-permute-start | bytes 8650760 | tf_op jit(solution)/shard_map/ppermute | solution.py:890
  364.0 284.8 %all-gather.9.cloned.1.call-start = ((), (), s32[]{:S(2)}) async-start(), calls=%async_computation.13 | async-start | bytes 8912896 | tf_op jit(solution)/shard_map/all_gather | solution.py:855
  364.5 64.7 %collective-permute-start.18 = (bf16[704,2048]{1,0:T(8,128)(2,1)}, bf16[704,2048]{1,0:T(8,128)(2,1)}, u32[]{:S(2)}, u32[]{:S(2)}) collective-permute-start(bf16[704,2048]{1,0:T(8,128)(2,1)} %bitcast.286), channel_id=1, source_target_pairs={{0,2},{2,0},{1,3},{3,1},{4,6},{6,4},{5,7},{7,5},{8,10},{10,8},{9,1... | collective-permute-start | bytes 8650760 | tf_op jit(solution)/shard_map/ppermute | solution.py:890
  505.3 16.2 %collective-permute-start.22 = (bf16[128,2048]{1,0:T(8,128)(2,1)}, bf16[128,2048]{1,0:T(8,128)(2,1)S(1)}, u32[]{:S(2)}, u32[]{:S(2)}) collective-permute-start(bf16[128,2048]{1,0:T(8,128)(2,1)} %slice.133), channel_id=1, source_target_pairs={{0,4},{4,0},{8,12},{12,8},{16,20},{20,16},{24,28},{28,24},{1,5},{5... | collective-permute-start | bytes 1572872 | tf_op jit(solution)/shard_map/ppermute | solution.py:649
  506.8 14.7 %collective-permute-start.23 = (bf16[128,2048]{1,0:T(8,128)(2,1)}, bf16[128,2048]{1,0:T(8,128)(2,1)}, u32[]{:S(2)}, u32[]{:S(2)}) collective-permute-start(bf16[128,2048]{1,0:T(8,128)(2,1)} %fusion.12), channel_id=1, source_target_pairs={{0,8},{4,12},{1,9},{5,13},{2,10},{6,14},{3,11},{7,15}} | collective-permute-start | bytes 1572872 | tf_op jit(solution)/shard_map/ppermute | solution.py:662
  526.7 16.3 %collective-permute-start.27 = (bf16[128,2048]{1,0:T(8,128)(2,1)}, bf16[128,2048]{1,0:T(8,128)(2,1)S(1)}, u32[]{:S(2)}, u32[]{:S(2)}) collective-permute-start(bf16[128,2048]{1,0:T(8,128)(2,1)} %get-tuple-element.368), channel_id=1, source_target_pairs={{0,8},{4,12},{8,16},{12,20},{1,9},{5,13},{9,17},{13,21},{2,10},{6,... | collective-permute-start | bytes 1572872 | tf_op jit(solution)/shard_map/ppermute | solution.py:662
  544.0 22.5 %collective-permute-start.30 = (bf16[128,2048]{1,0:T(8,128)(2,1)}, bf16[128,2048]{1,0:T(8,128)(2,1)}, u32[]{:S(2)}, u32[]{:S(2)}) collective-permute-start(bf16[128,2048]{1,0:T(8,128)(2,1)} %slice.139), channel_id=1, source_target_pairs={{0,4},{4,0},{8,12},{12,8},{16,20},{20,16},{24,28},{28,24},{1,5},{5... | collective-permute-start | bytes 1572872 | tf_op jit(solution)/shard_map/ppermute | solution.py:649
  547.3 19.4 %collective-permute-start.31 = (bf16[128,2048]{1,0:T(8,128)(2,1)}, bf16[128,2048]{1,0:T(8,128)(2,1)S(1)}, u32[]{:S(2)}, u32[]{:S(2)}) collective-permute-start(bf16[128,2048]{1,0:T(8,128)(2,1)} %get-tuple-element.366), channel_id=1, source_target_pairs={{0,8},{4,12},{8,16},{12,20},{16,24},{20,28},{1,9},{5,13},{9,17},{1... | collective-permute-start | bytes 1572872 | tf_op jit(solution)/shard_map/ppermute | solution.py:662
  556.0 14.6 %collective-permute-start.32 = (bf16[128,2048]{1,0:T(8,128)(2,1)S(1)}, bf16[128,2048]{1,0:T(8,128)(2,1)S(1)}, u32[]{:S(2)}, u32[]{:S(2)}) collective-permute-start(bf16[128,2048]{1,0:T(8,128)(2,1)S(1)} %get-tuple-element.365), channel_id=1, source_target_pairs={{24,16},{28,20},{16,8},{20,12},{8,0},{12,4},{25,17},{29,21},{17,9}... | collective-permute-start | bytes 1572872 | tf_op jit(solution)/shard_map/ppermute | solution.py:665
  575.6 283.5 %all-gather.11.cloned.1.call-start = ((), (), s32[]{:S(2)}) async-start(), calls=%async_computation.14 | async-start | bytes 8912896 | tf_op jit(solution)/shard_map/all_gather | solution.py:855
  712.1 17.4 %collective-permute-start.45 = (bf16[256,2048]{1,0:T(8,128)(2,1)}, bf16[256,2048]{1,0:T(8,128)(2,1)S(1)}, u32[]{:S(2)}, u32[]{:S(2)}) collective-permute-start(bf16[256,2048]{1,0:T(8,128)(2,1)} %get-tuple-element.248), channel_id=1, source_target_pairs={{0,1},{1,0},{2,3},{3,2},{4,5},{5,4},{6,7},{7,6},{8,9},{9,8},{10,11... | collective-permute-start | bytes 3145736 | tf_op jit(solution)/shard_map/ppermute | solution.py:653
  713.1 18.7 %collective-permute-start.43 = (bf16[128,2048]{1,0:T(8,128)(2,1)}, bf16[128,2048]{1,0:T(8,128)(2,1)S(1)}, u32[]{:S(2)}, u32[]{:S(2)}) collective-permute-start(bf16[128,2048]{1,0:T(8,128)(2,1)} %fusion.13), channel_id=1, source_target_pairs={{0,8},{4,12},{1,9},{5,13},{2,10},{6,14},{3,11},{7,15}} | collective-permute-start | bytes 1572872 | tf_op jit(solution)/shard_map/ppermute | solution.py:662
  716.0 15.8 %collective-permute-start.44 = (bf16[128,2048]{1,0:T(8,128)(2,1)}, bf16[128,2048]{1,0:T(8,128)(2,1)}, u32[]{:S(2)}, u32[]{:S(2)}) collective-permute-start(bf16[128,2048]{1,0:T(8,128)(2,1)} %fusion.13), channel_id=1, source_target_pairs={{24,16},{28,20},{25,17},{29,21},{26,18},{30,22},{27,19},{31,23}} | collective-permute-start | bytes 1572872 | tf_op jit(solution)/shard_map/ppermute | solution.py:665
  747.6 32.1 %collective-permute-start.50 = (bf16[128,2048]{1,0:T(8,128)(2,1)S(1)}, bf16[128,2048]{1,0:T(8,128)(2,1)S(1)}, u32[]{:S(2)}, u32[]{:S(2)}) collective-permute-start(bf16[128,2048]{1,0:T(8,128)(2,1)S(1)} %slice.147), channel_id=1, source_target_pairs={{0,4},{4,0},{8,12},{12,8},{16,20},{20,16},{24,28},{28,24},{1,5},{5... | collective-permute-start | bytes 1572872 | tf_op jit(solution)/shard_map/ppermute | solution.py:649
  749.7 30.0 %collective-permute-start.51 = (bf16[128,2048]{1,0:T(8,128)(2,1)S(1)}, bf16[128,2048]{1,0:T(8,128)(2,1)S(1)}, u32[]{:S(2)}, u32[]{:S(2)}) collective-permute-start(bf16[128,2048]{1,0:T(8,128)(2,1)S(1)} %get-tuple-element.362), channel_id=1, source_target_pairs={{0,8},{4,12},{8,16},{12,20},{16,24},{20,28},{1,9},{5,13},{9,17},{1... | collective-permute-start | bytes 1572872 | tf_op jit(solution)/shard_map/ppermute | solution.py:662
  757.1 22.7 %collective-permute-start.52 = (bf16[128,2048]{1,0:T(8,128)(2,1)S(1)}, bf16[128,2048]{1,0:T(8,128)(2,1)S(1)}, u32[]{:S(2)}, u32[]{:S(2)}) collective-permute-start(bf16[128,2048]{1,0:T(8,128)(2,1)S(1)} %get-tuple-element.361), channel_id=1, source_target_pairs={{24,16},{28,20},{16,8},{20,12},{8,0},{12,4},{25,17},{29,21},{17,9}... | collective-permute-start | bytes 1572872 | tf_op jit(solution)/shard_map/ppermute | solution.py:665
  782.6 63.5 %collective-permute-start.53 = (bf16[704,2048]{1,0:T(8,128)(2,1)}, bf16[704,2048]{1,0:T(8,128)(2,1)S(1)}, u32[]{:S(2)}, u32[]{:S(2)}) collective-permute-start(bf16[704,2048]{1,0:T(8,128)(2,1)} %slice.219), channel_id=1, source_target_pairs={{0,2},{2,0},{1,3},{3,1},{4,6},{6,4},{5,7},{7,5},{8,10},{10,8},{9,1... | collective-permute-start | bytes 8650760 | tf_op jit(solution)/shard_map/ppermute | solution.py:890
  848.9 68.1 %all-to-all-start.4 = ((bf16[8,704,256]{2,1,0:T(8,128)(2,1)}), bf16[8,704,256]{2,1,0:T(8,128)(2,1)}, u32[]{:S(2)}, u32[]{:S(2)}) async-start(bf16[8,704,256]{2,1,0:T(8,128)(2,1)} %bitcast.288), calls=%async_computation.5 | async-start | bytes 5767168 | tf_op jit(solution)/shard_map/all_to_all | solution.py:1044
  853.4 243.7 %reduce-scatter.5.cloned.1.call-start = ((), (), s32[]{:S(2)}) async-start(), calls=%async_computation.15 | async-start | bytes 8912896 | tf_op jit(solution)/shard_map/reduce_scatter | solution.py:858
  857.7 71.0 %collective-permute-start.56 = (bf16[704,2048]{1,0:T(8,128)(2,1)}, bf16[704,2048]{1,0:T(8,128)(2,1)}, u32[]{:S(2)}, u32[]{:S(2)}) collective-permute-start(bf16[704,2048]{1,0:T(8,128)(2,1)} %slice.218), channel_id=1, source_target_pairs={{0,2},{2,0},{1,3},{3,1},{4,6},{6,4},{5,7},{7,5},{8,10},{10,8},{9,1... | collective-permute-start | bytes 8650760 | tf_op jit(solution)/shard_map/ppermute | solution.py:890
  935.0 102.7 %all-to-all-start.5 = ((bf16[8,704,256]{2,1,0:T(8,128)(2,1)}), bf16[8,704,256]{2,1,0:T(8,128)(2,1)}, u32[]{:S(2)}, u32[]{:S(2)}) async-start(bf16[8,704,256]{2,1,0:T(8,128)(2,1)} %bitcast.285), calls=%async_computation.6 | async-start | bytes 5767168 | tf_op jit(solution)/shard_map/all_to_all | solution.py:1059
  950.8 20.4 %collective-permute-start.55 = (bf16[8,128,768]{2,1,0:T(8,128)(2,1)S(1)}, bf16[8,128,768]{2,1,0:T(8,128)(2,1)S(1)}, u32[]{:S(2)}, u32[]{:S(2)}) collective-permute-start(bf16[8,128,768]{2,1,0:T(8,128)(2,1)S(1)} %get-tuple-element.360), channel_id=1, source_target_pairs={{2,0},{0,1},{3,2},{1,3},{6,4},{4,5},{7,6},{5,7},{10,8},{8,9},{11,1... | collective-permute-start | bytes 4718600 | tf_op jit(solution)/shard_map/ppermute | solution.py:1071
  950.8 20.4 %collective-permute-start.54 = (bf16[8,128,768]{2,1,0:T(8,128)(2,1)S(1)}, bf16[8,128,768]{2,1,0:T(8,128)(2,1)S(1)}, u32[]{:S(2)}, u32[]{:S(2)}) collective-permute-start(bf16[8,128,768]{2,1,0:T(8,128)(2,1)S(1)} %get-tuple-element.359), channel_id=1, source_target_pairs={{1,2},{2,1},{5,6},{6,5},{9,10},{10,9},{13,14},{14,13},{17,18},{18,... | collective-permute-start | bytes 4718600 | tf_op jit(solution)/shard_map/ppermute | solution.py:1070
  974.2 63.6 %collective-permute-start.57 = (bf16[352,2048]{1,0:T(8,128)(2,1)}, bf16[352,2048]{1,0:T(8,128)(2,1)}, u32[]{:S(2)}, u32[]{:S(2)}) collective-permute-start(bf16[352,2048]{1,0:T(8,128)(2,1)} %slice.156), channel_id=1, source_target_pairs={{0,2},{2,0},{1,3},{3,1},{4,6},{6,4},{5,7},{7,5},{8,10},{10,8},{9,1... | collective-permute-start | bytes 4325384 | tf_op jit(solution)/shard_map/ppermute | solution.py:890
  993.2 32.4 %collective-permute-start.37 = (bf16[128,512]{1,0:T(8,128)(2,1)S(1)}, bf16[128,512]{1,0:T(8,128)(2,1)S(1)}, u32[]{:S(2)}, u32[]{:S(2)}) collective-permute-start(bf16[128,512]{1,0:T(8,128)(2,1)S(1)} %bitcast.330), channel_id=1, source_target_pairs={{0,2},{1,3},{2,0},{3,1},{4,6},{5,7},{6,4},{7,5},{8,10},{9,11},{10,... | collective-permute-start | bytes 393224 | tf_op jit(solution)/shard_map/ppermute | solution.py:842
  993.3 35.6 %collective-permute-start.38 = (bf16[128,512]{1,0:T(8,128)(2,1)S(1)}, bf16[128,512]{1,0:T(8,128)(2,1)S(1)}, u32[]{:S(2)}, u32[]{:S(2)}) collective-permute-start(bf16[128,512]{1,0:T(8,128)(2,1)S(1)} %bitcast.331), channel_id=1, source_target_pairs={{0,3},{1,2},{2,1},{3,0},{4,7},{5,6},{6,5},{7,4},{8,11},{9,10},{10,... | collective-permute-start | bytes 393224 | tf_op jit(solution)/shard_map/ppermute | solution.py:842
  995.4 33.5 %collective-permute-start.36 = (bf16[128,512]{1,0:T(8,128)(2,1)S(1)}, bf16[128,512]{1,0:T(8,128)(2,1)S(1)}, u32[]{:S(2)}, u32[]{:S(2)}) collective-permute-start(bf16[128,512]{1,0:T(8,128)(2,1)S(1)} %bitcast.332), channel_id=1, source_target_pairs={{0,1},{1,0},{2,3},{3,2},{4,5},{5,4},{6,7},{7,6},{8,9},{9,8},{10,11... | collective-permute-start | bytes 393224 | tf_op jit(solution)/shard_map/ppermute | solution.py:842
  1031.3 22.0 %collective-permute-start.59 = (bf16[8,128,512]{2,1,0:T(8,128)(2,1)}, bf16[8,128,512]{2,1,0:T(8,128)(2,1)}, u32[]{:S(2)}, u32[]{:S(2)}) collective-permute-start(bf16[8,128,512]{2,1,0:T(8,128)(2,1)} %get-tuple-element.376), channel_id=1, source_target_pairs={{2,0},{0,1},{3,2},{1,3},{6,4},{4,5},{7,6},{5,7},{10,8},{8,9},{11,1... | collective-permute-start | bytes 3145736 | tf_op jit(solution)/shard_map/ppermute | solution.py:1071
  1031.4 22.0 %collective-permute-start.58 = (bf16[8,128,512]{2,1,0:T(8,128)(2,1)}, bf16[8,128,512]{2,1,0:T(8,128)(2,1)}, u32[]{:S(2)}, u32[]{:S(2)}) collective-permute-start(bf16[8,128,512]{2,1,0:T(8,128)(2,1)} %get-tuple-element.375), channel_id=1, source_target_pairs={{1,2},{2,1},{5,6},{6,5},{9,10},{10,9},{13,14},{14,13},{17,18},{18,... | collective-permute-start | bytes 3145736 | tf_op jit(solution)/shard_map/ppermute | solution.py:1070
  1037.8 58.0 %all-to-all-start.6 = ((bf16[8,128,768]{2,1,0:T(8,128)(2,1)}), bf16[8,128,768]{2,1,0:T(8,128)(2,1)}, u32[]{:S(2)}, u32[]{:S(2)}) async-start(bf16[8,128,768]{2,1,0:T(8,128)(2,1)} %add_convert_fusion.2), calls=%async_computation.7 | async-start | bytes 3145728 | tf_op jit(solution)/shard_map/all_to_all | solution.py:914
  1057.5 42.5 %collective-permute-start.60 = (bf16[352,2048]{1,0:T(8,128)(2,1)}, bf16[352,2048]{1,0:T(8,128)(2,1)}, u32[]{:S(2)}, u32[]{:S(2)}) collective-permute-start(bf16[352,2048]{1,0:T(8,128)(2,1)} %slice.157), channel_id=1, source_target_pairs={{0,2},{2,0},{1,3},{3,1},{4,6},{6,4},{5,7},{7,5},{8,10},{10,8},{9,1... | collective-permute-start | bytes 4325384 | tf_op jit(solution)/shard_map/ppermute | solution.py:890
  1100.0 31.7 %all-to-all-start.7 = ((bf16[8,128,512]{2,1,0:T(8,128)(2,1)}), bf16[8,128,512]{2,1,0:T(8,128)(2,1)}, u32[]{:S(2)}, u32[]{:S(2)}) async-start(bf16[8,128,512]{2,1,0:T(8,128)(2,1)} %add_convert_fusion.3), calls=%async_computation.9 | async-start | bytes 2097152 | tf_op jit(solution)/shard_map/all_to_all | solution.py:1100
  1121.1 21.0 %collective-permute-start.67 = (f32[128,512]{1,0:T(8,128)S(1)}, f32[128,512]{1,0:T(8,128)S(1)}, u32[]{:S(2)}, u32[]{:S(2)}) collective-permute-start(f32[128,512]{1,0:T(8,128)S(1)} %bitcast.315), channel_id=1, source_target_pairs={{0,2},{1,3},{2,0},{3,1},{4,6},{5,7},{6,4},{7,5},{8,10},{9,11},{10,... | collective-permute-start | bytes 786440 | tf_op jit(solution)/shard_map/ppermute | solution.py:842
  1122.6 19.4 %collective-permute-start.68 = (f32[128,512]{1,0:T(8,128)S(1)}, f32[128,512]{1,0:T(8,128)S(1)}, u32[]{:S(2)}, u32[]{:S(2)}) collective-permute-start(f32[128,512]{1,0:T(8,128)S(1)} %bitcast.316), channel_id=1, source_target_pairs={{0,3},{1,2},{2,1},{3,0},{4,7},{5,6},{6,5},{7,4},{8,11},{9,10},{10,... | collective-permute-start | bytes 786440 | tf_op jit(solution)/shard_map/ppermute | solution.py:842
  1122.7 19.3 %collective-permute-start.66 = (f32[128,512]{1,0:T(8,128)S(1)}, f32[128,512]{1,0:T(8,128)S(1)}, u32[]{:S(2)}, u32[]{:S(2)}) collective-permute-start(f32[128,512]{1,0:T(8,128)S(1)} %bitcast.317), channel_id=1, source_target_pairs={{0,1},{1,0},{2,3},{3,2},{4,5},{5,4},{6,7},{7,6},{8,9},{9,8},{10,11... | collective-permute-start | bytes 786440 | tf_op jit(solution)/shard_map/ppermute | solution.py:842
  1124.1 16.1 %collective-permute-start.65 = (f32[3,2048]{1,0:T(4,128)S(1)}, f32[3,2048]{1,0:T(4,128)S(1)}, u32[]{:S(2)}, u32[]{:S(2)}) collective-permute-start(f32[3,2048]{1,0:T(4,128)S(1)} %add.417), channel_id=1, source_target_pairs={{0,16},{4,20},{8,24},{12,28},{16,0},{20,4},{24,8},{28,12},{1,17},{... | collective-permute-start | bytes 73736 | tf_op jit(solution)/shard_map/ppermute | solution.py:1120
  (102 other events, 1882.4 us)
Sparse Core Ops, SparseCore 0:
  20.3 104.6 all-gather.4
  222.3 138.7 reduce-scatter.2
  364.2 74.6 all-gather.6
  575.8 73.0 all-gather.8
  782.7 74.2 all-gather.10
  928.8 164.8 reduce-scatter.4
